TPU v7x, 32 devices: a whole 2x2x4 slice. The times are simulated.
32 devices in a mesh: dp: 16 (over z, x, core), seq: 2 (over y).
Axes of the slice: x: 2, y: 2, z: 4, core: 2. Of those that a mesh axis runs over, the one named last changes fastest.
Arguments:
- hidden_in: bfloat16 [32, 1024, 1024], P('dp', 'seq'), may hold values from -6 to 6
- family: int32 [16], P('dp'), may hold values from 0 to 63
- orient: int32 [32], P('dp'), may hold values from 0 to 1, as said below
- norm_gain: bfloat16 [1024], replicated, may hold values from 0.099609375 to 1.8984375
- norm_bias: bfloat16 [1024], replicated, may hold values from -4 to 4
- qkv_weight: bfloat16 [1024, 3072], replicated, may hold values from -0.1875 to 0.1875
- out_weight: bfloat16 [1024, 1024], replicated, may hold values from -0.5 to 0.5
- up_weight: bfloat16 [1024, 4096], replicated, may hold values from -0.1875 to 0.1875
- up_bias: bfloat16 [4096], replicated, may hold values from -6 to 6
- down_weight: bfloat16 [4096, 1024], replicated, may hold values from -0.09375 to 0.09375
- down_bias: bfloat16 [1024], replicated, may hold values from -4 to 4
- family_table: bfloat16 [64, 1024], replicated, may hold values from -6 to 6
- orient_table: bfloat16 [2, 1024], replicated, may hold values from -6 to 6
- cotangent: bfloat16 [32, 1024, 1024], P('dp', 'seq'), may hold values from -6 to 6
Outputs:
- layer_out: bfloat16 [32, 1024, 1024], P('dp', 'seq')
- input_grad: float32 [32, 1024, 1024], P('dp', 'seq')
- norm_gain_grad: float32 [1024], replicated
- norm_bias_grad: float32 [1024], replicated
- qkv_weight_grad: float32 [1024, 3072], P(('dp', 'seq'))
- out_weight_grad: float32 [1024, 1024], P(('dp', 'seq'))
- up_weight_grad: float32 [1024, 4096], P(('dp', 'seq'))
- up_bias_grad: float32 [4096], replicated
- down_weight_grad: float32 [4096, 1024], P(('dp', 'seq'))
- down_bias_grad: float32 [1024], replicated
- family_table_grad: float32 [64, 1024], replicated
- orient_table_grad: float32 [2, 1024], replicated
Inputs may be any that keep to these rules, and one draw needn't show every extreme that they name: `orient`: in each pair of rows 2p and 2p + 1 one row has flag 0 and the other flag 1.
All inputs are finite; a program needn't handle non-finite values.
Results may differ from a plain program's by a relative error of at most 0.006.
Values may be sent and summed in bfloat16 or wider, within the bound.
A program may use at most 256 MiB of HBM per device.

v0:
```python
import functools
import math

import jax
import jax.numpy as jnp
from jax import lax
from jax.experimental import pallas as pl
from jax.experimental.pallas import tpu as pltpu
from jax.sharding import PartitionSpec as P

H = 16
HD = 64
ROT = 32
MESH = pl.DeviceIdType.MESH
VMEM_LIMIT = 60 * 1024 * 1024
F32 = jnp.float32
BF16 = jnp.bfloat16


def for_sending(shard):

    def short(part):
        return part.astype(jnp.bfloat16) if part.dtype == jnp.float32 else part

    return jax.tree.map(short, shard)


def rope_tables(positions, features):
    column = jnp.arange(features, dtype=jnp.int32)
    within = column % HD
    frequency = jnp.exp(-(2.0 * (within // 2).astype(jnp.float32) / ROT) * math.log(10000.0))
    angles = positions[:, None] * frequency[None, :]
    rotary = within < ROT
    cosine = jnp.where(rotary[None, :], jnp.cos(angles), 1.0)
    sign_term = jnp.where(within % 2 == 0, -1.0, 1.0)
    sine_term = jnp.where(rotary[None, :], sign_term[None, :] * jnp.sin(angles), 0.0)
    return (cosine, sine_term)


def pair_swap(values):
    even_cols = jnp.arange(values.shape[-1]) % 2 == 0
    return jnp.where(even_cols, jnp.roll(values, -1, axis=-1), jnp.roll(values, 1, axis=-1))


def rotate(values, cosine, sine_term):
    return values * cosine + pair_swap(values) * sine_term


def rotate_back(values, cosine, sine_term):
    return values * cosine + pair_swap(values * sine_term)


def gelu_tanh(pre_values):
    return jax.nn.gelu(pre_values, approximate=True)


def body_by_heads(
    hidden_in,
    family,
    orient,
    norm_gain,
    norm_bias,
    qkv_weight,
    out_weight,
    up_weight,
    up_bias,
    down_weight,
    down_bias,
    family_table,
    orient_table,
    cotangent,
):
    seq_count = lax.axis_size("seq")
    row_count, seg_length, features = hidden_in.shape
    full_length = seg_length * seq_count
    local_heads = H // seq_count
    head_size = features // H
    slab_width = features // seq_count
    block_rows = min(512, full_length)
    block_count = full_length // block_rows
    score_scale = head_size ** (-0.5)
    token_count = row_count * seg_length
    family_rows = jnp.repeat(family, 2)
    family_hot = (family_rows[:, None] == jnp.arange(family_table.shape[0])[None, :]).astype(
        jnp.bfloat16
    )
    orient_hot = (orient[:, None] == jnp.arange(2)[None, :]).astype(jnp.bfloat16)
    embedding = jnp.dot(family_hot, family_table, preferred_element_type=jnp.float32) + jnp.dot(
        orient_hot, orient_table, preferred_element_type=jnp.float32
    )
    embedded = (hidden_in.astype(jnp.float32) + embedding[:, None, :]).reshape(
        token_count, features
    )
    row_mean = jnp.mean(embedded, -1, keepdims=True)
    centred = embedded - row_mean
    row_var = jnp.mean(centred * centred, -1, keepdims=True)
    inv_std = lax.rsqrt(row_var + 1e-05)
    normed_hat = centred * inv_std
    gain_f32 = norm_gain.astype(jnp.float32)
    normed_low = (normed_hat * gain_f32 + norm_bias.astype(jnp.float32)).astype(jnp.bfloat16)
    projected = jnp.dot(normed_low, qkv_weight, preferred_element_type=jnp.float32).reshape(
        row_count, seg_length, 3 * features
    )
    positions = (lax.axis_index("seq") * seg_length + jnp.arange(seg_length)).astype(jnp.float32)
    cosine, sine_term = rope_tables(positions, features)
    queries = rotate(projected[..., :features], cosine, sine_term).astype(jnp.bfloat16)
    keys_rot = rotate(projected[..., features : 2 * features], cosine, sine_term).astype(
        jnp.bfloat16
    )
    values = projected[..., 2 * features :].astype(jnp.bfloat16)
    query_heads, key_heads, value_heads = (
        lax.all_to_all(queries, "seq", split_axis=2, concat_axis=1, tiled=True),
        lax.all_to_all(keys_rot, "seq", split_axis=2, concat_axis=1, tiled=True),
        lax.all_to_all(values, "seq", split_axis=2, concat_axis=1, tiled=True),
    )

    def scores_for(query_block, key_rows, block_start):
        logits = (
            jnp.einsum("qhd,khd->hqk", query_block, key_rows, preferred_element_type=jnp.float32)
            * score_scale
        )
        causal = (block_start + jnp.arange(block_rows))[:, None] >= jnp.arange(full_length)[None, :]
        return jnp.where(causal[None], logits, -1e30)

    def attend(row_args):
        query_row, key_row, value_row = row_args
        key_rows = key_row.reshape(full_length, local_heads, head_size)
        value_rows = value_row.reshape(full_length, local_heads, head_size)
        pieces = []
        log_parts = []
        for block_index in range(block_count):
            block_start = block_index * block_rows
            query_block = query_row[block_start : block_start + block_rows].reshape(
                block_rows, local_heads, head_size
            )
            logits = scores_for(query_block, key_rows, block_start)
            row_peak = jnp.max(logits, -1, keepdims=True)
            weights = jnp.exp(logits - row_peak)
            row_total = jnp.sum(weights, -1, keepdims=True)
            prob_low = (weights / row_total).astype(jnp.bfloat16)
            output_block = jnp.einsum(
                "hqk,khd->qhd", prob_low, value_rows, preferred_element_type=jnp.float32
            )
            pieces.append(output_block.reshape(block_rows, slab_width).astype(jnp.bfloat16))
            log_parts.append((row_peak + jnp.log(row_total))[..., 0])
        return (jnp.concatenate(pieces, 0), jnp.concatenate(log_parts, 1))

    attended_heads, log_sums = lax.map(attend, (query_heads, key_heads, value_heads))
    attended = jax.tree.map(
        lambda part, own: part.astype(own.dtype),
        lax.all_to_all(for_sending(attended_heads), "seq", split_axis=1, concat_axis=2, tiled=True),
        attended_heads,
    )
    attended_flat = attended.reshape(token_count, features)
    branch_attn = jnp.dot(attended_flat, out_weight, preferred_element_type=jnp.float32)
    up_pre = jnp.dot(normed_low, up_weight, preferred_element_type=jnp.float32) + up_bias.astype(
        jnp.float32
    )
    up_act = gelu_tanh(up_pre).astype(jnp.bfloat16)
    branch_feed = jnp.dot(
        up_act, down_weight, preferred_element_type=jnp.float32
    ) + down_bias.astype(jnp.float32)
    layer_out = (
        (embedded + branch_attn + branch_feed)
        .astype(jnp.bfloat16)
        .reshape(row_count, seg_length, features)
    )
    grad_low = cotangent.reshape(token_count, features)
    grad_f32 = grad_low.astype(jnp.float32)
    down_grad = jnp.einsum("nf,nd->fd", up_act, grad_low, preferred_element_type=jnp.float32)
    down_bias_grad = jnp.sum(grad_f32, 0)
    act_grad = jnp.einsum("nd,fd->nf", grad_low, down_weight, preferred_element_type=jnp.float32)
    gelu_out, gelu_pull = jax.vjp(gelu_tanh, up_pre)
    pre_grad = gelu_pull(act_grad)[0].astype(jnp.bfloat16)
    up_bias_grad = jnp.sum(pre_grad.astype(jnp.float32), 0)
    up_grad = jnp.einsum("nd,nf->df", normed_low, pre_grad, preferred_element_type=jnp.float32)
    normed_grad = jnp.einsum("nf,df->nd", pre_grad, up_weight, preferred_element_type=jnp.float32)
    out_grad = jnp.einsum("nd,ne->de", attended_flat, grad_low, preferred_element_type=jnp.float32)
    attended_grad = jnp.einsum(
        "ne,de->nd", grad_low, out_weight, preferred_element_type=jnp.float32
    )
    attended_grad = attended_grad.astype(jnp.bfloat16).reshape(row_count, seg_length, features)
    grad_heads = lax.all_to_all(attended_grad, "seq", split_axis=2, concat_axis=1, tiled=True)

    def attend_back(row_args):
        query_row, key_row, value_row, grad_row, log_row = row_args
        key_rows = key_row.reshape(full_length, local_heads, head_size)
        value_rows = value_row.reshape(full_length, local_heads, head_size)
        keys_total = jnp.zeros((full_length, local_heads, head_size), jnp.float32)
        values_total = jnp.zeros((full_length, local_heads, head_size), jnp.float32)
        query_parts = []
        for block_index in range(block_count):
            block_start = block_index * block_rows
            query_block = query_row[block_start : block_start + block_rows].reshape(
                block_rows, local_heads, head_size
            )
            grad_block = grad_row[block_start : block_start + block_rows].reshape(
                block_rows, local_heads, head_size
            )
            logits = scores_for(query_block, key_rows, block_start)
            probs_full = jnp.exp(logits - log_row[:, block_start : block_start + block_rows, None])
            prob_low = probs_full.astype(jnp.bfloat16)
            probs_grad = jnp.einsum(
                "qhd,khd->hqk", grad_block, value_rows, preferred_element_type=jnp.float32
            )
            inner_sum = jnp.sum(probs_full * probs_grad, -1, keepdims=True)
            scores_grad = (probs_full * (probs_grad - inner_sum)).astype(jnp.bfloat16)
            values_total = values_total + jnp.einsum(
                "hqk,qhd->khd", prob_low, grad_block, preferred_element_type=jnp.float32
            )
            query_grad = (
                jnp.einsum(
                    "hqk,khd->qhd", scores_grad, key_rows, preferred_element_type=jnp.float32
                )
                * score_scale
            )
            query_parts.append(query_grad.reshape(block_rows, slab_width).astype(jnp.bfloat16))
            keys_total = (
                keys_total
                + jnp.einsum(
                    "hqk,qhd->khd", scores_grad, query_block, preferred_element_type=jnp.float32
                )
                * score_scale
            )
        return (
            jnp.concatenate(query_parts, 0),
            keys_total.reshape(full_length, slab_width).astype(jnp.bfloat16),
            values_total.reshape(full_length, slab_width).astype(jnp.bfloat16),
        )

    query_grad_heads, key_grad_heads, value_grad_heads = lax.map(
        attend_back, (query_heads, key_heads, value_heads, grad_heads, log_sums)
    )
    query_grad_pos, key_grad_pos, value_grad_pos = (
        lax.all_to_all(
            for_sending(query_grad_heads), "seq", split_axis=1, concat_axis=2, tiled=True
        ).astype(query_grad_heads.dtype),
        lax.all_to_all(
            for_sending(key_grad_heads), "seq", split_axis=1, concat_axis=2, tiled=True
        ).astype(key_grad_heads.dtype),
        lax.all_to_all(
            for_sending(value_grad_heads), "seq", split_axis=1, concat_axis=2, tiled=True
        ).astype(value_grad_heads.dtype),
    )
    projected_grad = jnp.concatenate(
        [
            rotate_back(query_grad_pos.astype(jnp.float32), cosine, sine_term),
            rotate_back(key_grad_pos.astype(jnp.float32), cosine, sine_term),
            value_grad_pos.astype(jnp.float32),
        ],
        -1,
    )
    projected_grad = projected_grad.astype(jnp.bfloat16).reshape(token_count, 3 * features)
    qkv_grad = jnp.einsum(
        "nd,ne->de", normed_low, projected_grad, preferred_element_type=jnp.float32
    )
    normed_grad = normed_grad + jnp.einsum(
        "ne,de->nd", projected_grad, qkv_weight, preferred_element_type=jnp.float32
    )
    gain_grad = jnp.sum(normed_grad * normed_hat, 0)
    bias_grad = jnp.sum(normed_grad, 0)
    scaled_grad = normed_grad * gain_f32
    hat_grad = (
        scaled_grad
        - jnp.mean(scaled_grad, -1, keepdims=True)
        - normed_hat * jnp.mean(scaled_grad * normed_hat, -1, keepdims=True)
    )
    input_grad = (grad_f32 + inv_std * hat_grad).reshape(row_count, seg_length, features)
    row_sums = jnp.sum(input_grad, 1)
    family_grad = jnp.einsum(
        "rf,rd->fd", family_hot.astype(jnp.float32), row_sums, precision=lax.Precision.HIGHEST
    )
    orient_grad = jnp.einsum(
        "rf,rd->fd", orient_hot.astype(jnp.float32), row_sums, precision=lax.Precision.HIGHEST
    )
    gain_sum, bias_sum, up_bias_sum, down_bias_sum, family_sum, orient_sum = lax.psum(
        (gain_grad, bias_grad, up_bias_grad, down_bias_grad, family_grad, orient_grad),
        ("dp", "seq"),
    )
    qkv_sum, out_sum, up_sum, down_sum = (
        lax.psum_scatter(qkv_grad, ("dp", "seq"), scatter_dimension=0, tiled=True),
        lax.psum_scatter(out_grad, ("dp", "seq"), scatter_dimension=0, tiled=True),
        lax.psum_scatter(up_grad, ("dp", "seq"), scatter_dimension=0, tiled=True),
        lax.psum_scatter(down_grad, ("dp", "seq"), scatter_dimension=0, tiled=True),
    )
    return (
        layer_out,
        input_grad,
        gain_sum,
        bias_sum,
        qkv_sum,
        out_sum,
        up_sum,
        up_bias_sum,
        down_sum,
        down_bias_sum,
        family_sum,
        orient_sum,
    )


def dot_nn(a, b):
    return lax.dot_general(a, b, (((1,), (0,)), ((), ())), preferred_element_type=F32)


def dot_nt(a, b):
    return lax.dot_general(a, b, (((1,), (1,)), ((), ())), preferred_element_type=F32)


def dot_tn(a, b):
    return lax.dot_general(a, b, (((0,), (0,)), ((), ())), preferred_element_type=F32)


def params(**more):
    return pltpu.CompilerParams(vmem_limit_bytes=VMEM_LIMIT, **more)


def cost(flops, moved, exps=0):
    return pl.CostEstimate(flops=flops, bytes_accessed=moved, transcendentals=exps)


def whole(shape):
    return pl.BlockSpec(shape, lambda *_: (0,) * len(shape), pipeline_mode=pl.Buffered(1))


def table_row(table, wanted):
    rows = lax.broadcasted_iota(jnp.int32, table.shape, 0)
    return jnp.sum(jnp.where(rows == wanted, table[...].astype(F32), 0.0), 0, keepdims=True)


def normalise(entries):
    centred = entries - jnp.mean(entries, -1, keepdims=True)
    inv_std = lax.rsqrt(jnp.mean(centred * centred, -1, keepdims=True) + 1e-05)
    return centred * inv_std, inv_std


GELU_C = math.sqrt(2.0 / math.pi)


def gelu_both(z):
    square = z * z
    t = jnp.tanh(GELU_C * z * (1.0 + 0.044715 * square))
    half = 0.5 * (1.0 + t)
    slope = half + (0.5 * GELU_C) * z * (1.0 - t * t) * (1.0 + (3 * 0.044715) * square)
    return z * half, slope


def ffn_kernel(rows, ids, hid, cot, fam, ori, gain, bias, wup, bup, wdn, norm, both, bupg, bdng):
    tokens = hid.shape[0]
    seg = tokens // rows
    step = 256

    @pl.when(pl.program_id(0) == 0)
    def _():
        total = jnp.zeros((1, cot.shape[1]), F32)
        for row in range(rows):
            emb = table_row(fam, ids[0]) + table_row(ori, ids[1 + row])
            for start in range(row * seg, (row + 1) * seg, step):
                part = pl.ds(start, step)
                hat, _ = normalise(hid[part, :].astype(F32) + emb)
                norm[part, :] = (hat * gain[...].astype(F32) + bias[...].astype(F32)).astype(BF16)
                total = total + jnp.sum(cot[part, :].astype(F32), 0, keepdims=True)
        bdng[...] = total

    total = jnp.zeros((1, wup.shape[1]), F32)
    for start in range(0, tokens, step):
        part = pl.ds(start, step)
        z = dot_nn(norm[part, :], wup[...]) + bup[...].astype(F32)
        into = dot_nt(cot[part, :], wdn[...])
        value, slope = gelu_both(z)
        both[0, part, :] = value.astype(BF16)
        low = (into * slope).astype(BF16)
        both[1, part, :] = low
        total = total + jnp.sum(low.astype(F32), 0, keepdims=True)
    bupg[...] = total


def ffn_forward(ids, hid, cot, fam, ori, gain, bias, wup, bup, wdn, rows):
    tokens, d = hid.shape
    ff = wup.shape[1]
    tile = 512
    return pl.pallas_call(
        functools.partial(ffn_kernel, rows),
        grid_spec=pltpu.PrefetchScalarGridSpec(
            num_scalar_prefetch=1,
            grid=(ff // tile,),
            in_specs=[
                whole((tokens, d)),
                whole((tokens, d)),
                whole(fam.shape),
                whole(ori.shape),
                whole((1, d)),
                whole((1, d)),
                pl.BlockSpec((d, tile), lambda i, s: (0, i)),
                pl.BlockSpec((1, tile), lambda i, s: (0, i)),
                pl.BlockSpec((tile, d), lambda i, s: (i, 0)),
            ],
            out_specs=[
                whole((tokens, d)),
                pl.BlockSpec((2, tokens, tile), lambda i, s: (0, 0, i)),
                pl.BlockSpec((1, tile), lambda i, s: (0, i)),
                whole((1, d)),
            ],
        ),
        out_shape=[
            jax.ShapeDtypeStruct((tokens, d), BF16),
            jax.ShapeDtypeStruct((2, tokens, ff), BF16),
            jax.ShapeDtypeStruct((1, ff), F32),
            jax.ShapeDtypeStruct((1, d), F32),
        ],
        compiler_params=params(),
        cost_estimate=cost(4 * tokens * d * ff, 4 * tokens * ff + 4 * d * ff, tokens * ff),
        name="ffn_forward",
    )(ids, hid, cot, fam, ori, gain, bias, wup, bup, wdn)


def turn(entries, cosine, sine):
    even = lax.broadcasted_iota(jnp.int32, entries.shape, 1) % 2 == 0
    other = jnp.where(even, pltpu.roll(entries, 127, 1), pltpu.roll(entries, 1, 1))
    return entries * cosine + other * sine


def turn_back(entries, cosine, sine):
    even = lax.broadcasted_iota(jnp.int32, entries.shape, 1) % 2 == 0
    side = entries * sine
    other = jnp.where(even, pltpu.roll(side, 127, 1), pltpu.roll(side, 1, 1))
    return entries * cosine + other


def attend(head_size, query_ref, k_ref, v_ref, g_ref, cos, sin, o_ref, dq_ref, dk_ref, dv_ref, dkt, dvt):
    full = query_ref.shape[0]
    block = 256
    scale = head_size ** (-0.5)
    lane = lax.broadcasted_iota(jnp.int32, (block, 128), 1)
    below = lax.broadcasted_iota(jnp.int32, (block, block), 0) >= lax.broadcasted_iota(
        jnp.int32, (block, block), 1
    )
    dkt[...] = jnp.zeros_like(dkt)
    dvt[...] = jnp.zeros_like(dvt)
    for start in range(0, full, block):
        part = pl.ds(start, block)
        end = start + block
        query = query_ref[part, :]
        grad = g_ref[part, :]
        out = None
        dq = None
        for head in range(128 // head_size):
            mine = (lane >= head * head_size) & (lane < (head + 1) * head_size)
            qm = jnp.where(mine, query.astype(F32) * scale, 0.0).astype(BF16)
            gm = jnp.where(mine, grad.astype(F32), 0.0).astype(BF16)
            scores = dot_nt(qm, k_ref[0:end, :])
            last = jnp.where(below, scores[:, start:end], -1e30)
            scores = last if start == 0 else jnp.concatenate([scores[:, :start], last], 1)
            weights = jnp.exp(scores - jnp.max(scores, -1, keepdims=True))
            probs = weights * (1.0 / jnp.sum(weights, -1, keepdims=True))
            low = probs.astype(BF16)
            piece = dot_nn(low, v_ref[0:end, :])
            out = piece if out is None else jnp.where(mine, piece, out)
            pg = dot_nt(gm, v_ref[0:end, :])
            inner = jnp.sum(probs * pg, -1, keepdims=True)
            sg = (probs * (pg - inner)).astype(BF16)
            piece = dot_nn(sg, k_ref[0:end, :])
            dq = piece if dq is None else jnp.where(mine, piece, dq)
            dkt[:, 0:end] += dot_tn(qm, sg)
            dvt[:, 0:end] += dot_tn(gm, low)
        o_ref[part, :] = out.astype(BF16)
        dq_ref[part, :] = turn_back(dq * scale, cos[part, :], sin[part, :]).astype(BF16)
    for start in range(0, full, block):
        part = pl.ds(start, block)
        dk = dkt[:, start : start + block].T
        dk_ref[part, :] = turn_back(dk, cos[part, :], sin[part, :]).astype(BF16)
        dv_ref[part, :] = dvt[:, start : start + block].T.astype(BF16)


def events_for(tiles, pairs):
    first = 4 * tiles
    return {
        0: [(0, 0), (2, 0), (3, 0)],
        first + 1: [(0, 1), (1, 0), (2, 1), (3, 1)],
        first + 3: [(0, 2), (3, 2)],
        first + 5: [(1, 1), (2, 2), (0, 3), (3, 3)],
        first + 6: [(1, 2), (2, 3), (0, 4), (3, 4)],
        first + 7: [(1, 3), (2, 4)],
        first + 8: [(1, 4)],
    }


def middle_kernel(tiles, pairs, head_size, bits, orders, *refs):
    ids, own, far, cown, cfar, fam, ori, gain, bias, wqkv, wout, cos, sin = refs[:13]
    near_up, far_up, near_down, far_down = refs[13:17]
    norm, cot, o_ref, dq_ref, dk_ref, dv_ref, far_att, up_out, down_out = refs[17:26]
    heads, dkt, dvt, att_send, att_got, att_sems = refs[26:32]
    seg = own.shape[0]
    step = 256
    i = pl.program_id(0)
    me = lax.axis_index("seq")
    mine = device_bits(bits + 1)
    up_half = up_out.shape[1] // 2
    down_half = down_out.shape[1] // 2
    chunks = chunks_from(
        refs[32:],
        bits,
        mine,
        [
            (orders[0], near_up, far_up, pl.ds(0, up_half), up_out),
            (orders[1], near_up, far_up, pl.ds(up_half, up_half), up_out),
            (orders[2], near_down, far_down, pl.ds(0, down_half), down_out),
            (orders[3], near_down, far_down, pl.ds(down_half, down_half), down_out),
        ],
    )

    def happen(events):
        for chunk, stage in events:
            chunks[chunk].happen(stage)

    @pl.when(i == 0)
    def _():
        meet([partner_along(axis, mine) for axis in orders[0]])

    events = events_for(tiles, pairs)
    last = 4 * tiles + pairs
    for when, what in events.items():
        if when < last:

            @pl.when(i == when)
            def _():
                happen(what)

    @pl.when(i == 0)
    def _():
        emb = table_row(fam, ids[0]) + table_row(ori, ids[1])
        for source, csource, where in ((own, cown, me), (far, cfar, 1 - me)):
            for start in range(0, seg, step):
                part = pl.ds(start, step)
                there = pl.ds(pl.multiple_of(where * seg + start, step), step)
                hat, _ = normalise(source[part, :].astype(F32) + emb)
                norm[there, :] = (hat * gain[...].astype(F32) + bias[...].astype(F32)).astype(BF16)
                cot[there, :] = csource[part, :]

    lanes = wqkv.shape[1] // 128

    def att_crossing(pair):
        return remote(
            att_send.at[pair],
            att_got.at[pair],
            att_sems.at[0, pair],
            att_sems.at[1, pair],
            partner_along("seq", mine),
        )

    @pl.when(i < 2 * tiles)
    def _():
        for start in range(0, 2 * seg, step):
            part = pl.ds(start, step)
            lin = dot_nn(norm[part, :], wqkv[...])
            for lane in range(lanes):
                piece = turn(lin[:, lane * 128 : (lane + 1) * 128], cos[part, :], sin[part, :])
                heads[i * lanes + lane, part, :] = piece.astype(BF16)

    @pl.when((i >= 2 * tiles) & (i < 3 * tiles))
    def _():
        for start in range(0, 2 * seg, step):
            part = pl.ds(start, step)
            lin = dot_nn(norm[part, :], wqkv[...]).astype(BF16)
            for lane in range(lanes):
                heads[i * lanes + lane, part, :] = lin[:, lane * 128 : (lane + 1) * 128]

    @pl.when((i >= 3 * tiles) & (i < 4 * tiles))
    def _():
        for start in range(0, 2 * seg, step):
            part = pl.ds(start, step)
            lin = dot_nt(cot[part, :], wout[...]).astype(BF16)
            for lane in range(lanes):
                heads[i * lanes + lane, part, :] = lin[:, lane * 128 : (lane + 1) * 128]

    @pl.when(i >= 4 * tiles)
    def _():
        pair = i - 4 * tiles
        attend(
            head_size,
            heads.at[pair],
            heads.at[pairs + pair],
            heads.at[2 * pairs + pair],
            heads.at[3 * pairs + pair],
            cos,
            sin,
            o_ref,
            dq_ref,
            dk_ref,
            dv_ref,
            dkt,
            dvt,
        )
        att_send[pair] = o_ref[pl.ds(pl.multiple_of((1 - me) * seg, seg), seg), :]
        att_crossing(pair).start()

    @pl.when(i == last - 1)
    def _():
        for pair in range(pairs):
            att_crossing(pair).wait()
            far_att[:, pair * 128 : (pair + 1) * 128] = att_got[pair]
        happen(events[last])


def middle(ids, own, far, cown, cfar, fam, ori, gain, bias, wqkv, wout, cos, sin, up, down, orders, head_size, collective):
    seg, d = own.shape
    full = 2 * seg
    tile = 512
    tiles = d // tile
    pairs = d // 128
    bits = len(orders[0])
    near_up, far_up = up
    near_down, far_down = down
    up_size, ff = near_up.shape[1:]
    down_size = near_down.shape[1]
    smem = pl.BlockSpec(memory_space=pltpu.SMEM)
    anywhere = pl.BlockSpec(memory_space=pl.ANY)
    head_out = pl.BlockSpec((full, 128), lambda i: (0, jnp.maximum(i - 4 * tiles, 0)))
    rows = jax.ShapeDtypeStruct((full, d), BF16)
    return pl.pallas_call(
        functools.partial(middle_kernel, tiles, pairs, head_size, bits, orders),
        grid=(4 * tiles + pairs,),
        in_specs=[
            smem,
            whole((seg, d)),
            whole((seg, d)),
            whole((seg, d)),
            whole((seg, d)),
            whole(fam.shape),
            whole(ori.shape),
            whole((1, d)),
            whole((1, d)),
            pl.BlockSpec((d, tile), lambda i: (0, jnp.minimum(i, 3 * tiles - 1))),
            pl.BlockSpec((tile, d), lambda i: (jnp.clip(i - 3 * tiles, 0, tiles - 1), 0)),
            whole((full, 128)),
            whole((full, 128)),
        ]
        + [anywhere] * 4,
        out_specs=[
            whole((full, d)),
            whole((full, d)),
            head_out,
            head_out,
            head_out,
            head_out,
            whole((seg, d)),
            whole((up_size, ff)),
            whole((down_size, d)),
        ],
        out_shape=[
            rows,
            rows,
            rows,
            rows,
            rows,
            rows,
            jax.ShapeDtypeStruct((seg, d), BF16),
            jax.ShapeDtypeStruct((up_size, ff), F32),
            jax.ShapeDtypeStruct((down_size, d), F32),
        ],
        scratch_shapes=[
            pltpu.VMEM((4 * pairs, full, 128), BF16),
            pltpu.VMEM((128, full), F32),
            pltpu.VMEM((128, full), F32),
            pltpu.VMEM((pairs, seg, 128), BF16),
            pltpu.VMEM((pairs, seg, 128), BF16),
            pltpu.SemaphoreType.DMA((2, pairs)),
        ]
        + chunk_scratch(orders[0], up_size, ff // 2)
        + chunk_scratch(orders[1], up_size, ff // 2)
        + chunk_scratch(orders[2], down_size, d // 2)
        + chunk_scratch(orders[3], down_size, d // 2),
        compiler_params=params(collective_id=collective, has_side_effects=True),
        cost_estimate=cost(8 * full * d * d + 12 * full * full * d, 8 * d * d + 18 * full * d, full * full * H),
        name="middle",
    )(ids, own, far, cown, cfar, fam, ori, gain, bias, wqkv, wout, cos, sin, near_up, far_up, near_down, far_down)


def device_bits(bits):
    dp = lax.axis_index("dp")
    found = {bit: lax.rem(dp // (1 << bit), 2) for bit in range(bits)}
    found["seq"] = lax.axis_index("seq")
    return found


def block_place(axes, mine, upper, seq):
    place = 0
    for axis in axes:
        bit = seq if axis == "seq" else (upper >> (axis - 1)) & 1
        place = 2 * place + (1 - mine[axis] if bit else mine[axis])
    return place


def other_core():
    dp = lax.axis_index("dp")
    return (dp + 1 - 2 * lax.rem(dp, 2), lax.axis_index("seq"))


def meet(partners):
    barrier = pltpu.get_barrier_semaphore()
    for partner in partners:
        pl.semaphore_signal(barrier, inc=1, device_id=partner, device_id_type=MESH)
    pl.semaphore_wait(barrier, len(partners))


def remote(src, dst, send_sem, recv_sem, partner):
    return pltpu.make_async_remote_copy(
        src_ref=src,
        dst_ref=dst,
        send_sem=send_sem,
        recv_sem=recv_sem,
        device_id=partner,
        device_id_type=MESH,
    )


def split_blocks(value, keep, send, size, core, places):
    for index, there in enumerate(places):
        up, seq = index // 2, index % 2
        first = (4 * up + seq) * size
        second = first + 2 * size
        a = value[first : first + size, :].astype(BF16)
        b = value[second : second + size, :].astype(BF16)
        keep[there] = jnp.where(core == 0, a, b)
        send[there] = jnp.where(core == 0, b, a)


def add_into(keep, got):
    for index in range(keep.shape[0]):
        keep[index] = (keep[index].astype(F32) + got[index].astype(F32)).astype(BF16)


def wide_grad_kernel(bits, counts, orders, firsts, *refs):
    lefts, rights = refs[: len(counts)], refs[len(counts) : 2 * len(counts)]
    near_out, far_out, turned, keep, send, got, send_sem, recv_sem, out_sem = refs[2 * len(counts) :]
    steps = sum(counts)
    i = pl.program_id(0)
    mine = device_bits(bits)
    partner = other_core()
    blocks = keep.shape[1]
    size = keep.shape[2]
    tile = keep.shape[3]

    def crossing(step):
        return remote(send.at[step], got.at[step], send_sem.at[step], recv_sem.at[step], partner)

    def stores(step):
        columns = pl.ds(pl.multiple_of(step * tile, tile), tile)
        half = blocks // 2
        return (
            pltpu.make_async_copy(
                keep.at[step, pl.ds(0, half)], near_out.at[:, :, columns], out_sem.at[0, step]
            ),
            pltpu.make_async_copy(
                keep.at[step, pl.ds(half, half)], far_out.at[:, :, columns], out_sem.at[1, step]
            ),
        )

    @pl.when(i == 0)
    def _():
        meet([partner])

    start = 0
    for left, right, count, axes, first in zip(lefts, rights, counts, orders, firsts):
        places = [block_place(axes, mine, up, seq) for up in range(blocks // 2) for seq in range(2)]
        if first:

            @pl.when(i == start)
            def _():
                turned[...] = left[...].T

        @pl.when((i >= start) & (i < start + count))
        def _():
            value = dot_nn(turned[...], right[...])
            split_blocks(value, keep.at[i], send.at[i], size, mine[0], places)
            crossing(i).start()

        start += count

    def finish(step):
        crossing(step).wait()
        add_into(keep.at[step], got.at[step])
        for copy in stores(step):
            copy.start()

    @pl.when(i > 0)
    def _():
        finish(i - 1)

    @pl.when(i == steps - 1)
    def _():
        finish(i)
        for step in range(steps):
            for copy in stores(step):
                copy.wait()


def wide_grad(entries, tile, collective):
    tokens, d = entries[0][0].shape
    bits = len(entries[0][4])
    blocks = 1 << bits
    size = d // (2 * blocks)
    counts = [entry[3] for entry in entries]
    orders = [entry[4] for entry in entries]
    firsts = [index == 0 or entries[index][0] is not entries[index - 1][0] for index in range(len(entries))]
    steps = sum(counts)
    specs = []
    start = 0
    for entry in entries:

        def at(i, start=start, offset=entry[2], last=entry[3] - 1):
            return (1, 0, offset + jnp.clip(i - start, 0, last))

        specs.append(pl.BlockSpec((None, tokens, tile), at))
        start += entry[3]
    shape = jax.ShapeDtypeStruct((blocks // 2, size, steps * tile), BF16)
    anywhere = pl.BlockSpec(memory_space=pl.ANY)
    buffers = pltpu.VMEM((steps, blocks, size, tile), BF16)
    return pl.pallas_call(
        functools.partial(wide_grad_kernel, bits, counts, orders, firsts),
        grid=(steps,),
        in_specs=[whole((tokens, d)) for _ in entries] + specs,
        out_specs=[anywhere, anywhere],
        out_shape=[shape, shape],
        scratch_shapes=[
            pltpu.VMEM((d, tokens), BF16),
            buffers,
            buffers,
            buffers,
            pltpu.SemaphoreType.DMA((steps,)),
            pltpu.SemaphoreType.DMA((steps,)),
            pltpu.SemaphoreType.DMA((2, steps)),
        ],
        compiler_params=params(collective_id=collective, has_side_effects=True),
        cost_estimate=cost(2 * tokens * d * steps * tile, 4 * tokens * (d + steps * tile)),
        name="wide_grad",
    )(*[entry[0] for entry in entries], *[entry[1] for entry in entries])


def tall_grad_kernel(bits, orders, left, right, near_out, far_out, keep, send, got, send_sem, recv_sem, out_sem):
    i = pl.program_id(0)
    steps, _, size, d = keep.shape
    width = d // len(orders)
    mine = device_bits(bits)
    partner = other_core()
    half = steps

    def crossing(step):
        return remote(send.at[step], got.at[step], send_sem.at[step], recv_sem.at[step], partner)

    def store(step, seq, act):
        for part, axes in enumerate(orders):
            place = 0
            for axis in axes:
                if axis == "seq":
                    apart = lax.rem(mine["seq"] + seq, 2)
                else:
                    apart = lax.rem(step // (1 << (axis - 1)) + mine[axis], 2)
                place = 2 * place + apart
            columns = pl.ds(part * width, width)
            source = keep.at[step, seq, :, columns]
            sem = out_sem.at[step, seq, part]
            there = lax.rem(place, half)

            @pl.when(place < half)
            def _():
                act(pltpu.make_async_copy(source, near_out.at[there, :, columns], sem))

            @pl.when(place >= half)
            def _():
                act(pltpu.make_async_copy(source, far_out.at[there, :, columns], sem))

    @pl.when(i == 0)
    def _():
        meet([partner])

    value = dot_nn(left[...].T, right[...])
    split_blocks(value, keep.at[i], send.at[i], size, mine[0], [0, 1])
    crossing(i).start()

    def finish(step):
        crossing(step).wait()
        add_into(keep.at[step], got.at[step])
        for seq in range(2):
            store(step, seq, lambda copy: copy.start())

    @pl.when(i > 0)
    def _():
        finish(i - 1)

    @pl.when(i == steps - 1)
    def _():
        finish(i)
        for step in range(steps):
            for seq in range(2):
                store(step, seq, lambda copy: copy.wait())


def tall_grad(orders, left, right, collective):
    _, tokens, m = left.shape
    d = right.shape[1]
    bits = len(orders[0])
    steps = 1 << (bits - 1)
    tile = m // steps
    size = tile // 4
    shape = jax.ShapeDtypeStruct((steps, size, d), BF16)
    anywhere = pl.BlockSpec(memory_space=pl.ANY)
    buffers = pltpu.VMEM((steps, 2, size, d), BF16)
    return pl.pallas_call(
        functools.partial(tall_grad_kernel, bits, orders),
        grid=(steps,),
        in_specs=[pl.BlockSpec((None, tokens, tile), lambda i: (0, 0, i)), whole((tokens, d))],
        out_specs=[anywhere, anywhere],
        out_shape=[shape, shape],
        scratch_shapes=[
            buffers,
            buffers,
            buffers,
            pltpu.SemaphoreType.DMA((steps,)),
            pltpu.SemaphoreType.DMA((steps,)),
            pltpu.SemaphoreType.DMA((steps, 2, len(orders))),
        ],
        compiler_params=params(collective_id=collective, has_side_effects=True),
        cost_estimate=cost(2 * tokens * d * m, 2 * (tokens * m + d * m + tokens * d)),
        name="tall_grad",
    )(left, right)


def partner_along(axis, mine):
    dp = lax.axis_index("dp")
    seq = lax.axis_index("seq")
    if axis == "seq":
        return (dp, 1 - seq)
    return (dp + (1 - 2 * mine[axis]) * (1 << axis), seq)


class Chunk:
    def __init__(self, axes, mine, near, far, columns, out, keep, got, near_sem, send_sem, recv_sem):
        self.axes, self.mine, self.near, self.far = axes, mine, near, far
        self.columns, self.out, self.keep, self.got = columns, out, keep, got
        self.near_sem, self.send_sem, self.recv_sem = near_sem, send_sem, recv_sem

    def load(self):
        return pltpu.make_async_copy(self.near.at[:, :, self.columns], self.keep, self.near_sem)

    def crossing(self, stage):
        count = (1 << len(self.axes)) >> (stage + 1)
        if stage == 0 and self.far is not None:
            source = self.far.at[:, :, self.columns]
        else:
            source = self.keep.at[pl.ds(count, count)]
        return remote(
            source,
            self.got[stage],
            self.send_sem.at[stage],
            self.recv_sem.at[stage],
            partner_along(self.axes[stage], self.mine),
        )

    def begin(self):
        if self.near is not None:
            self.load().start()
        self.crossing(0).start()

    def advance(self, stage):
        if stage == 1 and self.near is not None:
            self.load().wait()
        self.crossing(stage - 1).wait()
        count = (1 << len(self.axes)) >> stage

        def add(index, carry):
            self.keep[index] = (self.keep[index].astype(F32) + self.got[stage - 1][index].astype(F32)).astype(BF16)
            return carry

        lax.fori_loop(0, count, add, 0)
        self.crossing(stage).start()

    def finish(self):
        last = len(self.axes) - 1
        self.crossing(last).wait()
        self.out[:, self.columns] = self.keep[0].astype(F32) + self.got[last][0].astype(F32)

    def happen(self, stage):
        if stage == 0:
            self.begin()
        elif stage == len(self.axes):
            self.finish()
        else:
            self.advance(stage)


def chunk_scratch(axes, size, width, farther=False):
    half = 1 << (len(axes) - 1)
    return (
        [pltpu.VMEM((2 * half if farther else half, size, width), BF16)]
        + [pltpu.VMEM((half >> stage, size, width), BF16) for stage in range(len(axes))]
        + [
            pltpu.SemaphoreType.DMA,
            pltpu.SemaphoreType.DMA((len(axes),)),
            pltpu.SemaphoreType.DMA((len(axes),)),
        ]
    )


def chunks_from(refs, bits, mine, wanted):
    stages = bits
    found = []
    each = 1 + stages + 3
    for index, (axes, near, far, columns, out) in enumerate(wanted):
        part = refs[index * each : (index + 1) * each]
        found.append(
            Chunk(axes, mine, near, far, columns, out, part[0], part[1 : 1 + stages], *part[1 + stages :])
        )
    return found


def after(entry, *others):
    return lax.optimization_barrier((entry, *others))[0]


TAIL_TILE = 512
TAIL_STEP = 256


def tail_events(sums_at):
    return {
        2: [(0, 1)],
        3: [(1, 1)],
        4: [(2, 1)],
        6: [(3, 1)],
        9: [(0, 2), (1, 2)],
        16: [(0, 3), (1, 3), (2, 2), (3, 2)],
        22: [(0, 4), (1, 4), (2, 3), (3, 3)],
        27: [(2, 4), (3, 4), (0, 5), (1, 5)],
        sums_at + 1: [(2, 5), (3, 5)],
    }


def tail_kernel(bits, orders, rows, marks, *refs):
    ids, norm_hbm, att_hbm, cot_hbm, dq_hbm, dk_hbm, dv_hbm, wqkv_hbm, wout_hbm = refs[:9]
    fam, ori, gain, bdn, bup_part, bdn_part, far_att = refs[9:16]
    both, wdn, wup, hid, cot = refs[16:21]
    layer_out, input_out, qkv_out, out_out, sums_out, all_out = refs[21:27]
    left, right, dq, dk, dv, wqkv, wout, turned, acc, ng_send, ng_own, ng_got = refs[27:39]
    gg, bg, rg, load_sem, ng_sem, held, got, vec, vgot, table, ssem, rsem, gsend, grecv = refs[39:53]
    out_start, out_end, in_start, in_end, sums_at = marks
    i = pl.program_id(0)
    me = lax.axis_index("seq")
    dp = lax.axis_index("dp")
    mine = device_bits(bits)
    d = left.shape[1]
    seg = ng_own.shape[0]
    step = TAIL_STEP
    per_row = seg // step
    chunks = chunks_from(
        refs[53:],
        len(orders[0]),
        mine,
        [
            (orders[0], None, None, pl.ds(0, d), qkv_out),
            (orders[1], None, None, pl.ds(d, d), qkv_out),
            (orders[2], None, None, pl.ds(2 * d, d), qkv_out),
            (orders[3], None, None, pl.ds(0, d), out_out),
        ],
    )
    loads = {
        name: pltpu.make_async_copy(source, there, load_sem.at[index])
        for index, (name, source, there) in enumerate(
            (
                ("norm", norm_hbm, left),
                ("dq", dq_hbm, dq),
                ("dk", dk_hbm, dk),
                ("dv", dv_hbm, dv),
                ("wqkv", wqkv_hbm, wqkv),
                ("cot", cot_hbm, right),
                ("wout", wout_hbm, wout),
                ("att", att_hbm, left),
            )
        )
    }
    partners = [partner_along(axis, mine) for axis in ["seq"] + list(range(bits))]

    def gradient(index, operand):
        chunk = chunks[index]
        size = chunk.keep.shape[1]
        value = dot_nn(turned[...], operand[...])
        for block in range(chunk.keep.shape[0]):
            place = 0
            for axis in orders[index]:
                bit = block & 1 if axis == "seq" else (block >> (axis + 1)) & 1
                place = 2 * place + (1 - mine[axis] if bit else mine[axis])
            chunk.keep[place] = value[block * size : (block + 1) * size, :].astype(BF16)
        chunk.begin()

    def back_into(there, half):
        for start in range(0, seg, step):
            part = pl.ds(pl.multiple_of(half * seg + start, step), step)
            total = dot_nt(dq[part, :], wqkv[:, 0:d])
            total = total + dot_nt(dk[part, :], wqkv[:, d : 2 * d])
            total = total + dot_nt(dv[part, :], wqkv[:, 2 * d : 3 * d])
            there[start : start + step, :] = total.astype(BF16)

    ng_crossing = remote(ng_send, ng_got, ng_sem.at[0], ng_sem.at[1], partners[0])

    @pl.when(i == 0)
    def _():
        for name in ("norm", "dq", "dk", "dv", "wqkv", "cot", "wout"):
            loads[name].start()
        meet(partners)
        loads["norm"].wait()
        turned[...] = left[...].T
        loads["att"].start()
        loads["dq"].wait()
        gradient(0, dq)

    for when, what in tail_events(sums_at).items():
        if when <= sums_at:

            @pl.when(i == when)
            def _():
                for chunk, stage in what:
                    chunks[chunk].happen(stage)

    @pl.when(i == 1)
    def _():
        loads["dk"].wait()
        gradient(1, dk)

    @pl.when(i == 2)
    def _():
        loads["dv"].wait()
        gradient(2, dv)

    @pl.when(i == 3)
    def _():
        loads["wqkv"].wait()
        back_into(ng_send, 1 - me)
        ng_crossing.start()

    @pl.when(i == 4)
    def _():
        loads["att"].wait()
        loads["cot"].wait()
        turned[...] = left[...].T
        gradient(3, right)

    @pl.when(i == 5)
    def _():
        back_into(ng_own, me)

    @pl.when((i >= out_start) & (i < out_end))
    def _():
        value = dot_nn(both[0], wdn[...])

        @pl.when(i == out_start)
        def _():
            acc[...] = value

        @pl.when(i > out_start)
        def _():
            acc[...] += value

    @pl.when((i >= in_start) & (i < in_end))
    def _():
        value = dot_nt(both[0], wup[...])

        @pl.when(i == in_start)
        def _():
            acc[...] = value

        @pl.when(i > in_start)
        def _():
            acc[...] += value

    @pl.when(i == out_end)
    def _():
        loads["wout"].wait()

    def home_block(index, own, far, own_offset):
        row = index // per_row
        within = pl.multiple_of(lax.rem(index, per_row) * step, step)
        there = pl.ds(pl.multiple_of(own_offset + within, step), step)
        return row, jnp.where(row == me, own[there, :], far[pl.ds(within, step), :])

    @pl.when((i >= out_end) & (i < in_start))
    def _():
        index = i - out_end
        row, att = home_block(index, left, far_att, me * seg)
        flag = jnp.where(row == 0, ids[1], ids[2])
        emb = table_row(fam, ids[0]) + table_row(ori, flag)
        part = pl.ds(pl.multiple_of(index * step, step), step)
        total = hid[...].astype(F32) + emb + dot_nn(att, wout[...])
        layer_out[...] = (total + (acc[part, :] + bdn[...].astype(F32))).astype(BF16)

    @pl.when(i == in_end)
    def _():
        ng_crossing.wait()
        gg[...] = jnp.zeros_like(gg)
        bg[...] = jnp.zeros_like(bg)
        rg[...] = jnp.zeros_like(rg)

    @pl.when((i >= in_end) & (i < sums_at))
    def _():
        index = i - in_end
        row, back = home_block(index, ng_own, ng_got, 0)
        flag = jnp.where(row == 0, ids[1], ids[2])
        emb = table_row(fam, ids[0]) + table_row(ori, flag)
        part = pl.ds(pl.multiple_of(index * step, step), step)
        hat, inv_std = normalise(hid[...].astype(F32) + emb)
        grad = acc[part, :] + back.astype(F32)
        gg[...] += jnp.sum(grad * hat, 0, keepdims=True)
        bg[...] += jnp.sum(grad, 0, keepdims=True)
        scaled = grad * gain[...].astype(F32)
        inner = (
            scaled
            - jnp.mean(scaled, -1, keepdims=True)
            - hat * jnp.mean(scaled * hat, -1, keepdims=True)
        )
        result = cot[...].astype(F32) + inv_std * inner
        input_out[...] = result
        sums = jnp.sum(result, 0, keepdims=True)
        which = lax.broadcasted_iota(jnp.int32, rg.shape, 0)
        rg[...] += jnp.where(which == flag, sums, 0.0)

    @pl.when(i == sums_at)
    def _():
        at = 0
        for source in (bup_part[...], bdn_part[...], gg[...], bg[...], rg[0:1, :], rg[1:2, :]):
            for lane in range(0, source.shape[1], 128):
                held[0, at : at + 1, :] = source[:, lane : lane + 128]
                at += 1
        both_rows = rg[0:1, :] + rg[1:2, :]
        for lane in range(0, d, 128):
            vec[lane // 128 : lane // 128 + 1, :] = both_rows[:, lane : lane + 128]
        extra = d // 128
        vec[extra:, :] = jnp.full((vec.shape[0] - extra, 128), 0.5, F32) * ids[0].astype(F32)
        for index, partner in enumerate(partners):
            main = remote(held.at[index], got.at[index], ssem.at[index], rsem.at[index], partner)
            main.start()
            if index == 0:
                side = remote(vec, vgot, gsend.at[0], grecv.at[0], partner)
            else:
                size = 1 << (index - 1)
                now = pl.ds(dp - lax.rem(dp, size), size)
                side = remote(table.at[now], table.at[now], gsend.at[index], grecv.at[index], partner)
            side.start()
            main.wait()
            total = held[index] + got[index]
            if index + 1 < len(partners):
                held[index + 1] = total
            else:
                sums_out[...] = total
            side.wait()
            if index == 0:
                table[dp] = vec[...] + vgot[...]
        all_out[...] = table[...]
        for chunk, stage in tail_events(sums_at)[sums_at + 1]:
            chunks[chunk].happen(stage)


def tail(ids, norm, att, row_cot, dq, dk, dv, wqkv, wout, fam, ori, gain, bdn, bup_part, bdn_part, far_att, both, wdn, wup, hid, cot, orders, rows, collective):
    tokens, d = hid.shape
    ff = wup.shape[1]
    bits = len(orders[0]) - 1
    count = 1 << bits
    seg = far_att.shape[0]
    tile, step = TAIL_TILE, TAIL_STEP
    tiles, blocks = ff // tile, tokens // step
    out_start = 6
    out_end = out_start + tiles
    in_start = out_end + blocks
    in_end = in_start + tiles
    sums_at = in_end + blocks
    marks = (out_start, out_end, in_start, in_end, sums_at)
    size = d // (2 * count)
    rounds = bits + 1
    lines = (ff + 5 * d) // 128
    vec_shape = (d // 128 + 8, 128)
    anywhere = pl.BlockSpec(memory_space=pl.ANY)

    def plane(i):
        late = i >= in_start
        return (late.astype(jnp.int32), 0, jnp.clip(jnp.where(late, i - in_start, i - out_start), 0, tiles - 1))

    def home(i):
        return (jnp.clip(jnp.where(i >= in_start, i - in_end, i - out_end), 0, blocks - 1), 0)

    square = pltpu.VMEM((tokens, d), BF16)
    piece = pltpu.VMEM((seg, d), BF16)
    row = pltpu.VMEM((1, d), F32)
    return pl.pallas_call(
        functools.partial(tail_kernel, bits, orders, rows, marks),
        grid=(sums_at + 1,),
        in_specs=[pl.BlockSpec(memory_space=pltpu.SMEM)]
        + [anywhere] * 8
        + [
            whole(fam.shape),
            whole(ori.shape),
            whole((1, d)),
            whole((1, d)),
            whole((1, ff)),
            whole((1, d)),
            whole((seg, d)),
            pl.BlockSpec((1, tokens, tile), plane),
            pl.BlockSpec((tile, d), lambda i: (jnp.clip(i - out_start, 0, tiles - 1), 0)),
            pl.BlockSpec((d, tile), lambda i: (0, jnp.clip(i - in_start, 0, tiles - 1))),
            pl.BlockSpec((step, d), home),
            pl.BlockSpec((step, d), lambda i: (jnp.clip(i - in_end, 0, blocks - 1), 0)),
        ],
        out_specs=[
            pl.BlockSpec((step, d), lambda i: (jnp.clip(i - out_end, 0, blocks - 1), 0)),
            pl.BlockSpec((step, d), lambda i: (jnp.clip(i - in_end, 0, blocks - 1), 0)),
            whole((size, 3 * d)),
            whole((size, d)),
            whole((lines, 128)),
            whole((count,) + vec_shape),
        ],
        out_shape=[
            jax.ShapeDtypeStruct((tokens, d), BF16),
            jax.ShapeDtypeStruct((tokens, d), F32),
            jax.ShapeDtypeStruct((size, 3 * d), F32),
            jax.ShapeDtypeStruct((size, d), F32),
            jax.ShapeDtypeStruct((lines, 128), F32),
            jax.ShapeDtypeStruct((count,) + vec_shape, F32),
        ],
        scratch_shapes=[
            square,
            square,
            square,
            square,
            square,
            pltpu.VMEM((d, 3 * d), BF16),
            pltpu.VMEM((d, d), BF16),
            pltpu.VMEM((d, tokens), BF16),
            pltpu.VMEM((tokens, d), F32),
            piece,
            piece,
            piece,
            row,
            row,
            pltpu.VMEM((2, d), F32),
            pltpu.SemaphoreType.DMA((8,)),
            pltpu.SemaphoreType.DMA((2,)),
            pltpu.VMEM((rounds, lines, 128), F32),
            pltpu.VMEM((rounds, lines, 128), F32),
            pltpu.VMEM(vec_shape, F32),
            pltpu.VMEM(vec_shape, F32),
            pltpu.VMEM((count,) + vec_shape, F32),
            pltpu.SemaphoreType.DMA((rounds,)),
            pltpu.SemaphoreType.DMA((rounds,)),
            pltpu.SemaphoreType.DMA((rounds,)),
            pltpu.SemaphoreType.DMA((rounds,)),
        ]
        + [entry for axes in orders for entry in chunk_scratch(axes, size, d, True)],
        compiler_params=pltpu.CompilerParams(
            vmem_limit_bytes=67043328, collective_id=collective, has_side_effects=True
        ),
        cost_estimate=cost(16 * tokens * d * d + 4 * tokens * d * ff, 8 * d * ff + 40 * tokens * d),
        name="tail",
    )(ids, norm, att, row_cot, dq, dk, dv, wqkv, wout, fam, ori, gain, bdn, bup_part, bdn_part, far_att, both, wdn, wup, hid, cot)


def body_by_rows(
    hidden_in,
    family,
    orient,
    norm_gain,
    norm_bias,
    qkv_weight,
    out_weight,
    up_weight,
    up_bias,
    down_weight,
    down_bias,
    family_table,
    orient_table,
    cotangent,
):
    rows, seg, d = hidden_in.shape
    ff = up_weight.shape[1]
    tokens = rows * seg
    full = 2 * seg
    dp_count = lax.axis_size("dp")
    bits = int(math.log2(dp_count))
    upper = dp_count // 2
    dp = lax.axis_index("dp")
    seq = lax.axis_index("seq")
    ring = [(0, 1), (1, 0)]

    def mine(pair):
        return lax.dynamic_index_in_dim(pair, seq, 0, keepdims=False)

    def theirs(pair):
        return lax.dynamic_index_in_dim(pair, 1 - seq, 0, keepdims=False)

    far_hidden = lax.ppermute(theirs(hidden_in), "seq", ring)
    far_cot = lax.ppermute(theirs(cotangent), "seq", ring)

    gain = norm_gain.reshape(1, d)
    bias = norm_bias.reshape(1, d)
    hid = hidden_in.reshape(tokens, d)
    cot = cotangent.reshape(tokens, d)
    ids = jnp.concatenate([family, orient])
    row_ids = jnp.stack([family[0], mine(orient)])

    zs = list(range(2, bits))
    order_a = [1] + zs + ["seq"]
    order_b = [1, "seq"] + zs
    order_c = ["seq", 1] + zs
    order_d = [2, "seq", 1] + zs[1:]
    order_e = [2, 1] + zs[1:] + ["seq"]
    late_orders = [[0] + order_a, [0] + order_e, [0] + order_a, [0] + order_e]
    ffn_orders = [order_a, order_b, order_c, order_d]

    normed, both, up_bias_part, down_bias_part = ffn_forward(
        ids, hid, cot, family_table, orient_table, gain, bias, up_weight, up_bias.reshape(1, ff), down_weight, rows
    )
    half_tiles = ff // 2048
    ready = after(normed, far_hidden)
    up = wide_grad([(ready, both, 0, half_tiles, order_a), (ready, both, half_tiles, half_tiles, order_b)], 1024, 1)
    down = tall_grad([order_c, order_d], both, after(cot, up[0], far_cot), 2)

    cosine, sine = rope_tables(jnp.arange(full).astype(F32), 128)
    row_normed, row_cot, att, dq, dk, dv, far_att, up_total, down_total = middle(
        row_ids,
        mine(hidden_in),
        far_hidden,
        mine(cotangent),
        far_cot,
        family_table,
        orient_table,
        gain,
        bias,
        qkv_weight,
        out_weight,
        cosine,
        sine,
        up,
        down,
        ffn_orders,
        d // H,
        3,
    )
    layer_out, input_grad, qkv_total, out_total, sums, gathered = tail(
        ids,
        row_normed,
        att,
        row_cot,
        dq,
        dk,
        dv,
        qkv_weight,
        out_weight,
        family_table,
        orient_table,
        gain,
        down_bias.reshape(1, d),
        up_bias_part,
        down_bias_part,
        far_att,
        both,
        down_weight,
        up_weight,
        hid,
        cot,
        late_orders,
        rows,
        4,
    )
    flat = sums.reshape(-1)
    up_bias_sum = flat[:ff]
    down_bias_sum, gain_sum, bias_sum = flat[ff : ff + 3 * d].reshape(3, d)
    orient_sum = flat[ff + 3 * d :].reshape(2, d)
    families = family_table.shape[0]
    hot = gathered[:, -1, 0].astype(jnp.int32)[None, :] == jnp.arange(families)[:, None]
    family_sum = jnp.dot(
        hot.astype(F32), gathered[:, :-8].reshape(dp_count, d), precision=lax.Precision.HIGHEST
    )
    return (
        layer_out.reshape(rows, seg, d),
        input_grad.reshape(rows, seg, d),
        gain_sum,
        bias_sum,
        qkv_total,
        out_total,
        up_total,
        up_bias_sum,
        down_total,
        down_bias_sum,
        family_sum,
        orient_sum,
    )


def body(*args):
    hidden_in = args[0]
    dp_count = lax.axis_size("dp")
    two_rows = lax.axis_size("seq") == 2 and hidden_in.shape[0] == 2
    if two_rows and dp_count >= 4 and dp_count & (dp_count - 1) == 0:
        return body_by_rows(*args)
    return body_by_heads(*args)


def solution(mesh):
    return jax.shard_map(
        body,
        mesh=mesh,
        in_specs=(
            P("dp", "seq", None),
            P("dp"),
            P("dp"),
            P(),
            P(),
            P(),
            P(),
            P(),
            P(),
            P(),
            P(),
            P(),
            P(),
            P("dp", "seq", None),
        ),
        out_specs=(
            P("dp", "seq", None),
            P("dp", "seq", None),
            P(),
            P(),
            P(("dp", "seq"), None),
            P(("dp", "seq"), None),
            P(("dp", "seq"), None),
            P(),
            P(("dp", "seq"), None),
            P(),
            P(),
            P(),
        ),
        check_vma=False,
    )
```

profile of v0, /device:TPU:0, one launch (start us, length us, event | category | flops | bytes accessed | tf_op | source)
XLA Modules:
  0.0 312.8 jit_solution(15298624401494145361)
XLA Ops:
  0.6 0.0 copy-start.1
  0.7 2.8 dynamic-slice_bitcast_fusion.2
  3.5 0.0 copy-start.7
  3.5 0.0 copy-start.8
  3.5 0.0 copy-start.6
  3.5 0.0 copy-start.11
  3.5 3.0 collective-permute-start
  6.5 0.0 copy-done.1
  6.5 1.1 dynamic-slice_bitcast_fusion
  7.7 0.0 collective-permute-start.1
  7.7 0.0 copy-done.7
  7.7 0.6 reshape.124.gain.refs_7_.refs_11_
  9.0 0.0 copy-done.8
  9.0 0.6 reshape.125.bias.refs_8_
  9.6 0.0 copy-done.6
  9.6 0.6 reshape.128.bup
  10.2 0.0 copy-done.11
  10.2 0.6 pad_add_fusion.ids.refs_0_
  10.8 0.0 copy-start.9
  10.8 32.2 %ffn_forward.1 = (bf16[1024,1024]{1,0:T(8,128)(2,1)}, bf16[2,1024,4096]{2,1,0:T(8,128)(2,1)}, f32[1,4096]{1,0:T(1,128)}, f32[1,1024]{1,0:T(1,128)}) custom-call(s32[3]{0:T(128)} %pad_add_fusion.ids.refs_0_, bf16[1024,1024]{1,0:T(8,128)(2,1)} %bitcast.25, bf16[1024,1024]{1,0:T(8,128)(2,1)} %bitcast.27, bf16[64,1024]{1,0:T(8,128)(2,1)} %refs_9_.3, ...), custom_call_target="tpu_custom_call" | custom-call | flops 17179869184 | bytes 33554432 | tf_op jit(solution)/shard_map/ffn_forward/pallas_call | solution.py:382
  42.9 0.6 dynamic_slice.17
  43.5 0.0 copy-done.9
  43.5 0.6 reshape.129.refs_12_
  44.1 1.2 pad_add_fusion.1.refs_0_
  45.4 3.1 fusion.2
  48.5 0.0 collective-permute-done.refs_2_
  48.5 0.0 copy-start.10
  48.5 18.9 %wide_grad.1 = (bf16[8,32,4096]{2,1,0:T(8,128)(2,1)}, bf16[8,32,4096]{2,1,0:T(8,128)(2,1)}) custom-call(bf16[1024,1024]{1,0:T(8,128)(2,1)} %get-tuple-element.38.refs_0_.refs_1_, bf16[1024,1024]{1,0:T(8,128)(2,1)} %get-tuple-element.38.refs_0_.refs_1_, bf16[2,1024,4096]{2,1,0:T(8,128)(2,1)} %get-tuple-element.39.refs_2_.refs_3_.left.refs_16_, ...), custom_call_target="tpu_custom_call" | custom-call | flops 8589934592 | bytes 20971520 | tf_op jit(solution)/shard_map/wide_grad/pallas_call | solution.py:819
  67.4 0.0 copy-done.10
  67.4 0.0 collective-permute-done.1.refs_4_
  67.4 17.3 %tall_grad.1 = (bf16[8,128,1024]{2,1,0:T(8,128)(2,1)}, bf16[8,128,1024]{2,1,0:T(8,128)(2,1)}) custom-call(bf16[2,1024,4096]{2,1,0:T(8,128)(2,1)} %get-tuple-element.39.refs_2_.refs_3_.left.refs_16_, bf16[1024,1024]{1,0:T(8,128)(2,1)} %bitcast.28), custom_call_target="tpu_custom_call" | custom-call | flops 8589934592 | bytes 18874368 | tf_op jit(solution)/shard_map/tall_grad/pallas_call | solution.py:909
  84.7 109.1 %middle.1 = (bf16[1024,1024]{1,0:T(8,128)(2,1)}, bf16[1024,1024]{1,0:T(8,128)(2,1)}, bf16[1024,1024]{1,0:T(8,128)(2,1)}, bf16[1024,1024]{1,0:T(8,128)(2,1)}, bf1...) custom-call(s32[2]{0:T(128)} %pad_add_fusion.1.refs_0_, ...), custom_call_target="tpu_custom_call" | custom-call | flops 21474836480 | bytes 27262976 | tf_op jit(solution)/shard_map/middle/pallas_call | solution.py:620
  193.8 103.6 %tail.1 = (bf16[1024,1024]{1,0:T(8,128)(2,1)}, f32[1024,1024]{1,0:T(8,128)}, f32[32,3072]{1,0:T(8,128)}, f32[32,1024]{1,0:T(8,128)}, f32[72,128]{1,0:T(8,128)}, /*index=5*/f32[16,16,128]{2,1,0:T(8,128)}) custom-call(s32[3]{0:T(128)} %pad_add_fusion.ids.refs_0_, bf16[1024,1024]{1,0:T(8,128)(2,1)} %get-tuple-element.45.refs_1_, ...), custom_call_target="tpu_custom_call" | custom-call | flops 34359738368 | bytes 75497472 | tf_op jit(solution)/shard_map/tail/pallas_call | solution.py:1291
  297.4 0.8 slice.27
  298.2 1.2 convert_reduce_fusion
  299.5 0.7 slice.28
  300.2 1.3 slice_bitcast_fusion
  301.5 1.3 slice_bitcast_fusion.1
  302.8 0.6 reshape.133
  303.4 0.9 fusion.3
  304.3 0.0 copy-start
  304.4 3.2 %copy.38 = bf16[2,512,1024]{2,1,0:T(8,128)(2,1)} copy(bf16[2,512,1024]{2,1,0:T(8,128)(2,1)} %bitcast.30) | data formatting | bytes 4194304
  307.6 0.0 copy-done
  307.6 0.0 copy-start.4
  307.6 0.0 copy-start.5
  307.6 0.0 copy-start.3
  307.6 2.0 copy.39
  309.6 0.0 copy-done.4
  309.6 0.0 copy-start.2
  309.6 0.7 copy.40
  310.4 0.0 copy-done.5
  310.4 0.7 copy.41
  311.0 0.0 copy-done.3
  311.0 0.8 copy.42
  311.8 0.0 copy-done.2
  311.8 0.8 copy.43
  (3 shorter events, 0.0 us)
Async XLA Ops:
  0.6 5.9 %copy-start.1 = (bf16[2,512,1024]{2,1,0:T(8,128)(2,1)S(1)}, bf16[2,512,1024]{2,1,0:T(8,128)(2,1)}, u32[]{:S(2)}) copy-start(bf16[2,512,1024]{2,1,0:T(8,128)(2,1)} %param.27) | copy-start | bytes 6291460
  3.5 4.2 %copy-start.7 = (bf16[1024]{0:T(1024)(128)(2,1)S(1)}, bf16[1024]{0:T(1024)(128)(2,1)}, u32[]{:S(2)}) copy-start(bf16[1024]{0:T(1024)(128)(2,1)} %param.17) | copy-start | bytes 6148
  3.5 5.5 %copy-start.8 = (bf16[1024]{0:T(1024)(128)(2,1)S(1)}, bf16[1024]{0:T(1024)(128)(2,1)}, u32[]{:S(2)}) copy-start(bf16[1024]{0:T(1024)(128)(2,1)} %param.18) | copy-start | bytes 6148
  3.5 6.1 %copy-start.6 = (bf16[4096]{0:T(1024)(128)(2,1)S(1)}, bf16[4096]{0:T(1024)(128)(2,1)}, u32[]{:S(2)}) copy-start(bf16[4096]{0:T(1024)(128)(2,1)} %param.22) | copy-start | bytes 24580
  3.5 6.7 %copy-start.11 = (s32[2]{0:T(128)S(1)}, s32[2]{0:T(128)}, u32[]{:S(2)}) copy-start(s32[2]{0:T(128)} %param.16) | copy-start | bytes 28
  3.5 45.0 %collective-permute-start = (bf16[512,1024]{1,0:T(8,128)(2,1)S(1)}, bf16[512,1024]{1,0:T(8,128)(2,1)S(1)}, u32[]{:S(2)}, u32[]{:S(2)}) collective-permute-start(bf16[512,1024]{1,0:T(8,128)(2,1)S(1)} %get-tuple-element.64), channel_id=1, source_target_pairs={{0,1},{1,0},{2,3},{3,2},{4,5},{5,4},{6,7},{7,6},{8,9},{9,8},{10,11... | collective-permute-start | bytes 3145736 | tf_op jit(solution)/shard_map/ppermute | solution.py:1396
  7.7 59.8 %collective-permute-start.1 = (bf16[512,1024]{1,0:T(8,128)(2,1)S(1)}, bf16[512,1024]{1,0:T(8,128)(2,1)}, u32[]{:S(2)}, u32[]{:S(2)}) collective-permute-start(bf16[512,1024]{1,0:T(8,128)(2,1)S(1)} %get-tuple-element.62), channel_id=1, source_target_pairs={{0,1},{1,0},{2,3},{3,2},{4,5},{5,4},{6,7},{7,6},{8,9},{9,8},{10,11... | collective-permute-start | bytes 3145736 | tf_op jit(solution)/shard_map/ppermute | solution.py:1397
  10.8 32.8 %copy-start.9 = (bf16[1024]{0:T(1024)(128)(2,1)S(1)}, bf16[1024]{0:T(1024)(128)(2,1)}, u32[]{:S(2)}) copy-start(bf16[1024]{0:T(1024)(128)(2,1)} %param.24) | copy-start | bytes 6148
  48.5 18.9 %copy-start.10 = (bf16[512,1024]{1,0:T(8,128)(2,1)}, bf16[512,1024]{1,0:T(8,128)(2,1)S(1)}, u32[]{:S(2)}) copy-start(bf16[512,1024]{1,0:T(8,128)(2,1)S(1)} %collective-permute-done.refs_2_) | copy-start | bytes 3145732
  304.3 3.2 %copy-start = (f32[1024,1024]{1,0:T(8,128)S(1)}, f32[1024,1024]{1,0:T(8,128)}, u32[]{:S(2)}) copy-start(f32[1024,1024]{1,0:T(8,128)} %get-tuple-element.55) | copy-start | bytes 12582916
  307.6 2.0 copy-start.4
  307.6 2.8 copy-start.5
  307.6 3.4 %copy-start.3 = (f32[32,4096]{1,0:T(8,128)S(1)}, f32[32,4096]{1,0:T(8,128)}, u32[]{:S(2)}) copy-start(f32[32,4096]{1,0:T(8,128)} %get-tuple-element.91) | copy-start | bytes 1572868
  309.6 2.2 copy-start.2
where the time goes:
time: 316 us; the launch traced here: 313 us
  Pallas kernels  281 us (89%)
  local copies, waits for them, and re-layouts  20 us (6%)
  other arithmetic  6.15 us (2%)
    pallas_call x1, Pallas kernels, middle(): pl.pallas_call(functools.partial(middle_kernel, tiles, pairs, head_size,...  109 us
    pallas_call x1, Pallas kernels, tail(): pl.pallas_call(functools.partial(tail_kernel, bits, orders, rows, marks),...  104 us
    pallas_call x1, Pallas kernels, ffn_forward(): pl.pallas_call(functools.partial(ffn_kernel, rows), grid_spec=pltpu.Prefe...  32.2 us
    pallas_call x1, Pallas kernels, wide_grad(): pl.pallas_call(functools.partial(wide_grad_kernel, bits, counts, orders,...  18.9 us
    pallas_call x1, Pallas kernels, tall_grad(): pl.pallas_call(functools.partial(tall_grad_kernel, bits, orders), grid=(s...  17.3 us
    unnamed x30, local copies, waits for them, and re-layouts  8.29 us
  transfers between devices with their start and end apart: 2, of which 0 were waited for; matrix products, arithmetic and copies ran while one was open for 3% of the time, Pallas kernels for 16%

commit v1 on v0

--- a/solution.py
+++ b/solution.py
@@ -339,10 +339,10 @@
 
 def gelu_both(z):
     square = z * z
-    t = jnp.tanh(GELU_C * z * (1.0 + 0.044715 * square))
-    half = 0.5 * (1.0 + t)
-    slope = half + (0.5 * GELU_C) * z * (1.0 - t * t) * (1.0 + (3 * 0.044715) * square)
-    return z * half, slope
+    half = 0.5 + 0.5 * jnp.tanh(z * (GELU_C + (GELU_C * 0.044715) * square))
+    value = z * half
+    slope = half + value * (1.0 - half) * (2 * GELU_C + (6 * GELU_C * 0.044715) * square)
+    return value, slope
 
 
 def ffn_kernel(rows, ids, hid, cot, fam, ori, gain, bias, wup, bup, wdn, norm, both, bupg, bdng):
@@ -362,17 +362,19 @@
                 total = total + jnp.sum(cot[part, :].astype(F32), 0, keepdims=True)
         bdng[...] = total
 
-    total = jnp.zeros((1, wup.shape[1]), F32)
+    width = wup.shape[1]
+    total = jnp.zeros((8, width), F32)
+    lin = dot_nn(norm[...], wup[...])
+    into = dot_nt(cot[...], wdn[...])
+    step = 64
     for start in range(0, tokens, step):
         part = pl.ds(start, step)
-        z = dot_nn(norm[part, :], wup[...]) + bup[...].astype(F32)
-        into = dot_nt(cot[part, :], wdn[...])
-        value, slope = gelu_both(z)
+        value, slope = gelu_both(lin[start : start + step] + bup[...].astype(F32))
+        low = into[start : start + step] * slope
         both[0, part, :] = value.astype(BF16)
-        low = (into * slope).astype(BF16)
-        both[1, part, :] = low
-        total = total + jnp.sum(low.astype(F32), 0, keepdims=True)
-    bupg[...] = total
+        both[1, part, :] = low.astype(BF16)
+        total = total + jnp.sum(low.reshape(step // 8, 8, width), 0)
+    bupg[...] = jnp.sum(total, 0, keepdims=True)
 
 
 def ffn_forward(ids, hid, cot, fam, ori, gain, bias, wup, bup, wdn, rows):
@@ -431,40 +433,51 @@
     full = query_ref.shape[0]
     block = 256
     scale = head_size ** (-0.5)
-    lane = lax.broadcasted_iota(jnp.int32, (block, 128), 1)
+    first = lax.broadcasted_iota(jnp.int32, (block, 128), 1) < head_size
     below = lax.broadcasted_iota(jnp.int32, (block, block), 0) >= lax.broadcasted_iota(
         jnp.int32, (block, block), 1
     )
     dkt[...] = jnp.zeros_like(dkt)
     dvt[...] = jnp.zeros_like(dvt)
+
+    def by_head(entries):
+        none = jnp.zeros_like(entries)
+        return jnp.concatenate([jnp.where(first, entries, none), jnp.where(first, none, entries)], 0)
+
+    def front(start):
+        part, end = pl.ds(start, block), start + block
+        query = by_head((query_ref[part, :].astype(F32) * scale).astype(BF16))
+        grad = by_head(g_ref[part, :])
+        return query, grad, dot_nt(query, k_ref[0:end, :]), dot_nt(grad, v_ref[0:end, :])
+
+    def back(start, query, grad, scores, into):
+        part, end = pl.ds(start, block), start + block
+        lows, slopes = [], []
+        for head in range(2):
+            rows = slice(head * block, (head + 1) * block)
+            score = scores[rows]
+            last = jnp.where(below, score[:, start:end], -1e30)
+            score = last if start == 0 else jnp.concatenate([score[:, :start], last], 1)
+            weights = jnp.exp(score - jnp.max(score, -1, keepdims=True))
+            probs = weights * (1.0 / jnp.sum(weights, -1, keepdims=True))
+            lows.append(probs.astype(BF16))
+            inner = jnp.sum(probs * into[rows], -1, keepdims=True)
+            slopes.append((probs * (into[rows] - inner)).astype(BF16))
+        low = jnp.concatenate(lows, 0)
+        slope = jnp.concatenate(slopes, 0)
+        out = dot_nn(low, v_ref[0:end, :])
+        dq = dot_nn(slope, k_ref[0:end, :])
+        o_ref[part, :] = jnp.where(first, out[:block], out[block:]).astype(BF16)
+        dq = jnp.where(first, dq[:block], dq[block:]) * scale
+        dq_ref[part, :] = turn_back(dq, cos[part, :], sin[part, :]).astype(BF16)
+        dkt[:, 0:end] += dot_tn(query, slope)
+        dvt[:, 0:end] += dot_tn(grad, low)
+
+    ready = front(0)
     for start in range(0, full, block):
-        part = pl.ds(start, block)
-        end = start + block
-        query = query_ref[part, :]
-        grad = g_ref[part, :]
-        out = None
-        dq = None
-        for head in range(128 // head_size):
-            mine = (lane >= head * head_size) & (lane < (head + 1) * head_size)
-            qm = jnp.where(mine, query.astype(F32) * scale, 0.0).astype(BF16)
-            gm = jnp.where(mine, grad.astype(F32), 0.0).astype(BF16)
-            scores = dot_nt(qm, k_ref[0:end, :])
-            last = jnp.where(below, scores[:, start:end], -1e30)
-            scores = last if start == 0 else jnp.concatenate([scores[:, :start], last], 1)
-            weights = jnp.exp(scores - jnp.max(scores, -1, keepdims=True))
-            probs = weights * (1.0 / jnp.sum(weights, -1, keepdims=True))
-            low = probs.astype(BF16)
-            piece = dot_nn(low, v_ref[0:end, :])
-            out = piece if out is None else jnp.where(mine, piece, out)
-            pg = dot_nt(gm, v_ref[0:end, :])
-            inner = jnp.sum(probs * pg, -1, keepdims=True)
-            sg = (probs * (pg - inner)).astype(BF16)
-            piece = dot_nn(sg, k_ref[0:end, :])
-            dq = piece if dq is None else jnp.where(mine, piece, dq)
-            dkt[:, 0:end] += dot_tn(qm, sg)
-            dvt[:, 0:end] += dot_tn(gm, low)
-        o_ref[part, :] = out.astype(BF16)
-        dq_ref[part, :] = turn_back(dq * scale, cos[part, :], sin[part, :]).astype(BF16)
+        later = front(start + block) if start + block < full else None
+        back(start, *ready)
+        ready = later
     for start in range(0, full, block):
         part = pl.ds(start, block)
         dk = dkt[:, start : start + block].T
@@ -472,40 +485,80 @@
         dv_ref[part, :] = dvt[:, start : start + block].T.astype(BF16)
 
 
-def events_for(tiles, pairs):
-    first = 4 * tiles
-    return {
-        0: [(0, 0), (2, 0), (3, 0)],
-        first + 1: [(0, 1), (1, 0), (2, 1), (3, 1)],
-        first + 3: [(0, 2), (3, 2)],
-        first + 5: [(1, 1), (2, 2), (0, 3), (3, 3)],
-        first + 6: [(1, 2), (2, 3), (0, 4), (3, 4)],
-        first + 7: [(1, 3), (2, 4)],
-        first + 8: [(1, 4)],
-    }
+FFN_ORDERS = [
+    [2, 3, 1, "seq"],
+    [2, 1, 3, "seq"],
+    ["seq", 1, 2, 3],
+    ["seq", 3, 1, 2],
+    [1, "seq", 2, 3],
+    ["seq", 2, 1, 3],
+    [2, 1, 3, "seq"],
+    ["seq", 3, 1, 2],
+]
+LATE_ORDERS = [
+    [0, 1, 2, "seq", 3],
+    [0, 2, 1, "seq", 3],
+    [0, 1, 2, 3, "seq"],
+    [0, 2, 1, "seq", 3],
+]
+FFN_EVENTS = {
+    0: [(0, 0), (1, 0), (2, 0), (3, 0)],
+    9: [(4, 0), (5, 0), (6, 0), (7, 0)],
+    10: [(0, 1), (1, 1), (2, 1), (3, 1)],
+    18: [(1, 2), (2, 2), (4, 1), (0, 2), (5, 1), (7, 1), (3, 2)],
+    19: [(6, 1), (0, 3)],
+    20: [(1, 3), (2, 3), (3, 3), (4, 2), (0, 4)],
+    21: [(1, 4), (5, 2), (6, 2), (7, 2)],
+    22: [(2, 4), (3, 4), (4, 3)],
+    23: [(5, 3), (6, 3), (7, 3), (4, 4)],
+    24: [(6, 4), (5, 4), (7, 4)],
+}
+LATE_EVENTS = {
+    2: [(0, 1)],
+    3: [(1, 1)],
+    4: [(2, 1)],
+    6: [(3, 1)],
+    8: [(0, 2), (1, 2)],
+    13: [(2, 2)],
+    14: [(1, 3)],
+    16: [(0, 3)],
+    18: [(1, 4), (3, 2)],
+    19: [(2, 3)],
+    20: [(0, 4)],
+    22: [(1, 5)],
+    24: [(3, 3)],
+    26: [(0, 5), (2, 4)],
+    29: [(3, 4)],
+    30: [(2, 5), (3, 5)],
+}
 
 
 def middle_kernel(tiles, pairs, head_size, bits, orders, *refs):
-    ids, own, far, cown, cfar, fam, ori, gain, bias, wqkv, wout, cos, sin = refs[:13]
-    near_up, far_up, near_down, far_down = refs[13:17]
-    norm, cot, o_ref, dq_ref, dk_ref, dv_ref, far_att, up_out, down_out = refs[17:26]
-    heads, dkt, dvt, att_send, att_got, att_sems = refs[26:32]
+    ids, own, far, home_cot, cfar, act, fam, ori, gain, bias, wqkv, wout, cos, sin = refs[:14]
+    near_up, far_up = refs[14:16]
+    norm, cot, o_ref, dq_ref, dk_ref, dv_ref, far_att, up_out, down_out, near_down, far_down = refs[16:27]
+    heads, dkt, dvt, att_send, att_got, att_sems, keep, send, got, send_sem, recv_sem, out_sem = refs[27:39]
     seg = own.shape[0]
     step = 256
-    i = pl.program_id(0)
+    base = 1 << (bits - 1)
+    now = pl.program_id(0)
+    i = now - base
     me = lax.axis_index("seq")
-    mine = device_bits(bits + 1)
-    up_half = up_out.shape[1] // 2
-    down_half = down_out.shape[1] // 2
+    mine = device_bits(bits)
+    parts = len(orders) // 2
+    up_part = up_out.shape[1] // parts
+    down_part = down_out.shape[1] // parts
     chunks = chunks_from(
-        refs[32:],
+        refs[39:],
         bits,
         mine,
         [
-            (orders[0], near_up, far_up, pl.ds(0, up_half), up_out),
-            (orders[1], near_up, far_up, pl.ds(up_half, up_half), up_out),
-            (orders[2], near_down, far_down, pl.ds(0, down_half), down_out),
-            (orders[3], near_down, far_down, pl.ds(down_half, down_half), down_out),
+            (orders[part], near_up, far_up, pl.ds(part * up_part, up_part), up_out)
+            for part in range(parts)
+        ]
+        + [
+            (orders[parts + part], near_down, far_down, pl.ds(part * down_part, down_part), down_out)
+            for part in range(parts)
         ],
     )
 
@@ -513,29 +566,82 @@
         for chunk, stage in events:
             chunks[chunk].happen(stage)
 
-    @pl.when(i == 0)
-    def _():
-        meet([partner_along(axis, mine) for axis in orders[0]])
-
-    events = events_for(tiles, pairs)
-    last = 4 * tiles + pairs
-    for when, what in events.items():
+    @pl.when(now == 0)
+    def _():
+        meet([partner_along(axis, mine) for axis in [0] + orders[0]])
+
+    last = base + 4 * tiles + pairs
+    for when, what in FFN_EVENTS.items():
         if when < last:
 
-            @pl.when(i == when)
+            @pl.when(now == when)
             def _():
                 happen(what)
 
+    def crossing(index):
+        slot = lax.rem(index, 2)
+        return remote(
+            send.at[slot], got.at[slot], send_sem.at[slot], recv_sem.at[slot], partner_along(0, mine)
+        )
+
+    def store(index, act_on):
+        slot = lax.rem(index, 2)
+        width = home_cot.shape[1] // parts
+        for seq in range(2):
+            for part in range(parts):
+                place = 0
+                for axis in orders[parts + part]:
+                    if axis == "seq":
+                        apart = lax.rem(mine["seq"] + seq, 2)
+                    else:
+                        apart = lax.rem(index // (1 << (axis - 1)) + mine[axis], 2)
+                    place = 2 * place + apart
+                columns = pl.ds(part * width, width)
+                source = keep.at[slot, seq, :, columns]
+                sem = out_sem.at[slot, seq, part]
+                there = lax.rem(place, base)
+
+                @pl.when(place < base)
+                def _():
+                    act_on(pltpu.make_async_copy(source, near_down.at[there, :, columns], sem))
+
+                @pl.when(place >= base)
+                def _():
+                    act_on(pltpu.make_async_copy(source, far_down.at[there, :, columns], sem))
+
+    @pl.when((now > 0) & (now <= base))
+    def _():
+        crossing(now - 1).wait()
+        add_into(keep.at[lax.rem(now - 1, 2)], got.at[lax.rem(now - 1, 2)])
+        store(now - 1, lambda copy: copy.start())
+
+    @pl.when((now > 1) & (now <= base))
+    def _():
+        store(now - 2, lambda copy: copy.wait())
+
+    @pl.when(now < base)
+    def _():
+        value = dot_nn(act[...].T, home_cot[...])
+        slot = lax.rem(now, 2)
+        split_blocks(value, keep.at[slot], send.at[slot], keep.shape[2], mine[0], [0, 1])
+        crossing(now).start()
+
+    @pl.when(now == base)
+    def _():
+        store(now - 1, lambda copy: copy.wait())
+
     @pl.when(i == 0)
     def _():
         emb = table_row(fam, ids[0]) + table_row(ori, ids[1])
-        for source, csource, where in ((own, cown, me), (far, cfar, 1 - me)):
+        for source, where in ((own, me), (far, 1 - me)):
             for start in range(0, seg, step):
                 part = pl.ds(start, step)
                 there = pl.ds(pl.multiple_of(where * seg + start, step), step)
                 hat, _ = normalise(source[part, :].astype(F32) + emb)
                 norm[there, :] = (hat * gain[...].astype(F32) + bias[...].astype(F32)).astype(BF16)
-                cot[there, :] = csource[part, :]
+        held = pl.ds(pl.multiple_of(me * seg, seg), seg)
+        cot[held, :] = home_cot[held, :]
+        cot[pl.ds(pl.multiple_of((1 - me) * seg, seg), seg), :] = cfar[...]
 
     lanes = wqkv.shape[1] // 128
 
@@ -548,30 +654,26 @@
             partner_along("seq", mine),
         )
 
-    @pl.when(i < 2 * tiles)
-    def _():
+    @pl.when((i >= 0) & (i < 2 * tiles))
+    def _():
+        lin = dot_nn(norm[...], wqkv[...])
         for start in range(0, 2 * seg, step):
             part = pl.ds(start, step)
-            lin = dot_nn(norm[part, :], wqkv[...])
             for lane in range(lanes):
-                piece = turn(lin[:, lane * 128 : (lane + 1) * 128], cos[part, :], sin[part, :])
-                heads[i * lanes + lane, part, :] = piece.astype(BF16)
+                piece = lin[start : start + step, lane * 128 : (lane + 1) * 128]
+                heads[i * lanes + lane, part, :] = turn(piece, cos[part, :], sin[part, :]).astype(BF16)
 
     @pl.when((i >= 2 * tiles) & (i < 3 * tiles))
     def _():
-        for start in range(0, 2 * seg, step):
-            part = pl.ds(start, step)
-            lin = dot_nn(norm[part, :], wqkv[...]).astype(BF16)
-            for lane in range(lanes):
-                heads[i * lanes + lane, part, :] = lin[:, lane * 128 : (lane + 1) * 128]
+        lin = dot_nn(norm[...], wqkv[...]).astype(BF16)
+        for lane in range(lanes):
+            heads[i * lanes + lane] = lin[:, lane * 128 : (lane + 1) * 128]
 
     @pl.when((i >= 3 * tiles) & (i < 4 * tiles))
     def _():
-        for start in range(0, 2 * seg, step):
-            part = pl.ds(start, step)
-            lin = dot_nt(cot[part, :], wout[...]).astype(BF16)
-            for lane in range(lanes):
-                heads[i * lanes + lane, part, :] = lin[:, lane * 128 : (lane + 1) * 128]
+        lin = dot_nt(cot[...], wout[...]).astype(BF16)
+        for lane in range(lanes):
+            heads[i * lanes + lane] = lin[:, lane * 128 : (lane + 1) * 128]
 
     @pl.when(i >= 4 * tiles)
     def _():
@@ -594,48 +696,56 @@
         att_send[pair] = o_ref[pl.ds(pl.multiple_of((1 - me) * seg, seg), seg), :]
         att_crossing(pair).start()
 
-    @pl.when(i == last - 1)
+    @pl.when(now == last - 1)
     def _():
         for pair in range(pairs):
             att_crossing(pair).wait()
             far_att[:, pair * 128 : (pair + 1) * 128] = att_got[pair]
-        happen(events[last])
-
-
-def middle(ids, own, far, cown, cfar, fam, ori, gain, bias, wqkv, wout, cos, sin, up, down, orders, head_size, collective):
+        happen(FFN_EVENTS[last])
+
+
+def middle(
+    ids, own, far, home_cot, cfar, both, fam, ori, gain, bias, wqkv, wout, cos, sin, up, orders, head_size, collective
+):
     seg, d = own.shape
     full = 2 * seg
     tile = 512
     tiles = d // tile
     pairs = d // 128
     bits = len(orders[0])
+    base = 1 << (bits - 1)
+    parts = len(orders) // 2
     near_up, far_up = up
-    near_down, far_down = down
     up_size, ff = near_up.shape[1:]
-    down_size = near_down.shape[1]
+    down_tile = ff // base
+    down_size = down_tile // 4
     smem = pl.BlockSpec(memory_space=pltpu.SMEM)
     anywhere = pl.BlockSpec(memory_space=pl.ANY)
-    head_out = pl.BlockSpec((full, 128), lambda i: (0, jnp.maximum(i - 4 * tiles, 0)))
+    attend_at = base + 4 * tiles
+    head_out = pl.BlockSpec((full, 128), lambda i: (0, jnp.maximum(i - attend_at, 0)))
     rows = jax.ShapeDtypeStruct((full, d), BF16)
+    down = jax.ShapeDtypeStruct((base, down_size, d), BF16)
+    slots = pltpu.VMEM((2, 2, down_size, d), BF16)
     return pl.pallas_call(
         functools.partial(middle_kernel, tiles, pairs, head_size, bits, orders),
-        grid=(4 * tiles + pairs,),
+        grid=(attend_at + pairs,),
         in_specs=[
             smem,
             whole((seg, d)),
             whole((seg, d)),
+            whole((full, d)),
             whole((seg, d)),
-            whole((seg, d)),
+            pl.BlockSpec((None, full, down_tile), lambda i: (0, 0, jnp.minimum(i, base - 1))),
             whole(fam.shape),
             whole(ori.shape),
             whole((1, d)),
             whole((1, d)),
-            pl.BlockSpec((d, tile), lambda i: (0, jnp.minimum(i, 3 * tiles - 1))),
-            pl.BlockSpec((tile, d), lambda i: (jnp.clip(i - 3 * tiles, 0, tiles - 1), 0)),
+            pl.BlockSpec((d, tile), lambda i: (0, jnp.clip(i - base, 0, 3 * tiles - 1))),
+            pl.BlockSpec((tile, d), lambda i: (jnp.clip(i - base - 3 * tiles, 0, tiles - 1), 0)),
             whole((full, 128)),
             whole((full, 128)),
         ]
-        + [anywhere] * 4,
+        + [anywhere] * 2,
         out_specs=[
             whole((full, d)),
             whole((full, d)),
@@ -646,6 +756,8 @@
             whole((seg, d)),
             whole((up_size, ff)),
             whole((down_size, d)),
+            anywhere,
+            anywhere,
         ],
         out_shape=[
             rows,
@@ -657,6 +769,8 @@
             jax.ShapeDtypeStruct((seg, d), BF16),
             jax.ShapeDtypeStruct((up_size, ff), F32),
             jax.ShapeDtypeStruct((down_size, d), F32),
+            down,
+            down,
         ],
         scratch_shapes=[
             pltpu.VMEM((4 * pairs, full, 128), BF16),
@@ -665,15 +779,24 @@
             pltpu.VMEM((pairs, seg, 128), BF16),
             pltpu.VMEM((pairs, seg, 128), BF16),
             pltpu.SemaphoreType.DMA((2, pairs)),
+            slots,
+            slots,
+            slots,
+            pltpu.SemaphoreType.DMA((2,)),
+            pltpu.SemaphoreType.DMA((2,)),
+            pltpu.SemaphoreType.DMA((2, 2, parts)),
         ]
-        + chunk_scratch(orders[0], up_size, ff // 2)
-        + chunk_scratch(orders[1], up_size, ff // 2)
-        + chunk_scratch(orders[2], down_size, d // 2)
-        + chunk_scratch(orders[3], down_size, d // 2),
+        + [
+            entry
+            for index, axes in enumerate(orders)
+            for entry in chunk_scratch(
+                axes, *((up_size, ff // parts) if index < parts else (down_size, d // parts))
+            )
+        ],
         compiler_params=params(collective_id=collective, has_side_effects=True),
-        cost_estimate=cost(8 * full * d * d + 12 * full * full * d, 8 * d * d + 18 * full * d, full * full * H),
+        cost_estimate=cost(16 * full * d * d + 12 * full * full * d, 8 * d * d + 18 * full * d, full * full * H),
         name="middle",
-    )(ids, own, far, cown, cfar, fam, ori, gain, bias, wqkv, wout, cos, sin, near_up, far_up, near_down, far_down)
+    )(ids, own, far, home_cot, cfar, both, fam, ori, gain, bias, wqkv, wout, cos, sin, near_up, far_up)
 
 
 def device_bits(bits):
@@ -730,9 +853,9 @@
         keep[index] = (keep[index].astype(F32) + got[index].astype(F32)).astype(BF16)
 
 
-def wide_grad_kernel(bits, counts, orders, firsts, *refs):
-    lefts, rights = refs[: len(counts)], refs[len(counts) : 2 * len(counts)]
-    near_out, far_out, turned, keep, send, got, send_sem, recv_sem, out_sem = refs[2 * len(counts) :]
+def wide_grad_kernel(bits, counts, orders, *refs):
+    left, rights = refs[0], refs[1 : 1 + len(counts)]
+    near_out, far_out, turned, keep, send, got, send_sem, recv_sem, out_sem = refs[1 + len(counts) :]
     steps = sum(counts)
     i = pl.program_id(0)
     mine = device_bits(bits)
@@ -759,16 +882,11 @@
     @pl.when(i == 0)
     def _():
         meet([partner])
+        turned[...] = left[...].T
 
     start = 0
-    for left, right, count, axes, first in zip(lefts, rights, counts, orders, firsts):
+    for right, count, axes in zip(rights, counts, orders):
         places = [block_place(axes, mine, up, seq) for up in range(blocks // 2) for seq in range(2)]
-        if first:
-
-            @pl.when(i == start)
-            def _():
-                turned[...] = left[...].T
-
         @pl.when((i >= start) & (i < start + count))
         def _():
             value = dot_nn(turned[...], right[...])
@@ -795,31 +913,30 @@
                 copy.wait()
 
 
-def wide_grad(entries, tile, collective):
-    tokens, d = entries[0][0].shape
-    bits = len(entries[0][4])
+def wide_grad(left, entries, tile, collective):
+    tokens, d = left.shape
+    bits = len(entries[0][3])
     blocks = 1 << bits
     size = d // (2 * blocks)
-    counts = [entry[3] for entry in entries]
-    orders = [entry[4] for entry in entries]
-    firsts = [index == 0 or entries[index][0] is not entries[index - 1][0] for index in range(len(entries))]
+    counts = [entry[2] for entry in entries]
+    orders = [entry[3] for entry in entries]
     steps = sum(counts)
     specs = []
     start = 0
     for entry in entries:
 
-        def at(i, start=start, offset=entry[2], last=entry[3] - 1):
+        def at(i, start=start, offset=entry[1], last=entry[2] - 1):
             return (1, 0, offset + jnp.clip(i - start, 0, last))
 
         specs.append(pl.BlockSpec((None, tokens, tile), at))
-        start += entry[3]
+        start += entry[2]
     shape = jax.ShapeDtypeStruct((blocks // 2, size, steps * tile), BF16)
     anywhere = pl.BlockSpec(memory_space=pl.ANY)
     buffers = pltpu.VMEM((steps, blocks, size, tile), BF16)
     return pl.pallas_call(
-        functools.partial(wide_grad_kernel, bits, counts, orders, firsts),
+        functools.partial(wide_grad_kernel, bits, counts, orders),
         grid=(steps,),
-        in_specs=[whole((tokens, d)) for _ in entries] + specs,
+        in_specs=[whole((tokens, d))] + specs,
         out_specs=[anywhere, anywhere],
         out_shape=[shape, shape],
         scratch_shapes=[
@@ -834,96 +951,7 @@
         compiler_params=params(collective_id=collective, has_side_effects=True),
         cost_estimate=cost(2 * tokens * d * steps * tile, 4 * tokens * (d + steps * tile)),
         name="wide_grad",
-    )(*[entry[0] for entry in entries], *[entry[1] for entry in entries])
-
-
-def tall_grad_kernel(bits, orders, left, right, near_out, far_out, keep, send, got, send_sem, recv_sem, out_sem):
-    i = pl.program_id(0)
-    steps, _, size, d = keep.shape
-    width = d // len(orders)
-    mine = device_bits(bits)
-    partner = other_core()
-    half = steps
-
-    def crossing(step):
-        return remote(send.at[step], got.at[step], send_sem.at[step], recv_sem.at[step], partner)
-
-    def store(step, seq, act):
-        for part, axes in enumerate(orders):
-            place = 0
-            for axis in axes:
-                if axis == "seq":
-                    apart = lax.rem(mine["seq"] + seq, 2)
-                else:
-                    apart = lax.rem(step // (1 << (axis - 1)) + mine[axis], 2)
-                place = 2 * place + apart
-            columns = pl.ds(part * width, width)
-            source = keep.at[step, seq, :, columns]
-            sem = out_sem.at[step, seq, part]
-            there = lax.rem(place, half)
-
-            @pl.when(place < half)
-            def _():
-                act(pltpu.make_async_copy(source, near_out.at[there, :, columns], sem))
-
-            @pl.when(place >= half)
-            def _():
-                act(pltpu.make_async_copy(source, far_out.at[there, :, columns], sem))
-
-    @pl.when(i == 0)
-    def _():
-        meet([partner])
-
-    value = dot_nn(left[...].T, right[...])
-    split_blocks(value, keep.at[i], send.at[i], size, mine[0], [0, 1])
-    crossing(i).start()
-
-    def finish(step):
-        crossing(step).wait()
-        add_into(keep.at[step], got.at[step])
-        for seq in range(2):
-            store(step, seq, lambda copy: copy.start())
-
-    @pl.when(i > 0)
-    def _():
-        finish(i - 1)
-
-    @pl.when(i == steps - 1)
-    def _():
-        finish(i)
-        for step in range(steps):
-            for seq in range(2):
-                store(step, seq, lambda copy: copy.wait())
-
-
-def tall_grad(orders, left, right, collective):
-    _, tokens, m = left.shape
-    d = right.shape[1]
-    bits = len(orders[0])
-    steps = 1 << (bits - 1)
-    tile = m // steps
-    size = tile // 4
-    shape = jax.ShapeDtypeStruct((steps, size, d), BF16)
-    anywhere = pl.BlockSpec(memory_space=pl.ANY)
-    buffers = pltpu.VMEM((steps, 2, size, d), BF16)
-    return pl.pallas_call(
-        functools.partial(tall_grad_kernel, bits, orders),
-        grid=(steps,),
-        in_specs=[pl.BlockSpec((None, tokens, tile), lambda i: (0, 0, i)), whole((tokens, d))],
-        out_specs=[anywhere, anywhere],
-        out_shape=[shape, shape],
-        scratch_shapes=[
-            buffers,
-            buffers,
-            buffers,
-            pltpu.SemaphoreType.DMA((steps,)),
-            pltpu.SemaphoreType.DMA((steps,)),
-            pltpu.SemaphoreType.DMA((steps, 2, len(orders))),
-        ],
-        compiler_params=params(collective_id=collective, has_side_effects=True),
-        cost_estimate=cost(2 * tokens * d * m, 2 * (tokens * m + d * m + tokens * d)),
-        name="tall_grad",
-    )(left, right)
+    )(left, *[entry[0] for entry in entries])
 
 
 def partner_along(axis, mine):
@@ -1022,20 +1050,6 @@
 TAIL_STEP = 256
 
 
-def tail_events(sums_at):
-    return {
-        2: [(0, 1)],
-        3: [(1, 1)],
-        4: [(2, 1)],
-        6: [(3, 1)],
-        9: [(0, 2), (1, 2)],
-        16: [(0, 3), (1, 3), (2, 2), (3, 2)],
-        22: [(0, 4), (1, 4), (2, 3), (3, 3)],
-        27: [(2, 4), (3, 4), (0, 5), (1, 5)],
-        sums_at + 1: [(2, 5), (3, 5)],
-    }
-
-
 def tail_kernel(bits, orders, rows, marks, *refs):
     ids, norm_hbm, att_hbm, cot_hbm, dq_hbm, dk_hbm, dv_hbm, wqkv_hbm, wout_hbm = refs[:9]
     fam, ori, gain, bdn, bup_part, bdn_part, far_att = refs[9:16]
@@ -1043,7 +1057,7 @@
     layer_out, input_out, qkv_out, out_out, sums_out, all_out = refs[21:27]
     left, right, dq, dk, dv, wqkv, wout, turned, acc, ng_send, ng_own, ng_got = refs[27:39]
     gg, bg, rg, load_sem, ng_sem, held, got, vec, vgot, table, ssem, rsem, gsend, grecv = refs[39:53]
-    out_start, out_end, in_start, in_end, sums_at = marks
+    in_start, in_end, out_start, out_end, last = marks
     i = pl.program_id(0)
     me = lax.axis_index("seq")
     dp = lax.axis_index("dp")
@@ -1093,12 +1107,11 @@
         chunk.begin()
 
     def back_into(there, half):
-        for start in range(0, seg, step):
-            part = pl.ds(pl.multiple_of(half * seg + start, step), step)
-            total = dot_nt(dq[part, :], wqkv[:, 0:d])
-            total = total + dot_nt(dk[part, :], wqkv[:, d : 2 * d])
-            total = total + dot_nt(dv[part, :], wqkv[:, 2 * d : 3 * d])
-            there[start : start + step, :] = total.astype(BF16)
+        part = pl.ds(pl.multiple_of(half * seg, seg), seg)
+        total = dot_nt(dq[part, :], wqkv[:, 0:d])
+        total = total + dot_nt(dk[part, :], wqkv[:, d : 2 * d])
+        total = total + dot_nt(dv[part, :], wqkv[:, 2 * d : 3 * d])
+        there[...] = total.astype(BF16)
 
     ng_crossing = remote(ng_send, ng_got, ng_sem.at[0], ng_sem.at[1], partners[0])
 
@@ -1113,8 +1126,8 @@
         loads["dq"].wait()
         gradient(0, dq)
 
-    for when, what in tail_events(sums_at).items():
-        if when <= sums_at:
+    for when, what in LATE_EVENTS.items():
+        if when < last:
 
             @pl.when(i == when)
             def _():
@@ -1182,7 +1195,7 @@
         there = pl.ds(pl.multiple_of(own_offset + within, step), step)
         return row, jnp.where(row == me, own[there, :], far[pl.ds(within, step), :])
 
-    @pl.when((i >= out_end) & (i < in_start))
+    @pl.when(i >= out_end)
     def _():
         index = i - out_end
         row, att = home_block(index, left, far_att, me * seg)
@@ -1199,7 +1212,7 @@
         bg[...] = jnp.zeros_like(bg)
         rg[...] = jnp.zeros_like(rg)
 
-    @pl.when((i >= in_end) & (i < sums_at))
+    @pl.when((i >= in_end) & (i < out_start))
     def _():
         index = i - in_end
         row, back = home_block(index, ng_own, ng_got, 0)
@@ -1222,7 +1235,17 @@
         which = lax.broadcasted_iota(jnp.int32, rg.shape, 0)
         rg[...] += jnp.where(which == flag, sums, 0.0)
 
-    @pl.when(i == sums_at)
+    def sums_main(index):
+        return remote(held.at[index], got.at[index], ssem.at[index], rsem.at[index], partners[index])
+
+    def sums_side(index):
+        if index == 0:
+            return remote(vec, vgot, gsend.at[0], grecv.at[0], partners[0])
+        size = 1 << (index - 1)
+        now = pl.ds(dp - lax.rem(dp, size), size)
+        return remote(table.at[now], table.at[now], gsend.at[index], grecv.at[index], partners[index])
+
+    @pl.when(i == out_start)
     def _():
         at = 0
         for source in (bup_part[...], bdn_part[...], gg[...], bg[...], rg[0:1, :], rg[1:2, :]):
@@ -1234,27 +1257,29 @@
             vec[lane // 128 : lane // 128 + 1, :] = both_rows[:, lane : lane + 128]
         extra = d // 128
         vec[extra:, :] = jnp.full((vec.shape[0] - extra, 128), 0.5, F32) * ids[0].astype(F32)
-        for index, partner in enumerate(partners):
-            main = remote(held.at[index], got.at[index], ssem.at[index], rsem.at[index], partner)
-            main.start()
+        sums_main(0).start()
+        sums_side(0).start()
+
+    for index in range(len(partners)):
+
+        @pl.when(i == out_start + 2 * (index + 1))
+        def _():
+            sums_main(index).wait()
+            sums_side(index).wait()
+            total = held[index] + got[index]
             if index == 0:
-                side = remote(vec, vgot, gsend.at[0], grecv.at[0], partner)
-            else:
-                size = 1 << (index - 1)
-                now = pl.ds(dp - lax.rem(dp, size), size)
-                side = remote(table.at[now], table.at[now], gsend.at[index], grecv.at[index], partner)
-            side.start()
-            main.wait()
-            total = held[index] + got[index]
+                table[dp] = vec[...] + vgot[...]
             if index + 1 < len(partners):
                 held[index + 1] = total
+                sums_main(index + 1).start()
+                sums_side(index + 1).start()
             else:
                 sums_out[...] = total
-            side.wait()
-            if index == 0:
-                table[dp] = vec[...] + vgot[...]
-        all_out[...] = table[...]
-        for chunk, stage in tail_events(sums_at)[sums_at + 1]:
+                all_out[...] = table[...]
+
+    @pl.when(i == last - 1)
+    def _():
+        for chunk, stage in LATE_EVENTS[last]:
             chunks[chunk].happen(stage)
 
 
@@ -1266,12 +1291,12 @@
     seg = far_att.shape[0]
     tile, step = TAIL_TILE, TAIL_STEP
     tiles, blocks = ff // tile, tokens // step
-    out_start = 6
+    in_start = 6
+    in_end = in_start + tiles
+    out_start = in_end + blocks
     out_end = out_start + tiles
-    in_start = out_end + blocks
-    in_end = in_start + tiles
-    sums_at = in_end + blocks
-    marks = (out_start, out_end, in_start, in_end, sums_at)
+    last = out_end + blocks
+    marks = (in_start, in_end, out_start, out_end, last)
     size = d // (2 * count)
     rounds = bits + 1
     lines = (ff + 5 * d) // 128
@@ -1279,18 +1304,18 @@
     anywhere = pl.BlockSpec(memory_space=pl.ANY)
 
     def plane(i):
-        late = i >= in_start
-        return (late.astype(jnp.int32), 0, jnp.clip(jnp.where(late, i - in_start, i - out_start), 0, tiles - 1))
+        late = i >= out_start
+        return (jnp.where(late, 0, 1), 0, jnp.clip(jnp.where(late, i - out_start, i - in_start), 0, tiles - 1))
 
     def home(i):
-        return (jnp.clip(jnp.where(i >= in_start, i - in_end, i - out_end), 0, blocks - 1), 0)
+        return (jnp.clip(jnp.where(i >= out_start, i - out_end, i - in_end), 0, blocks - 1), 0)
 
     square = pltpu.VMEM((tokens, d), BF16)
     piece = pltpu.VMEM((seg, d), BF16)
     row = pltpu.VMEM((1, d), F32)
     return pl.pallas_call(
         functools.partial(tail_kernel, bits, orders, rows, marks),
-        grid=(sums_at + 1,),
+        grid=(last,),
         in_specs=[pl.BlockSpec(memory_space=pltpu.SMEM)]
         + [anywhere] * 8
         + [
@@ -1403,30 +1428,21 @@
     ids = jnp.concatenate([family, orient])
     row_ids = jnp.stack([family[0], mine(orient)])
 
-    zs = list(range(2, bits))
-    order_a = [1] + zs + ["seq"]
-    order_b = [1, "seq"] + zs
-    order_c = ["seq", 1] + zs
-    order_d = [2, "seq", 1] + zs[1:]
-    order_e = [2, 1] + zs[1:] + ["seq"]
-    late_orders = [[0] + order_a, [0] + order_e, [0] + order_a, [0] + order_e]
-    ffn_orders = [order_a, order_b, order_c, order_d]
-
     normed, both, up_bias_part, down_bias_part = ffn_forward(
         ids, hid, cot, family_table, orient_table, gain, bias, up_weight, up_bias.reshape(1, ff), down_weight, rows
     )
-    half_tiles = ff // 2048
+    parts = len(FFN_ORDERS) // 2
     ready = after(normed, far_hidden)
-    up = wide_grad([(ready, both, 0, half_tiles, order_a), (ready, both, half_tiles, half_tiles, order_b)], 1024, 1)
-    down = tall_grad([order_c, order_d], both, after(cot, up[0], far_cot), 2)
+    up = wide_grad(ready, [(both, part, 1, FFN_ORDERS[part]) for part in range(parts)], ff // parts, 1)
 
     cosine, sine = rope_tables(jnp.arange(full).astype(F32), 128)
-    row_normed, row_cot, att, dq, dk, dv, far_att, up_total, down_total = middle(
+    row_normed, row_cot, att, dq, dk, dv, far_att, up_total, down_total, _, _ = middle(
         row_ids,
         mine(hidden_in),
         far_hidden,
-        mine(cotangent),
+        cot,
         far_cot,
+        both,
         family_table,
         orient_table,
         gain,
@@ -1436,8 +1452,7 @@
         cosine,
         sine,
         up,
-        down,
-        ffn_orders,
+        FFN_ORDERS,
         d // H,
         3,
     )
@@ -1463,7 +1478,7 @@
         up_weight,
         hid,
         cot,
-        late_orders,
+        LATE_ORDERS,
         rows,
         4,
     )
@@ -1496,7 +1511,7 @@
     hidden_in = args[0]
     dp_count = lax.axis_size("dp")
     two_rows = lax.axis_size("seq") == 2 and hidden_in.shape[0] == 2
-    if two_rows and dp_count >= 4 and dp_count & (dp_count - 1) == 0:
+    if two_rows and dp_count == 16:
         return body_by_rows(*args)
     return body_by_heads(*args)
 

time: 316 us -> 269 us (0.85)
  Pallas kernels: 281 us -> 233 us
    pallas_call x1, Pallas kernels: 104 us -> 77.8 us  [tail(): pl.pallas_call(functools.partial(tail_kernel, bits, orders, rows, marks),...]
    pallas_call x2 -> x1, Pallas kernels: 36.2 us -> 19.4 us  [wide_grad(): pl.pallas_call(functools.partial(wide_grad_kernel, bits, counts, orders),...]
    pallas_call x1, Pallas kernels: 32.2 us -> 26.3 us  [ffn_forward(): pl.pallas_call(functools.partial(ffn_kernel, rows), grid_spec=pltpu.Prefe...]
  transfers between devices with their start and end apart: 2 -> 2, of which waited for: 0 -> 0; matrix products, arithmetic and copies ran while one was open for 3% -> 3% of each run, Pallas kernels for 16% -> 17%
where the time goes in v1:
time: 269 us; the launch traced here: 264 us
  Pallas kernels  233 us (87%)
  local copies, waits for them, and re-layouts  19 us (7%)
  other arithmetic  6.15 us (2%)
  starting transfers between devices  3.13 us (1%)
    pallas_call x1, Pallas kernels, middle(): pl.pallas_call(functools.partial(middle_kernel, tiles, pairs, head_size,...  110 us
    pallas_call x1, Pallas kernels, tail(): pl.pallas_call(functools.partial(tail_kernel, bits, orders, rows, marks),...  77.8 us
    pallas_call x1, Pallas kernels, ffn_forward(): pl.pallas_call(functools.partial(ffn_kernel, rows), grid_spec=pltpu.Prefe...  26.3 us
    pallas_call x1, Pallas kernels, wide_grad(): pl.pallas_call(functools.partial(wide_grad_kernel, bits, counts, orders),...  19.4 us
    unnamed x30, local copies, waits for them, and re-layouts  8.29 us
  transfers between devices with their start and end apart: 2, of which 0 were waited for; matrix products, arithmetic and copies ran while one was open for 3% of the time, Pallas kernels for 17%

profile of v1, /device:TPU:0, one launch (start us, length us, event | category | flops | bytes accessed | tf_op | source)
XLA Modules:
  0.0 263.9 jit_solution(5198561265870733839)
XLA Ops:
  0.6 0.0 copy-start.1
  0.7 2.8 %dynamic-slice_bitcast_fusion.1 = (bf16[512,1024]{1,0:T(8,128)(2,1)S(1)}, bf16[512,1024]{1,0:T(8,128)(2,1)}) fusion(bf16[2,512,1024]{2,1,0:T(8,128)(2,1)} %param.14, s32[]{:T(128)S(6)} %select_n.64, s32[]{:T(128)S(6)} %select_n.63), kind=kLoop, calls=%fused_computation.1 | loop fusion | bytes 4194312 | tf_op jit(solution)/shard_map/jit(dynamic_index_in_dim)/squeeze | solution.py:1419
  3.5 0.0 copy-start.7
  3.5 0.0 copy-start.8
  3.5 0.0 copy-start.6
  3.5 0.0 copy-start.11
  3.5 3.0 %collective-permute-start = (bf16[512,1024]{1,0:T(8,128)(2,1)S(1)}, bf16[512,1024]{1,0:T(8,128)(2,1)S(1)}, u32[]{:S(2)}, u32[]{:S(2)}) collective-permute-start(bf16[512,1024]{1,0:T(8,128)(2,1)S(1)} %get-tuple-element.56), channel_id=1, source_target_pairs={{0,1},{1,0},{2,3},{3,2},{4,5},{5,4},{6,7},{7,6},{8,9},{9,8},{10,11... | collective-permute-start | bytes 3145736 | tf_op jit(solution)/shard_map/ppermute | solution.py:1421
  6.5 0.0 copy-done.1
  6.5 0.1 dynamic-slice_bitcast_fusion
  6.6 0.1 collective-permute-start.1
  6.7 0.0 copy-done.7
  6.7 0.6 reshape.126.gain.refs_8_.refs_11_
  8.0 0.0 copy-done.8
  8.0 0.6 reshape.127.bias.refs_9_
  8.6 0.0 copy-done.6
  8.6 0.6 reshape.128.bup
  9.2 0.0 copy-done.11
  9.2 0.6 pad_add_fusion.ids.refs_0_
  9.8 0.0 copy-start.9
  9.8 26.3 %ffn_forward.1 = (bf16[1024,1024]{1,0:T(8,128)(2,1)}, bf16[2,1024,4096]{2,1,0:T(8,128)(2,1)}, f32[1,4096]{1,0:T(1,128)}, f32[1,1024]{1,0:T(1,128)}) custom-call(s32[3]{0:T(128)} %pad_add_fusion.ids.refs_0_, bf16[1024,1024]{1,0:T(8,128)(2,1)} %bitcast.23, bf16[1024,1024]{1,0:T(8,128)(2,1)} %bitcast.26, bf16[64,1024]{1,0:T(8,128)(2,1)} %refs_9_.1, ...), custom_call_target="tpu_custom_call" | custom-call | flops 17179869184 | bytes 33554432 | tf_op jit(solution)/shard_map/ffn_forward/pallas_call | solution.py:384
  36.1 0.6 dynamic_slice.14
  36.7 0.0 copy-done.9
  36.7 0.6 reshape.129.refs_12_
  37.3 1.2 pad_add_fusion.1.refs_0_
  38.5 3.1 %fusion.2 = (f32[1024,128]{1,0:T(8,128)}, f32[1024,128]{1,0:T(8,128)}) fusion(f32[128]{0:T(128)S(1)} %get-tuple-element.63, f32[128]{0:T(128)S(1)} %get-tuple-element.64, f32[1024]{0:T(1024)S(1)} %iota_convert_fusion, pred[128]{0:T(512)(128)(4,1)S(1)} %broadcast_compare_fusion), kind=kLoop, calls=%fused_computation.7 | loop fusion | flops 524288 | bytes 1053824 | tf_op jit(solution)/shard_map/jit(_where)/select_n | solution.py:36
  41.6 0.0 collective-permute-done.refs_2_
  41.6 0.0 copy-start.10
  41.6 19.4 %wide_grad.1 = (bf16[8,32,4096]{2,1,0:T(8,128)(2,1)}, bf16[8,32,4096]{2,1,0:T(8,128)(2,1)}) custom-call(bf16[1024,1024]{1,0:T(8,128)(2,1)} %get-tuple-element.36.refs_0_, bf16[2,1024,4096]{2,1,0:T(8,128)(2,1)} %get-tuple-element.34.refs_1_.refs_2_.refs_3_.refs_4_.refs_5_.refs_16_, ...), custom_call_target="tpu_custom_call" | custom-call | flops 8589934592 | bytes 20971520 | tf_op jit(solution)/shard_map/wide_grad/pallas_call | solution.py:936
  61.0 0.0 copy-done.10
  61.0 0.0 collective-permute-done.1.refs_4_
  61.0 109.7 %middle.1 = (bf16[1024,1024]{1,0:T(8,128)(2,1)}, bf16[1024,1024]{1,0:T(8,128)(2,1)}, bf16[1024,1024]{1,0:T(8,128)(2,1)}, bf16[1024,1024]{1,0:T(8,128)(2,1)}, bf1...) custom-call(s32[2]{0:T(128)} %pad_add_fusion.1.refs_0_, ...), custom_call_target="tpu_custom_call" | custom-call | flops 30064771072 | bytes 27262976 | tf_op jit(solution)/shard_map/middle/pallas_call | solution.py:729
  170.7 77.8 %tail.1 = (bf16[1024,1024]{1,0:T(8,128)(2,1)}, f32[1024,1024]{1,0:T(8,128)}, f32[32,3072]{1,0:T(8,128)}, f32[32,1024]{1,0:T(8,128)}, f32[72,128]{1,0:T(8,128)}, /*index=5*/f32[16,16,128]{2,1,0:T(8,128)}) custom-call(s32[3]{0:T(128)} %pad_add_fusion.ids.refs_0_, bf16[1024,1024]{1,0:T(8,128)(2,1)} %get-tuple-element.39.refs_1_, ...), custom_call_target="tpu_custom_call" | custom-call | flops 34359738368 | bytes 75497472 | tf_op jit(solution)/shard_map/tail/pallas_call | solution.py:1316
  248.6 0.8 slice.27
  249.4 1.2 convert_reduce_fusion
  250.6 0.7 slice.28
  251.3 1.3 slice_bitcast_fusion
  252.6 1.3 slice_bitcast_fusion.1
  253.9 0.6 reshape.133
  254.5 0.9 fusion.3
  255.5 0.0 copy-start
  255.5 3.2 %copy.38 = bf16[2,512,1024]{2,1,0:T(8,128)(2,1)} copy(bf16[2,512,1024]{2,1,0:T(8,128)(2,1)} %bitcast.25) | data formatting | bytes 4194304
  258.7 0.0 copy-done
  258.7 0.0 copy-start.4
  258.7 0.0 copy-start.5
  258.7 0.0 copy-start.3
  258.7 2.0 copy.39
  260.8 0.0 copy-done.4
  260.8 0.0 copy-start.2
  260.8 0.7 copy.40
  261.5 0.0 copy-done.5
  261.5 0.7 copy.41
  262.2 0.0 copy-done.3
  262.2 0.8 copy.42
  263.0 0.0 copy-done.2
  263.0 0.8 copy.43
  (3 shorter events, 0.0 us)
Async XLA Ops:
  0.6 5.9 %copy-start.1 = (bf16[2,512,1024]{2,1,0:T(8,128)(2,1)S(1)}, bf16[2,512,1024]{2,1,0:T(8,128)(2,1)}, u32[]{:S(2)}) copy-start(bf16[2,512,1024]{2,1,0:T(8,128)(2,1)} %param.27) | copy-start | bytes 6291460
  3.5 3.2 %copy-start.7 = (bf16[1024]{0:T(1024)(128)(2,1)S(1)}, bf16[1024]{0:T(1024)(128)(2,1)}, u32[]{:S(2)}) copy-start(bf16[1024]{0:T(1024)(128)(2,1)} %param.17) | copy-start | bytes 6148
  3.5 4.5 %copy-start.8 = (bf16[1024]{0:T(1024)(128)(2,1)S(1)}, bf16[1024]{0:T(1024)(128)(2,1)}, u32[]{:S(2)}) copy-start(bf16[1024]{0:T(1024)(128)(2,1)} %param.18) | copy-start | bytes 6148
  3.5 5.1 %copy-start.6 = (bf16[4096]{0:T(1024)(128)(2,1)S(1)}, bf16[4096]{0:T(1024)(128)(2,1)}, u32[]{:S(2)}) copy-start(bf16[4096]{0:T(1024)(128)(2,1)} %param.22) | copy-start | bytes 24580
  3.5 5.7 %copy-start.11 = (s32[2]{0:T(128)S(1)}, s32[2]{0:T(128)}, u32[]{:S(2)}) copy-start(s32[2]{0:T(128)} %param.16) | copy-start | bytes 28
  3.5 38.1 %collective-permute-start = (bf16[512,1024]{1,0:T(8,128)(2,1)S(1)}, bf16[512,1024]{1,0:T(8,128)(2,1)S(1)}, u32[]{:S(2)}, u32[]{:S(2)}) collective-permute-start(bf16[512,1024]{1,0:T(8,128)(2,1)S(1)} %get-tuple-element.56), channel_id=1, source_target_pairs={{0,1},{1,0},{2,3},{3,2},{4,5},{5,4},{6,7},{7,6},{8,9},{9,8},{10,11... | collective-permute-start | bytes 3145736 | tf_op jit(solution)/shard_map/ppermute | solution.py:1421
  6.6 54.4 %collective-permute-start.1 = (bf16[512,1024]{1,0:T(8,128)(2,1)S(1)}, bf16[512,1024]{1,0:T(8,128)(2,1)}, u32[]{:S(2)}, u32[]{:S(2)}) collective-permute-start(bf16[512,1024]{1,0:T(8,128)(2,1)S(1)} %dynamic-slice_bitcast_fusion), channel_id=1, source_target_pairs={{0,1},{1,0},{2,3},{3,2},{4,5},{5,4},{6,7},{7,6},{8,9},{9,8},{10,11... | collective-permute-start | bytes 3145736 | tf_op jit(solution)/shard_map/ppermute | solution.py:1422
  9.8 26.9 %copy-start.9 = (bf16[1024]{0:T(1024)(128)(2,1)S(1)}, bf16[1024]{0:T(1024)(128)(2,1)}, u32[]{:S(2)}) copy-start(bf16[1024]{0:T(1024)(128)(2,1)} %param.24) | copy-start | bytes 6148
  41.6 19.4 %copy-start.10 = (bf16[512,1024]{1,0:T(8,128)(2,1)}, bf16[512,1024]{1,0:T(8,128)(2,1)S(1)}, u32[]{:S(2)}) copy-start(bf16[512,1024]{1,0:T(8,128)(2,1)S(1)} %collective-permute-done.refs_2_) | copy-start | bytes 3145732
  255.5 3.2 %copy-start = (f32[1024,1024]{1,0:T(8,128)S(1)}, f32[1024,1024]{1,0:T(8,128)}, u32[]{:S(2)}) copy-start(f32[1024,1024]{1,0:T(8,128)} %get-tuple-element.49) | copy-start | bytes 12582916
  258.7 2.0 copy-start.4
  258.7 2.8 %copy-start.5 = (f32[32,1024]{1,0:T(8,128)S(1)}, f32[32,1024]{1,0:T(8,128)}, u32[]{:S(2)}) copy-start(f32[32,1024]{1,0:T(8,128)} %get-tuple-element.82) | copy-start | bytes 393220
  258.7 3.4 %copy-start.3 = (f32[32,4096]{1,0:T(8,128)S(1)}, f32[32,4096]{1,0:T(8,128)}, u32[]{:S(2)}) copy-start(f32[32,4096]{1,0:T(8,128)} %get-tuple-element.83) | copy-start | bytes 1572868
  260.8 2.2 copy-start.2

commit v2 on v1

--- a/solution.py
+++ b/solution.py
@@ -345,7 +345,7 @@
     return value, slope
 
 
-def ffn_kernel(rows, ids, hid, cot, fam, ori, gain, bias, wup, bup, wdn, norm, both, bupg, bdng):
+def ffn_kernel(rows, ids, hid, cot, fam, ori, gain, bias, wup, bup, wdn, turned, both, bupg, bdng, norm):
     tokens = hid.shape[0]
     seg = tokens // rows
     step = 256
@@ -361,6 +361,7 @@
                 norm[part, :] = (hat * gain[...].astype(F32) + bias[...].astype(F32)).astype(BF16)
                 total = total + jnp.sum(cot[part, :].astype(F32), 0, keepdims=True)
         bdng[...] = total
+        turned[...] = norm[...].T
 
     width = wup.shape[1]
     total = jnp.zeros((8, width), F32)
@@ -398,14 +399,15 @@
                 pl.BlockSpec((tile, d), lambda i, s: (i, 0)),
             ],
             out_specs=[
-                whole((tokens, d)),
+                whole((d, tokens)),
                 pl.BlockSpec((2, tokens, tile), lambda i, s: (0, 0, i)),
                 pl.BlockSpec((1, tile), lambda i, s: (0, i)),
                 whole((1, d)),
             ],
+            scratch_shapes=[pltpu.VMEM((tokens, d), BF16)],
         ),
         out_shape=[
-            jax.ShapeDtypeStruct((tokens, d), BF16),
+            jax.ShapeDtypeStruct((d, tokens), BF16),
             jax.ShapeDtypeStruct((2, tokens, ff), BF16),
             jax.ShapeDtypeStruct((1, ff), F32),
             jax.ShapeDtypeStruct((1, d), F32),
@@ -486,70 +488,82 @@
 
 
 FFN_ORDERS = [
-    [2, 3, 1, "seq"],
-    [2, 1, 3, "seq"],
-    ["seq", 1, 2, 3],
-    ["seq", 3, 1, 2],
+    [2, "seq", 1, 3],
+    [2, 1, "seq", 3],
+    [1, "seq", 3, 2],
     [1, "seq", 2, 3],
+    [1, "seq", 3, 2],
+    [2, 1, "seq", 3],
+    [2, 1, "seq", 3],
     ["seq", 2, 1, 3],
-    [2, 1, 3, "seq"],
-    ["seq", 3, 1, 2],
 ]
 LATE_ORDERS = [
-    [0, 1, 2, "seq", 3],
     [0, 2, 1, "seq", 3],
-    [0, 1, 2, 3, "seq"],
+    [0, 1, 3, 2, "seq"],
     [0, 2, 1, "seq", 3],
+    [0, 1, "seq", 3, 2],
 ]
 FFN_EVENTS = {
-    0: [(0, 0), (1, 0), (2, 0), (3, 0)],
-    9: [(4, 0), (5, 0), (6, 0), (7, 0)],
-    10: [(0, 1), (1, 1), (2, 1), (3, 1)],
-    18: [(1, 2), (2, 2), (4, 1), (0, 2), (5, 1), (7, 1), (3, 2)],
-    19: [(6, 1), (0, 3)],
-    20: [(1, 3), (2, 3), (3, 3), (4, 2), (0, 4)],
-    21: [(1, 4), (5, 2), (6, 2), (7, 2)],
-    22: [(2, 4), (3, 4), (4, 3)],
-    23: [(5, 3), (6, 3), (7, 3), (4, 4)],
-    24: [(6, 4), (5, 4), (7, 4)],
+    4: [(0, 0)],
+    6: [(1, 0)],
+    8: [(2, 0)],
+    9: [(3, 0)],
+    14: [(0, 1)],
+    17: [(6, 0), (7, 0), (4, 0), (5, 0), (2, 1)],
+    19: [(1, 1), (0, 2)],
+    22: [(3, 1)],
+    25: [(6, 1), (7, 1)],
+    26: [(4, 1), (2, 2)],
+    27: [(1, 2), (5, 1), (3, 2), (0, 3)],
+    28: [(7, 2), (6, 2), (4, 2)],
+    29: [(2, 3), (3, 3), (1, 3), (5, 2), (0, 4)],
+    30: [(7, 3), (6, 3), (4, 3)],
+    31: [(2, 4), (5, 3), (3, 4), (1, 4)],
+    32: [(7, 4), (6, 4), (4, 4), (5, 4)],
 }
 LATE_EVENTS = {
     2: [(0, 1)],
     3: [(1, 1)],
     4: [(2, 1)],
     6: [(3, 1)],
-    8: [(0, 2), (1, 2)],
+    7: [(0, 2)],
+    8: [(1, 2)],
     13: [(2, 2)],
-    14: [(1, 3)],
-    16: [(0, 3)],
-    18: [(1, 4), (3, 2)],
-    19: [(2, 3)],
-    20: [(0, 4)],
-    22: [(1, 5)],
-    24: [(3, 3)],
-    26: [(0, 5), (2, 4)],
-    29: [(3, 4)],
+    14: [(3, 2)],
+    17: [(0, 3)],
+    18: [(1, 3)],
+    20: [(3, 3), (2, 3)],
+    21: [(0, 4)],
+    23: [(1, 4)],
+    25: [(2, 4)],
+    26: [(3, 4)],
+    27: [(1, 5)],
+    28: [(0, 5)],
     30: [(2, 5), (3, 5)],
 }
 
 
 def middle_kernel(tiles, pairs, head_size, bits, orders, *refs):
-    ids, own, far, home_cot, cfar, act, fam, ori, gain, bias, wqkv, wout, cos, sin = refs[:14]
-    near_up, far_up = refs[14:16]
-    norm, cot, o_ref, dq_ref, dk_ref, dv_ref, far_att, up_out, down_out, near_down, far_down = refs[16:27]
-    heads, dkt, dvt, att_send, att_got, att_sems, keep, send, got, send_sem, recv_sem, out_sem = refs[27:39]
+    ids, own, far, home_cot, turned, pre, act, fam, ori, gain, bias, wqkv, wout, cos, sin, cot_hbm = refs[:16]
+    norm, cot, o_ref, dq_ref, dk_ref, dv_ref, far_att, up_out, down_out = refs[16:25]
+    near_up, far_up, near_down, far_down = refs[25:29]
+    heads, dkt, dvt, att_send, att_got, att_sems, cfar, cfar_sems = refs[29:37]
+    keep, send, got, send_sem, recv_sem, out_sem = refs[37:43]
+    up_keep, up_send, up_got, up_ssem, up_rsem, up_osem = refs[43:49]
     seg = own.shape[0]
     step = 256
     base = 1 << (bits - 1)
     now = pl.program_id(0)
-    i = now - base
+    ups = up_out.shape[1] // up_keep.shape[3]
+    late = now - ups
+    i = late - base
     me = lax.axis_index("seq")
     mine = device_bits(bits)
     parts = len(orders) // 2
     up_part = up_out.shape[1] // parts
     down_part = down_out.shape[1] // parts
     chunks = chunks_from(
-        refs[39:],
+        refs[49:],
         bits,
         mine,
         [
@@ -570,13 +584,77 @@
     def _():
         meet([partner_along(axis, mine) for axis in [0] + orders[0]])
 
-    last = base + 4 * tiles + pairs
+    cot_crossing = remote(
+        cot_hbm.at[pl.ds(pl.multiple_of((1 - me) * seg, seg), seg)],
+        cfar,
+        cfar_sems.at[0],
+        cfar_sems.at[1],
+        partner_along("seq", mine),
+    )
+
+    @pl.when(now == 0)
+    def _():
+        cot_crossing.start()
+
+    last = ups + base + 4 * tiles + pairs
+    def up_crossing(index):
+        slot = lax.rem(index, 2)
+        return remote(
+            up_send.at[slot], up_got.at[slot], up_ssem.at[slot], up_rsem.at[slot], partner_along(0, mine)
+        )
+
+    def up_stores(index):
+        slot = lax.rem(index, 2)
+        width = up_keep.shape[3]
+        columns = pl.ds(pl.multiple_of(index * width, width), width)
+        return [
+            pltpu.make_async_copy(
+                up_keep.at[slot, pl.ds(half * base, base)], there.at[:, :, columns], up_osem.at[half, slot]
+            )
+            for half, there in enumerate((near_up, far_up))
+        ]
+
+    def up_finish(index):
+        slot = lax.rem(index, 2)
+        up_crossing(index).wait()
+        add_into(up_keep.at[slot], up_got.at[slot])
+        for copy in up_stores(index):
+            copy.start()
+
     for when, what in FFN_EVENTS.items():
         if when < last:
 
             @pl.when(now == when)
             def _():
                 happen(what)
+
+    per_chunk = ups // parts
+    for part in range(parts):
+        places = [block_place(orders[part], mine, up, seq) for up in range(base) for seq in range(2)]
+
+        @pl.when((now >= part * per_chunk) & (now < (part + 1) * per_chunk))
+        def _():
+            value = dot_nn(turned[...], pre[...])
+            slot = lax.rem(now, 2)
+
+            @pl.when(now > 0)
+            def _():
+                up_finish(now - 1)
+
+            @pl.when(now > 1)
+            def _():
+                for copy in up_stores(now - 2):
+                    copy.wait()
+
+            split_blocks(value, up_keep.at[slot], up_send.at[slot], up_keep.shape[2], mine[0], places)
+            up_crossing(now).start()
+
+    @pl.when(now == ups)
+    def _():
+        up_finish(now - 1)
+        for index in (now - 2, now - 1):
+            for copy in up_stores(index):
+                copy.wait()
 
     def crossing(index):
         slot = lax.rem(index, 2)
@@ -609,26 +687,33 @@
                 def _():
                     act_on(pltpu.make_async_copy(source, far_down.at[there, :, columns], sem))
 
-    @pl.when((now > 0) & (now <= base))
-    def _():
-        crossing(now - 1).wait()
-        add_into(keep.at[lax.rem(now - 1, 2)], got.at[lax.rem(now - 1, 2)])
-        store(now - 1, lambda copy: copy.start())
-
-    @pl.when((now > 1) & (now <= base))
-    def _():
-        store(now - 2, lambda copy: copy.wait())
-
-    @pl.when(now < base)
+    def finish(index):
+        slot = lax.rem(index, 2)
+        crossing(index).wait()
+        add_into(keep.at[slot], got.at[slot])
+        store(index, lambda copy: copy.start())
+
+    @pl.when((late >= 0) & (late < base))
     def _():
         value = dot_nn(act[...].T, home_cot[...])
-        slot = lax.rem(now, 2)
+        slot = lax.rem(late, 2)
+
+        @pl.when(late > 0)
+        def _():
+            finish(late - 1)
+
+        @pl.when(late > 1)
+        def _():
+            store(late - 2, lambda copy: copy.wait())
+
         split_blocks(value, keep.at[slot], send.at[slot], keep.shape[2], mine[0], [0, 1])
-        crossing(now).start()
-
-    @pl.when(now == base)
-    def _():
-        store(now - 1, lambda copy: copy.wait())
+        crossing(late).start()
+
+    @pl.when(late == base)
+    def _():
+        finish(late - 1)
+        store(late - 2, lambda copy: copy.wait())
+        store(late - 1, lambda copy: copy.wait())
 
     @pl.when(i == 0)
     def _():
@@ -641,7 +726,6 @@
                 norm[there, :] = (hat * gain[...].astype(F32) + bias[...].astype(F32)).astype(BF16)
         held = pl.ds(pl.multiple_of(me * seg, seg), seg)
         cot[held, :] = home_cot[held, :]
-        cot[pl.ds(pl.multiple_of((1 - me) * seg, seg), seg), :] = cfar[...]
 
     lanes = wqkv.shape[1] // 128
 
@@ -668,6 +752,11 @@
         lin = dot_nn(norm[...], wqkv[...]).astype(BF16)
         for lane in range(lanes):
             heads[i * lanes + lane] = lin[:, lane * 128 : (lane + 1) * 128]
+
+    @pl.when(i == 3 * tiles)
+    def _():
+        cot_crossing.wait()
+        cot[pl.ds(pl.multiple_of((1 - me) * seg, seg), seg), :] = cfar[...]
 
     @pl.when((i >= 3 * tiles) & (i < 4 * tiles))
     def _():
@@ -705,7 +794,7 @@
 
 
 def middle(
-    ids, own, far, home_cot, cfar, both, fam, ori, gain, bias, wqkv, wout, cos, sin, up, orders, head_size, collective
+    ids, own, far, home_cot, turned, both, fam, ori, gain, bias, wqkv, wout, cos, sin, orders, head_size, collective
 ):
     seg, d = own.shape
     full = 2 * seg
@@ -715,17 +804,22 @@
     bits = len(orders[0])
     base = 1 << (bits - 1)
     parts = len(orders) // 2
-    near_up, far_up = up
-    up_size, ff = near_up.shape[1:]
+    ff = both.shape[2]
+    up_size = d // (4 * base)
+    up_tile = 512
+    ups = ff // up_tile
     down_tile = ff // base
     down_size = down_tile // 4
     smem = pl.BlockSpec(memory_space=pltpu.SMEM)
     anywhere = pl.BlockSpec(memory_space=pl.ANY)
-    attend_at = base + 4 * tiles
+    late = ups + base
+    attend_at = late + 4 * tiles
     head_out = pl.BlockSpec((full, 128), lambda i: (0, jnp.maximum(i - attend_at, 0)))
     rows = jax.ShapeDtypeStruct((full, d), BF16)
     down = jax.ShapeDtypeStruct((base, down_size, d), BF16)
+    up = jax.ShapeDtypeStruct((base, up_size, ff), BF16)
     slots = pltpu.VMEM((2, 2, down_size, d), BF16)
+    up_slots = pltpu.VMEM((2, 2 * base, up_size, up_tile), BF16)
     return pl.pallas_call(
         functools.partial(middle_kernel, tiles, pairs, head_size, bits, orders),
         grid=(attend_at + pairs,),
@@ -734,18 +828,19 @@
             whole((seg, d)),
             whole((seg, d)),
             whole((full, d)),
-            whole((seg, d)),
-            pl.BlockSpec((None, full, down_tile), lambda i: (0, 0, jnp.minimum(i, base - 1))),
+            whole((d, full)),
+            pl.BlockSpec((None, full, up_tile), lambda i: (1, 0, jnp.minimum(i, ups - 1))),
+            pl.BlockSpec((None, full, down_tile), lambda i: (0, 0, jnp.clip(i - ups, 0, base - 1))),
             whole(fam.shape),
             whole(ori.shape),
             whole((1, d)),
             whole((1, d)),
-            pl.BlockSpec((d, tile), lambda i: (0, jnp.clip(i - base, 0, 3 * tiles - 1))),
-            pl.BlockSpec((tile, d), lambda i: (jnp.clip(i - base - 3 * tiles, 0, tiles - 1), 0)),
+            pl.BlockSpec((d, tile), lambda i: (0, jnp.clip(i - late, 0, 3 * tiles - 1))),
+            pl.BlockSpec((tile, d), lambda i: (jnp.clip(i - late - 3 * tiles, 0, tiles - 1), 0)),
             whole((full, 128)),
             whole((full, 128)),
         ]
-        + [anywhere] * 2,
+        + [anywhere],
         out_specs=[
             whole((full, d)),
             whole((full, d)),
@@ -756,6 +851,8 @@
             whole((seg, d)),
             whole((up_size, ff)),
             whole((down_size, d)),
+            anywhere,
+            anywhere,
             anywhere,
             anywhere,
         ],
@@ -769,6 +866,8 @@
             jax.ShapeDtypeStruct((seg, d), BF16),
             jax.ShapeDtypeStruct((up_size, ff), F32),
             jax.ShapeDtypeStruct((down_size, d), F32),
+            up,
+            up,
             down,
             down,
         ],
@@ -779,12 +878,20 @@
             pltpu.VMEM((pairs, seg, 128), BF16),
             pltpu.VMEM((pairs, seg, 128), BF16),
             pltpu.SemaphoreType.DMA((2, pairs)),
+            pltpu.VMEM((seg, d), BF16),
+            pltpu.SemaphoreType.DMA((2,)),
             slots,
             slots,
             slots,
             pltpu.SemaphoreType.DMA((2,)),
             pltpu.SemaphoreType.DMA((2,)),
             pltpu.SemaphoreType.DMA((2, 2, parts)),
+            up_slots,
+            up_slots,
+            up_slots,
+            pltpu.SemaphoreType.DMA((2,)),
+            pltpu.SemaphoreType.DMA((2,)),
+            pltpu.SemaphoreType.DMA((2, 2)),
         ]
         + [
             entry
@@ -793,10 +900,12 @@
                 axes, *((up_size, ff // parts) if index < parts else (down_size, d // parts))
             )
         ],
-        compiler_params=params(collective_id=collective, has_side_effects=True),
+        compiler_params=pltpu.CompilerParams(
+            vmem_limit_bytes=67043328, collective_id=collective, has_side_effects=True
+        ),
         cost_estimate=cost(16 * full * d * d + 12 * full * full * d, 8 * d * d + 18 * full * d, full * full * H),
         name="middle",
-    )(ids, own, far, home_cot, cfar, both, fam, ori, gain, bias, wqkv, wout, cos, sin, near_up, far_up)
+    )(ids, own, far, home_cot, turned, both, both, fam, ori, gain, bias, wqkv, wout, cos, sin, home_cot)
 
 
 def device_bits(bits):
@@ -849,109 +958,11 @@
 
 
 def add_into(keep, got):
-    for index in range(keep.shape[0]):
+    def add(index, carry):
         keep[index] = (keep[index].astype(F32) + got[index].astype(F32)).astype(BF16)
-
-
-def wide_grad_kernel(bits, counts, orders, *refs):
-    left, rights = refs[0], refs[1 : 1 + len(counts)]
-    near_out, far_out, turned, keep, send, got, send_sem, recv_sem, out_sem = refs[1 + len(counts) :]
-    steps = sum(counts)
-    i = pl.program_id(0)
-    mine = device_bits(bits)
-    partner = other_core()
-    blocks = keep.shape[1]
-    size = keep.shape[2]
-    tile = keep.shape[3]
-
-    def crossing(step):
-        return remote(send.at[step], got.at[step], send_sem.at[step], recv_sem.at[step], partner)
-
-    def stores(step):
-        columns = pl.ds(pl.multiple_of(step * tile, tile), tile)
-        half = blocks // 2
-        return (
-            pltpu.make_async_copy(
-                keep.at[step, pl.ds(0, half)], near_out.at[:, :, columns], out_sem.at[0, step]
-            ),
-            pltpu.make_async_copy(
-                keep.at[step, pl.ds(half, half)], far_out.at[:, :, columns], out_sem.at[1, step]
-            ),
-        )
-
-    @pl.when(i == 0)
-    def _():
-        meet([partner])
-        turned[...] = left[...].T
-
-    start = 0
-    for right, count, axes in zip(rights, counts, orders):
-        places = [block_place(axes, mine, up, seq) for up in range(blocks // 2) for seq in range(2)]
-        @pl.when((i >= start) & (i < start + count))
-        def _():
-            value = dot_nn(turned[...], right[...])
-            split_blocks(value, keep.at[i], send.at[i], size, mine[0], places)
-            crossing(i).start()
-
-        start += count
-
-    def finish(step):
-        crossing(step).wait()
-        add_into(keep.at[step], got.at[step])
-        for copy in stores(step):
-            copy.start()
-
-    @pl.when(i > 0)
-    def _():
-        finish(i - 1)
-
-    @pl.when(i == steps - 1)
-    def _():
-        finish(i)
-        for step in range(steps):
-            for copy in stores(step):
-                copy.wait()
-
-
-def wide_grad(left, entries, tile, collective):
-    tokens, d = left.shape
-    bits = len(entries[0][3])
-    blocks = 1 << bits
-    size = d // (2 * blocks)
-    counts = [entry[2] for entry in entries]
-    orders = [entry[3] for entry in entries]
-    steps = sum(counts)
-    specs = []
-    start = 0
-    for entry in entries:
-
-        def at(i, start=start, offset=entry[1], last=entry[2] - 1):
-            return (1, 0, offset + jnp.clip(i - start, 0, last))
-
-        specs.append(pl.BlockSpec((None, tokens, tile), at))
-        start += entry[2]
-    shape = jax.ShapeDtypeStruct((blocks // 2, size, steps * tile), BF16)
-    anywhere = pl.BlockSpec(memory_space=pl.ANY)
-    buffers = pltpu.VMEM((steps, blocks, size, tile), BF16)
-    return pl.pallas_call(
-        functools.partial(wide_grad_kernel, bits, counts, orders),
-        grid=(steps,),
-        in_specs=[whole((tokens, d))] + specs,
-        out_specs=[anywhere, anywhere],
-        out_shape=[shape, shape],
-        scratch_shapes=[
-            pltpu.VMEM((d, tokens), BF16),
-            buffers,
-            buffers,
-            buffers,
-            pltpu.SemaphoreType.DMA((steps,)),
-            pltpu.SemaphoreType.DMA((steps,)),
-            pltpu.SemaphoreType.DMA((2, steps)),
-        ],
-        compiler_params=params(collective_id=collective, has_side_effects=True),
-        cost_estimate=cost(2 * tokens * d * steps * tile, 4 * tokens * (d + steps * tile)),
-        name="wide_grad",
-    )(left, *[entry[0] for entry in entries])
+        return carry
+
+    lax.fori_loop(0, keep.shape[0], add, 0)
 
 
 def partner_along(axis, mine):
@@ -1385,6 +1396,56 @@
     )(ids, norm, att, row_cot, dq, dk, dv, wqkv, wout, fam, ori, gain, bdn, bup_part, bdn_part, far_att, both, wdn, wup, hid, cot)
 
 
+def finish_kernel(ff, layer, inputs, qkv, out, up, down, sums, table, *outs):
+    layer_out, input_out, qkv_out, out_out, up_out, down_out, bup, bdn, gain, bias, fam_out, ori_out = outs
+    layer_out[...] = layer[...]
+    input_out[...] = inputs[...]
+    qkv_out[...] = qkv[...]
+    out_out[...] = out[...]
+    up_out[...] = up[...]
+    down_out[...] = down[...]
+
+    @pl.when(pl.program_id(0) == 0)
+    def _():
+        d = gain.shape[1]
+        at = 0
+        for there in (bup, bdn, gain, bias, ori_out.at[0:1], ori_out.at[1:2]):
+            for lane in range(0, there.shape[1], 128):
+                there[:, lane : lane + 128] = sums[at : at + 1, :]
+                at += 1
+        extra = d // 128
+        rows = lax.broadcasted_iota(jnp.int32, (fam_out.shape[0], 128), 0).astype(F32)
+        for lane in range(extra):
+            total = jnp.zeros((fam_out.shape[0], 128), F32)
+            for index in range(table.shape[0]):
+                total = total + jnp.where(
+                    rows == table[index, extra : extra + 1, :], table[index, lane : lane + 1, :], 0.0
+                )
+            fam_out[:, lane * 128 : (lane + 1) * 128] = total
+
+
+def finish(layer, inputs, qkv, out, up, down, sums, table, families):
+    tokens, d = layer.shape
+    ff = up.shape[1]
+    steps = 4
+
+    def rows(entry):
+        return pl.BlockSpec((entry.shape[0] // steps, entry.shape[1]), lambda i: (i, 0))
+
+    big = [layer, inputs, qkv, out, up, down]
+    small = [(1, ff), (1, d), (1, d), (1, d), (families, d), (2, d)]
+    return pl.pallas_call(
+        functools.partial(finish_kernel, ff),
+        grid=(steps,),
+        in_specs=[rows(entry) for entry in big] + [whole(sums.shape), whole(table.shape)],
+        out_specs=[rows(entry) for entry in big] + [whole(shape) for shape in small],
+        out_shape=[jax.ShapeDtypeStruct(entry.shape, entry.dtype) for entry in big]
+        + [jax.ShapeDtypeStruct(shape, F32) for shape in small],
+        compiler_params=params(),
+        name="finish",
+    )(*big, sums, table)
+
+
 def body_by_rows(
     hidden_in,
     family,
@@ -1419,7 +1480,6 @@
         return lax.dynamic_index_in_dim(pair, 1 - seq, 0, keepdims=False)
 
     far_hidden = lax.ppermute(theirs(hidden_in), "seq", ring)
-    far_cot = lax.ppermute(theirs(cotangent), "seq", ring)
 
     gain = norm_gain.reshape(1, d)
     bias = norm_bias.reshape(1, d)
@@ -1428,20 +1488,16 @@
     ids = jnp.concatenate([family, orient])
     row_ids = jnp.stack([family[0], mine(orient)])
 
-    normed, both, up_bias_part, down_bias_part = ffn_forward(
+    turned, both, up_bias_part, down_bias_part = ffn_forward(
         ids, hid, cot, family_table, orient_table, gain, bias, up_weight, up_bias.reshape(1, ff), down_weight, rows
     )
-    parts = len(FFN_ORDERS) // 2
-    ready = after(normed, far_hidden)
-    up = wide_grad(ready, [(both, part, 1, FFN_ORDERS[part]) for part in range(parts)], ff // parts, 1)
-
     cosine, sine = rope_tables(jnp.arange(full).astype(F32), 128)
-    row_normed, row_cot, att, dq, dk, dv, far_att, up_total, down_total, _, _ = middle(
+    row_normed, row_cot, att, dq, dk, dv, far_att, up_total, down_total, *_ = middle(
         row_ids,
         mine(hidden_in),
         far_hidden,
         cot,
-        far_cot,
+        turned,
         both,
         family_table,
         orient_table,
@@ -1451,7 +1507,6 @@
         out_weight,
         cosine,
         sine,
-        up,
         FFN_ORDERS,
         d // H,
         3,
@@ -1482,28 +1537,23 @@
         rows,
         4,
     )
-    flat = sums.reshape(-1)
-    up_bias_sum = flat[:ff]
-    down_bias_sum, gain_sum, bias_sum = flat[ff : ff + 3 * d].reshape(3, d)
-    orient_sum = flat[ff + 3 * d :].reshape(2, d)
-    families = family_table.shape[0]
-    hot = gathered[:, -1, 0].astype(jnp.int32)[None, :] == jnp.arange(families)[:, None]
-    family_sum = jnp.dot(
-        hot.astype(F32), gathered[:, :-8].reshape(dp_count, d), precision=lax.Precision.HIGHEST
-    )
+    layer_out, input_grad, qkv_sum, out_sum, up_sum, down_sum, *small = finish(
+        layer_out, input_grad, qkv_total, out_total, up_total, down_total, sums, gathered, family_table.shape[0]
+    )
+    up_bias_sum, down_bias_sum, gain_sum, bias_sum = (part.reshape(-1) for part in small[:4])
     return (
         layer_out.reshape(rows, seg, d),
         input_grad.reshape(rows, seg, d),
         gain_sum,
         bias_sum,
-        qkv_total,
-        out_total,
-        up_total,
+        qkv_sum,
+        out_sum,
+        up_sum,
         up_bias_sum,
-        down_total,
+        down_sum,
         down_bias_sum,
-        family_sum,
-        orient_sum,
+        small[4],
+        small[5],
     )
 
 

time: 269 us -> 253 us (0.941); the launches traced: 264 us -> 255 us
  local copies, waits for them, and re-layouts: 19 us -> 6.66 us
  Pallas kernels: 233 us -> 239 us
    pallas_call x1, Pallas kernels: 19.4 us -> 7.5 us  [finish(): pl.pallas_call(functools.partial(finish_kernel, ff), grid=(steps,), in_sp...]
    pallas_call x1, Pallas kernels: 77.8 us -> 88.9 us  [tail(): pl.pallas_call(functools.partial(tail_kernel, bits, orders, rows, marks),...]
    unnamed x30 -> x12, local copies, waits for them, and re-layouts: 8.29 us -> 0.95 us
    pallas_call x1, Pallas kernels: 110 us -> 116 us  [middle(): pl.pallas_call(functools.partial(middle_kernel, tiles, pairs, head_size,...]
    slice x3 -> x0, local copies, waits for them, and re-layouts: 2.88 us -> none  [the longest x1 1.32 us: body_by_rows(): up_bias_sum = flat[:ff]]
  transfers between devices with their start and end apart: 2 -> 1, of which waited for: 0 -> 0; matrix products, arithmetic and copies ran while one was open for 3% -> 3% of each run, Pallas kernels for 17% -> 10%
where the time goes in v2:
time: 253 us; the launch traced here: 255 us
  Pallas kernels  239 us (94%)
  local copies, waits for them, and re-layouts  6.66 us (3%)
  other arithmetic  4.91 us (2%)
  starting transfers between devices  2.97 us (1%)
    pallas_call x1, Pallas kernels, middle(): pl.pallas_call(functools.partial(middle_kernel, tiles, pairs, head_size,...  116 us
    pallas_call x1, Pallas kernels, tail(): pl.pallas_call(functools.partial(tail_kernel, bits, orders, rows, marks),...  88.9 us
    pallas_call x1, Pallas kernels, ffn_forward(): pl.pallas_call(functools.partial(ffn_kernel, rows), grid_spec=pltpu.Prefe...  26.4 us
    pallas_call x1, Pallas kernels, finish(): pl.pallas_call(functools.partial(finish_kernel, ff), grid=(steps,), in_sp...  7.5 us
  transfers between devices with their start and end apart: 1, of which 0 were waited for; matrix products, arithmetic and copies ran while one was open for 3% of the time, Pallas kernels for 10%

profile of v2, /device:TPU:0, one launch (start us, length us, event | category | flops | bytes accessed | tf_op | source)
XLA Modules:
  0.0 254.8 jit_solution(11410162595061607916)
XLA Ops:
  0.7 0.0 copy-start.5
  0.7 0.0 copy-start.1
  0.7 0.0 copy-start.2
  0.7 0.0 copy-start
  0.7 0.0 copy-start.3
  0.7 2.7 %dynamic-slice_bitcast_fusion = (bf16[512,1024]{1,0:T(8,128)(2,1)S(1)}, bf16[512,1024]{1,0:T(8,128)(2,1)}) fusion(bf16[2,512,1024]{2,1,0:T(8,128)(2,1)} %param.14, s32[]{:T(128)S(6)} %select_n.63, s32[]{:T(128)S(6)} %select_n.62), kind=kLoop, calls=%fused_computation | loop fusion | bytes 4194312 | tf_op jit(solution)/shard_map/jit(dynamic_index_in_dim)/squeeze | solution.py:1480
  3.4 3.0 %collective-permute-start = (bf16[512,1024]{1,0:T(8,128)(2,1)S(1)}, bf16[512,1024]{1,0:T(8,128)(2,1)S(1)}, u32[]{:S(2)}, u32[]{:S(2)}) collective-permute-start(bf16[512,1024]{1,0:T(8,128)(2,1)S(1)} %get-tuple-element.74), channel_id=1, source_target_pairs={{0,1},{1,0},{2,3},{3,2},{4,5},{5,4},{6,7},{7,6},{8,9},{9,8},{10,11... | collective-permute-start | bytes 3145736 | tf_op jit(solution)/shard_map/ppermute | solution.py:1482
  6.4 0.0 copy-done.5
  6.4 0.6 dynamic_slice.11
  7.7 0.6 pad_add_fusion.ids.refs_0_
  8.2 1.2 pad_add_fusion.1.refs_0_
  9.5 0.0 copy-done.1
  9.5 0.6 reshape.113.gain.refs_9_.refs_11_
  10.1 0.0 copy-done.2
  10.1 0.6 reshape.114.bias.refs_10_
  10.7 0.0 copy-done
  10.7 0.6 reshape.115.bup
  11.3 0.0 copy-done.3
  11.3 0.6 reshape.116.refs_12_
  11.9 3.1 %fusion.2 = (f32[1024,128]{1,0:T(8,128)}, f32[1024,128]{1,0:T(8,128)}) fusion(f32[128]{0:T(128)S(1)} %get-tuple-element.78, f32[128]{0:T(128)S(1)} %get-tuple-element.79, f32[1024]{0:T(1024)S(1)} %iota_convert_fusion, pred[128]{0:T(512)(128)(4,1)S(1)} %broadcast_compare_fusion), kind=kLoop, calls=%fused_computation.6 | loop fusion | flops 524288 | bytes 1053824 | tf_op jit(solution)/shard_map/jit(_where)/select_n | solution.py:36
  15.0 26.4 %ffn_forward.1 = (bf16[1024,1024]{1,0:T(8,128)(2,1)}, bf16[2,1024,4096]{2,1,0:T(8,128)(2,1)}, f32[1,4096]{1,0:T(1,128)}, f32[1,1024]{1,0:T(1,128)}) custom-call(s32[3]{0:T(128)} %pad_add_fusion.ids.refs_0_, bf16[1024,1024]{1,0:T(8,128)(2,1)} %bitcast.12, bf16[1024,1024]{1,0:T(8,128)(2,1)} %bitcast.15, bf16[64,1024]{1,0:T(8,128)(2,1)} %refs_9_.1, ...), custom_call_target="tpu_custom_call" | custom-call | flops 17179869184 | bytes 33554432 | tf_op jit(solution)/shard_map/ffn_forward/pallas_call | solution.py:385
  41.4 0.0 collective-permute-done.refs_2_
  41.4 0.0 copy-start.4
  41.4 0.9 copy-done.4
  42.4 115.9 %middle.1 = (bf16[1024,1024]{1,0:T(8,128)(2,1)}, bf16[1024,1024]{1,0:T(8,128)(2,1)}, bf16[1024,1024]{1,0:T(8,128)(2,1)}, bf16[1024,1024]{1,0:T(8,128)(2,1)}, bf1...) custom-call(s32[2]{0:T(128)} %pad_add_fusion.1.refs_0_, ...), custom_call_target="tpu_custom_call" | custom-call | flops 30064771072 | bytes 27262976 | tf_op jit(solution)/shard_map/middle/pallas_call | solution.py:823
  158.2 88.9 %tail.1 = (bf16[1024,1024]{1,0:T(8,128)(2,1)}, f32[1024,1024]{1,0:T(8,128)}, f32[32,3072]{1,0:T(8,128)}, f32[32,1024]{1,0:T(8,128)}, f32[72,128]{1,0:T(8,128)}, /*index=5*/f32[16,16,128]{2,1,0:T(8,128)}) custom-call(s32[3]{0:T(128)} %pad_add_fusion.ids.refs_0_, bf16[1024,1024]{1,0:T(8,128)(2,1)} %get-tuple-element.45.refs_1_, ...), custom_call_target="tpu_custom_call" | custom-call | flops 34359738368 | bytes 75497472 | tf_op jit(solution)/shard_map/tail/pallas_call | solution.py:1327
  247.1 7.5 %finish.1 = (bf16[1024,1024]{1,0:T(8,128)(2,1)}, f32[1024,1024]{1,0:T(8,128)}, f32[32,3072]{1,0:T(8,128)}, f32[32,1024]{1,0:T(8,128)}, f32[32,4096]{1,0:T(8,128)...) custom-call(bf16[1024,1024]{1,0:T(8,128)(2,1)} %get-tuple-element.54, ...), custom_call_target="tpu_custom_call" | custom-call | tf_op jit(solution)/shard_map/finish/pallas_call | solution.py:1437
  (3 shorter events, 0.0 us)
Async XLA Ops:
  0.7 5.8 %copy-start.5 = (s32[2]{0:T(128)S(1)}, s32[2]{0:T(128)}, u32[]{:S(2)}) copy-start(s32[2]{0:T(128)} %param.16) | copy-start | bytes 28
  0.7 8.8 %copy-start.1 = (bf16[1024]{0:T(1024)(128)(2,1)S(1)}, bf16[1024]{0:T(1024)(128)(2,1)}, u32[]{:S(2)}) copy-start(bf16[1024]{0:T(1024)(128)(2,1)} %param.17) | copy-start | bytes 6148
  0.7 9.4 %copy-start.2 = (bf16[1024]{0:T(1024)(128)(2,1)S(1)}, bf16[1024]{0:T(1024)(128)(2,1)}, u32[]{:S(2)}) copy-start(bf16[1024]{0:T(1024)(128)(2,1)} %param.18) | copy-start | bytes 6148
  0.7 10.0 %copy-start = (bf16[4096]{0:T(1024)(128)(2,1)S(1)}, bf16[4096]{0:T(1024)(128)(2,1)}, u32[]{:S(2)}) copy-start(bf16[4096]{0:T(1024)(128)(2,1)} %param.22) | copy-start | bytes 24580
  0.7 10.6 %copy-start.3 = (bf16[1024]{0:T(1024)(128)(2,1)S(1)}, bf16[1024]{0:T(1024)(128)(2,1)}, u32[]{:S(2)}) copy-start(bf16[1024]{0:T(1024)(128)(2,1)} %param.24) | copy-start | bytes 6148
  3.4 38.0 %collective-permute-start = (bf16[512,1024]{1,0:T(8,128)(2,1)S(1)}, bf16[512,1024]{1,0:T(8,128)(2,1)S(1)}, u32[]{:S(2)}, u32[]{:S(2)}) collective-permute-start(bf16[512,1024]{1,0:T(8,128)(2,1)S(1)} %get-tuple-element.74), channel_id=1, source_target_pairs={{0,1},{1,0},{2,3},{3,2},{4,5},{5,4},{6,7},{7,6},{8,9},{9,8},{10,11... | collective-permute-start | bytes 3145736 | tf_op jit(solution)/shard_map/ppermute | solution.py:1482
  41.4 0.9 copy-start.4

commit v3 on v2

--- a/solution.py
+++ b/solution.py
@@ -328,6 +328,10 @@
     return jnp.sum(jnp.where(rows == wanted, table[...].astype(F32), 0.0), 0, keepdims=True)
 
 
+def line(vector):
+    return vector[...].astype(F32).reshape(1, -1)
+
+
 def normalise(entries):
     centred = entries - jnp.mean(entries, -1, keepdims=True)
     inv_std = lax.rsqrt(jnp.mean(centred * centred, -1, keepdims=True) + 1e-05)
@@ -345,32 +349,34 @@
     return value, slope
 
 
-def ffn_kernel(rows, ids, hid, cot, fam, ori, gain, bias, wup, bup, wdn, turned, both, bupg, bdng, norm):
+def ffn_kernel(rows, fid, oid, hid, cot, fam, ori, gain, bias, wup, bup, wdn, turned, both, bupg, bdng, norm, shifts):
     tokens = hid.shape[0]
     seg = tokens // rows
     step = 256
-
-    @pl.when(pl.program_id(0) == 0)
+    i = pl.program_id(0)
+    @pl.when(i == 0)
     def _():
         total = jnp.zeros((1, cot.shape[1]), F32)
         for row in range(rows):
-            emb = table_row(fam, ids[0]) + table_row(ori, ids[1 + row])
+            emb = table_row(fam, fid[0]) + table_row(ori, oid[row])
             for start in range(row * seg, (row + 1) * seg, step):
                 part = pl.ds(start, step)
                 hat, _ = normalise(hid[part, :].astype(F32) + emb)
-                norm[part, :] = (hat * gain[...].astype(F32) + bias[...].astype(F32)).astype(BF16)
+                norm[part, :] = (hat * line(gain) + line(bias)).astype(BF16)
                 total = total + jnp.sum(cot[part, :].astype(F32), 0, keepdims=True)
         bdng[...] = total
         turned[...] = norm[...].T
+        shifts[...] = line(bup)
 
     width = wup.shape[1]
     total = jnp.zeros((8, width), F32)
     lin = dot_nn(norm[...], wup[...])
     into = dot_nt(cot[...], wdn[...])
+    shift = shifts[:, pl.ds(pl.multiple_of(i * width, width), width)]
     step = 64
     for start in range(0, tokens, step):
         part = pl.ds(start, step)
-        value, slope = gelu_both(lin[start : start + step] + bup[...].astype(F32))
+        value, slope = gelu_both(lin[start : start + step] + shift)
         low = into[start : start + step] * slope
         both[0, part, :] = value.astype(BF16)
         both[1, part, :] = low.astype(BF16)
@@ -378,44 +384,47 @@
     bupg[...] = jnp.sum(total, 0, keepdims=True)
 
 
-def ffn_forward(ids, hid, cot, fam, ori, gain, bias, wup, bup, wdn, rows):
+def ffn_forward(fid, oid, hid, cot, fam, ori, gain, bias, wup, bup, wdn, rows):
     tokens, d = hid.shape
     ff = wup.shape[1]
     tile = 512
+    smem = pl.BlockSpec(memory_space=pltpu.SMEM)
     return pl.pallas_call(
         functools.partial(ffn_kernel, rows),
-        grid_spec=pltpu.PrefetchScalarGridSpec(
-            num_scalar_prefetch=1,
-            grid=(ff // tile,),
-            in_specs=[
-                whole((tokens, d)),
-                whole((tokens, d)),
-                whole(fam.shape),
-                whole(ori.shape),
-                whole((1, d)),
-                whole((1, d)),
-                pl.BlockSpec((d, tile), lambda i, s: (0, i)),
-                pl.BlockSpec((1, tile), lambda i, s: (0, i)),
-                pl.BlockSpec((tile, d), lambda i, s: (i, 0)),
-            ],
-            out_specs=[
-                whole((d, tokens)),
-                pl.BlockSpec((2, tokens, tile), lambda i, s: (0, 0, i)),
-                pl.BlockSpec((1, tile), lambda i, s: (0, i)),
-                whole((1, d)),
-            ],
-            scratch_shapes=[pltpu.VMEM((tokens, d), BF16)],
-        ),
+        grid=(ff // tile,),
+        in_specs=[
+            smem,
+            smem,
+            whole((tokens, d)),
+            whole((tokens, d)),
+            whole(fam.shape),
+            whole(ori.shape),
+            whole(gain.shape),
+            whole(bias.shape),
+            pl.BlockSpec((d, tile), lambda i: (0, i)),
+            whole(bup.shape),
+            pl.BlockSpec((tile, d), lambda i: (i, 0)),
+        ],
+        out_specs=[
+            whole((d, tokens)),
+            pl.BlockSpec((2, tokens, tile), lambda i: (0, 0, i)),
+            pl.BlockSpec((1, tile), lambda i: (0, i)),
+            whole((1, d)),
+        ],
         out_shape=[
             jax.ShapeDtypeStruct((d, tokens), BF16),
             jax.ShapeDtypeStruct((2, tokens, ff), BF16),
             jax.ShapeDtypeStruct((1, ff), F32),
             jax.ShapeDtypeStruct((1, d), F32),
         ],
+        scratch_shapes=[
+            pltpu.VMEM((tokens, d), BF16),
+            pltpu.VMEM((1, ff), F32),
+        ],
         compiler_params=params(),
         cost_estimate=cost(4 * tokens * d * ff, 4 * tokens * ff + 4 * d * ff, tokens * ff),
         name="ffn_forward",
-    )(ids, hid, cot, fam, ori, gain, bias, wup, bup, wdn)
+    )(fid, oid, hid, cot, fam, ori, gain, bias, wup, bup, wdn)
 
 
 def turn(entries, cosine, sine):
@@ -488,14 +497,14 @@
 
 
 FFN_ORDERS = [
-    [2, "seq", 1, 3],
     [2, 1, "seq", 3],
-    [1, "seq", 3, 2],
-    [1, "seq", 2, 3],
+    [1, 2, "seq", 3],
     [1, "seq", 3, 2],
     [2, 1, "seq", 3],
     [2, 1, "seq", 3],
-    ["seq", 2, 1, 3],
+    [2, 1, "seq", 3],
+    [1, 2, "seq", 3],
+    ["seq", 1, 3, 2],
 ]
 LATE_ORDERS = [
     [0, 2, 1, "seq", 3],
@@ -509,17 +518,20 @@
     8: [(2, 0)],
     9: [(3, 0)],
     14: [(0, 1)],
-    17: [(6, 0), (7, 0), (4, 0), (5, 0), (2, 1)],
-    19: [(1, 1), (0, 2)],
-    22: [(3, 1)],
-    25: [(6, 1), (7, 1)],
-    26: [(4, 1), (2, 2)],
-    27: [(1, 2), (5, 1), (3, 2), (0, 3)],
-    28: [(7, 2), (6, 2), (4, 2)],
-    29: [(2, 3), (3, 3), (1, 3), (5, 2), (0, 4)],
-    30: [(7, 3), (6, 3), (4, 3)],
-    31: [(2, 4), (5, 3), (3, 4), (1, 4)],
-    32: [(7, 4), (6, 4), (4, 4), (5, 4)],
+    15: [(1, 1)],
+    17: [(7, 0), (4, 0), (5, 0), (6, 0)],
+    18: [(3, 1)],
+    20: [(2, 1)],
+    21: [(1, 2)],
+    23: [(0, 2)],
+    25: [(4, 1)],
+    26: [(6, 1), (7, 1)],
+    27: [(3, 2), (2, 2), (5, 1), (1, 3)],
+    28: [(4, 2), (0, 3), (6, 2), (7, 2)],
+    29: [(3, 3), (2, 3), (5, 2)],
+    30: [(1, 4), (4, 3), (0, 4), (6, 3)],
+    31: [(7, 3), (5, 3), (3, 4)],
+    32: [(2, 4), (4, 4), (6, 4), (7, 4), (5, 4)],
 }
 LATE_EVENTS = {
     2: [(0, 1)],
@@ -544,13 +556,14 @@
 
 
 def middle_kernel(tiles, pairs, head_size, bits, orders, *refs):
-    ids, own, far, home_cot, turned, pre, act, fam, ori, gain, bias, wqkv, wout, cos, sin, cot_hbm = refs[:16]
-    norm, cot, o_ref, dq_ref, dk_ref, dv_ref, far_att, up_out, down_out = refs[16:25]
-    near_up, far_up, near_down, far_down = refs[25:29]
-    heads, dkt, dvt, att_send, att_got, att_sems, cfar, cfar_sems = refs[29:37]
-    keep, send, got, send_sem, recv_sem, out_sem = refs[37:43]
-    up_keep, up_send, up_got, up_ssem, up_rsem, up_osem = refs[43:49]
-    seg = own.shape[0]
+    fid, oid, home_cot, turned, pre, act, fam, ori, gain, bias, wqkv, wout, angles, hid_hbm, cot_hbm = refs[:15]
+    norm, cot, o_ref, dq_ref, dk_ref, dv_ref, far_att, up_out, down_out = refs[15:24]
+    near_up, far_up, near_down, far_down = refs[24:28]
+    heads, dkt, dvt, att_send, att_got, att_sems, cfar, cfar_sems = refs[28:36]
+    keep, send, got, send_sem, recv_sem, out_sem = refs[36:42]
+    up_keep, up_send, up_got, up_ssem, up_rsem, up_osem = refs[42:48]
+    own, cos, sin, own_sem, far, far_sems = refs[48:54]
+    seg = far.shape[0]
     step = 256
     base = 1 << (bits - 1)
     now = pl.program_id(0)
@@ -563,7 +576,7 @@
     up_part = up_out.shape[1] // parts
     down_part = down_out.shape[1] // parts
     chunks = chunks_from(
-        refs[49:],
+        refs[54:],
         bits,
         mine,
         [
@@ -592,9 +605,20 @@
         partner_along("seq", mine),
     )
 
+    far_crossing = remote(
+        hid_hbm.at[pl.ds(pl.multiple_of((1 - me) * seg, seg), seg)],
+        far,
+        far_sems.at[0],
+        far_sems.at[1],
+        partner_along("seq", mine),
+    )
+    own_load = pltpu.make_async_copy(hid_hbm.at[pl.ds(pl.multiple_of(me * seg, seg), seg)], own, own_sem)
+
     @pl.when(now == 0)
     def _():
+        far_crossing.start()
         cot_crossing.start()
+        own_load.start()
 
     last = ups + base + 4 * tiles + pairs
     def up_crossing(index):
@@ -717,13 +741,21 @@
 
     @pl.when(i == 0)
     def _():
-        emb = table_row(fam, ids[0]) + table_row(ori, ids[1])
+        own_load.wait()
+        far_crossing.wait()
+        fine = angles.shape[1]
+        for coarse in range(2 * seg // fine):
+            there = pl.ds(coarse * fine, fine)
+            cos_a, sin_a = angles[0, coarse : coarse + 1, :], angles[1, coarse : coarse + 1, :]
+            cos[there, :] = cos_a * angles[2] - sin_a * angles[3]
+            sin[there, :] = sin_a * angles[2] + cos_a * angles[3]
+        emb = table_row(fam, fid[0]) + table_row(ori, oid[me])
         for source, where in ((own, me), (far, 1 - me)):
             for start in range(0, seg, step):
                 part = pl.ds(start, step)
                 there = pl.ds(pl.multiple_of(where * seg + start, step), step)
                 hat, _ = normalise(source[part, :].astype(F32) + emb)
-                norm[there, :] = (hat * gain[...].astype(F32) + bias[...].astype(F32)).astype(BF16)
+                norm[there, :] = (hat * line(gain) + line(bias)).astype(BF16)
         held = pl.ds(pl.multiple_of(me * seg, seg), seg)
         cot[held, :] = home_cot[held, :]
 
@@ -794,10 +826,10 @@
 
 
 def middle(
-    ids, own, far, home_cot, turned, both, fam, ori, gain, bias, wqkv, wout, cos, sin, orders, head_size, collective
+    fid, oid, hid, home_cot, turned, both, fam, ori, gain, bias, wqkv, wout, angles, orders, head_size, collective
 ):
-    seg, d = own.shape
-    full = 2 * seg
+    full, d = hid.shape
+    seg = full // 2
     tile = 512
     tiles = d // tile
     pairs = d // 128
@@ -825,22 +857,20 @@
         grid=(attend_at + pairs,),
         in_specs=[
             smem,
-            whole((seg, d)),
-            whole((seg, d)),
+            smem,
             whole((full, d)),
             whole((d, full)),
             pl.BlockSpec((None, full, up_tile), lambda i: (1, 0, jnp.minimum(i, ups - 1))),
             pl.BlockSpec((None, full, down_tile), lambda i: (0, 0, jnp.clip(i - ups, 0, base - 1))),
             whole(fam.shape),
             whole(ori.shape),
-            whole((1, d)),
-            whole((1, d)),
+            whole(gain.shape),
+            whole(bias.shape),
             pl.BlockSpec((d, tile), lambda i: (0, jnp.clip(i - late, 0, 3 * tiles - 1))),
             pl.BlockSpec((tile, d), lambda i: (jnp.clip(i - late - 3 * tiles, 0, tiles - 1), 0)),
-            whole((full, 128)),
-            whole((full, 128)),
+            whole(angles.shape),
         ]
-        + [anywhere],
+        + [anywhere] * 2,
         out_specs=[
             whole((full, d)),
             whole((full, d)),
@@ -892,6 +922,12 @@
             pltpu.SemaphoreType.DMA((2,)),
             pltpu.SemaphoreType.DMA((2,)),
             pltpu.SemaphoreType.DMA((2, 2)),
+            pltpu.VMEM((seg, d), BF16),
+            pltpu.VMEM((full, 128), F32),
+            pltpu.VMEM((full, 128), F32),
+            pltpu.SemaphoreType.DMA,
+            pltpu.VMEM((seg, d), BF16),
+            pltpu.SemaphoreType.DMA((2,)),
         ]
         + [
             entry
@@ -905,7 +941,7 @@
         ),
         cost_estimate=cost(16 * full * d * d + 12 * full * full * d, 8 * d * d + 18 * full * d, full * full * H),
         name="middle",
-    )(ids, own, far, home_cot, turned, both, both, fam, ori, gain, bias, wqkv, wout, cos, sin, home_cot)
+    )(fid, oid, home_cot, turned, both, both, fam, ori, gain, bias, wqkv, wout, angles, hid, home_cot)
 
 
 def device_bits(bits):
@@ -962,7 +998,7 @@
         keep[index] = (keep[index].astype(F32) + got[index].astype(F32)).astype(BF16)
         return carry
 
-    lax.fori_loop(0, keep.shape[0], add, 0)
+    lax.fori_loop(0, got.shape[0], add, 0, unroll=2 if got.shape[0] > 1 else 1)
 
 
 def partner_along(axis, mine):
@@ -1005,13 +1041,7 @@
         if stage == 1 and self.near is not None:
             self.load().wait()
         self.crossing(stage - 1).wait()
-        count = (1 << len(self.axes)) >> stage
-
-        def add(index, carry):
-            self.keep[index] = (self.keep[index].astype(F32) + self.got[stage - 1][index].astype(F32)).astype(BF16)
-            return carry
-
-        lax.fori_loop(0, count, add, 0)
+        add_into(self.keep, self.got[stage - 1])
         self.crossing(stage).start()
 
     def finish(self):
@@ -1062,11 +1092,11 @@
 
 
 def tail_kernel(bits, orders, rows, marks, *refs):
-    ids, norm_hbm, att_hbm, cot_hbm, dq_hbm, dk_hbm, dv_hbm, wqkv_hbm, wout_hbm = refs[:9]
-    fam, ori, gain, bdn, bup_part, bdn_part, far_att = refs[9:16]
-    both, wdn, wup, hid, cot = refs[16:21]
-    layer_out, input_out, qkv_out, out_out, sums_out, all_out = refs[21:27]
-    left, right, dq, dk, dv, wqkv, wout, turned, acc, ng_send, ng_own, ng_got = refs[27:39]
+    fid, oid, norm_hbm, att_hbm, cot_hbm, dq_hbm, dk_hbm, dv_hbm, wqkv_hbm, wout_hbm = refs[:10]
+    fam, ori, gain, bdn, bup_part, bdn_part, far_att = refs[10:17]
+    both, wdn, wup, hid, cot = refs[17:22]
+    layer_out, input_out, qkv_out, out_out, sums_out, all_out = refs[22:28]
+    left, right, dq, dk, dv, wqkv, wout, turned, acc, ng_here, ng_got = refs[28:39]
     gg, bg, rg, load_sem, ng_sem, held, got, vec, vgot, table, ssem, rsem, gsend, grecv = refs[39:53]
     in_start, in_end, out_start, out_end, last = marks
     i = pl.program_id(0)
@@ -1074,7 +1104,7 @@
     dp = lax.axis_index("dp")
     mine = device_bits(bits)
     d = left.shape[1]
-    seg = ng_own.shape[0]
+    seg = ng_got.shape[0]
     step = TAIL_STEP
     per_row = seg // step
     chunks = chunks_from(
@@ -1117,48 +1147,54 @@
             chunk.keep[place] = value[block * size : (block + 1) * size, :].astype(BF16)
         chunk.begin()
 
-    def back_into(there, half):
+    ng_crossing = remote(ng_here.at[0], ng_got, ng_sem.at[0], ng_sem.at[1], partners[0])
+
+    @pl.when(i == 0)
+    def _():
+        loads["norm"].start()
+        loads["dq"].start()
+        meet(partners)
+        loads["norm"].wait()
+        turned[...] = left[...].T
+        loads["dq"].wait()
+        for name in ("dk", "dv", "wqkv", "att", "cot", "wout"):
+            loads[name].start()
+        gradient(0, dq)
+
+    for when, what in LATE_EVENTS.items():
+        if when < last:
+
+            @pl.when(i == when)
+            def _():
+                for chunk, stage in what:
+                    chunks[chunk].happen(stage)
+
+    @pl.when(i == 1)
+    def _():
+        loads["dk"].wait()
+        gradient(1, dk)
+
+    @pl.when(i == 2)
+    def _():
+        loads["dv"].wait()
+        gradient(2, dv)
+
+    @pl.when(i == 3)
+    def _():
+        loads["wqkv"].wait()
+
+    @pl.when((i == 3) | (i == 5))
+    def _():
+        first = (5 - i) // 2
+        half = first * (1 - me) + (1 - first) * me
         part = pl.ds(pl.multiple_of(half * seg, seg), seg)
         total = dot_nt(dq[part, :], wqkv[:, 0:d])
         total = total + dot_nt(dk[part, :], wqkv[:, d : 2 * d])
         total = total + dot_nt(dv[part, :], wqkv[:, 2 * d : 3 * d])
-        there[...] = total.astype(BF16)
-
-    ng_crossing = remote(ng_send, ng_got, ng_sem.at[0], ng_sem.at[1], partners[0])
-
-    @pl.when(i == 0)
-    def _():
-        for name in ("norm", "dq", "dk", "dv", "wqkv", "cot", "wout"):
-            loads[name].start()
-        meet(partners)
-        loads["norm"].wait()
-        turned[...] = left[...].T
-        loads["att"].start()
-        loads["dq"].wait()
-        gradient(0, dq)
-
-    for when, what in LATE_EVENTS.items():
-        if when < last:
-
-            @pl.when(i == when)
-            def _():
-                for chunk, stage in what:
-                    chunks[chunk].happen(stage)
-
-    @pl.when(i == 1)
-    def _():
-        loads["dk"].wait()
-        gradient(1, dk)
-
-    @pl.when(i == 2)
-    def _():
-        loads["dv"].wait()
-        gradient(2, dv)
+        ng_here[1 - first] = total.astype(BF16)
 
     @pl.when(i == 3)
     def _():
-        loads["wqkv"].wait()
-        back_into(ng_send, 1 - me)
         ng_crossing.start()
 
     @pl.when(i == 4)
@@ -1167,10 +1203,6 @@
         loads["cot"].wait()
         turned[...] = left[...].T
         gradient(3, right)
-
-    @pl.when(i == 5)
-    def _():
-        back_into(ng_own, me)
 
     @pl.when((i >= out_start) & (i < out_end))
     def _():
@@ -1210,11 +1242,11 @@
     def _():
         index = i - out_end
         row, att = home_block(index, left, far_att, me * seg)
-        flag = jnp.where(row == 0, ids[1], ids[2])
-        emb = table_row(fam, ids[0]) + table_row(ori, flag)
+        flag = oid[row]
+        emb = table_row(fam, fid[0]) + table_row(ori, flag)
         part = pl.ds(pl.multiple_of(index * step, step), step)
         total = hid[...].astype(F32) + emb + dot_nn(att, wout[...])
-        layer_out[...] = (total + (acc[part, :] + bdn[...].astype(F32))).astype(BF16)
+        layer_out[...] = (total + (acc[part, :] + line(bdn))).astype(BF16)
 
     @pl.when(i == in_end)
     def _():
@@ -1226,15 +1258,15 @@
     @pl.when((i >= in_end) & (i < out_start))
     def _():
         index = i - in_end
-        row, back = home_block(index, ng_own, ng_got, 0)
-        flag = jnp.where(row == 0, ids[1], ids[2])
-        emb = table_row(fam, ids[0]) + table_row(ori, flag)
+        row, back = home_block(index, ng_here.at[1], ng_got, 0)
+        flag = oid[row]
+        emb = table_row(fam, fid[0]) + table_row(ori, flag)
         part = pl.ds(pl.multiple_of(index * step, step), step)
         hat, inv_std = normalise(hid[...].astype(F32) + emb)
         grad = acc[part, :] + back.astype(F32)
         gg[...] += jnp.sum(grad * hat, 0, keepdims=True)
         bg[...] += jnp.sum(grad, 0, keepdims=True)
-        scaled = grad * gain[...].astype(F32)
+        scaled = grad * line(gain)
         inner = (
             scaled
             - jnp.mean(scaled, -1, keepdims=True)
@@ -1267,7 +1299,7 @@
         for lane in range(0, d, 128):
             vec[lane // 128 : lane // 128 + 1, :] = both_rows[:, lane : lane + 128]
         extra = d // 128
-        vec[extra:, :] = jnp.full((vec.shape[0] - extra, 128), 0.5, F32) * ids[0].astype(F32)
+        vec[extra:, :] = jnp.full((vec.shape[0] - extra, 128), 0.5, F32) * fid[0].astype(F32)
         sums_main(0).start()
         sums_side(0).start()
 
@@ -1294,7 +1326,7 @@
             chunks[chunk].happen(stage)
 
 
-def tail(ids, norm, att, row_cot, dq, dk, dv, wqkv, wout, fam, ori, gain, bdn, bup_part, bdn_part, far_att, both, wdn, wup, hid, cot, orders, rows, collective):
+def tail(fid, oid, norm, att, row_cot, dq, dk, dv, wqkv, wout, fam, ori, gain, bdn, bup_part, bdn_part, far_att, both, wdn, wup, hid, cot, orders, rows, collective):
     tokens, d = hid.shape
     ff = wup.shape[1]
     bits = len(orders[0]) - 1
@@ -1327,13 +1359,13 @@
     return pl.pallas_call(
         functools.partial(tail_kernel, bits, orders, rows, marks),
         grid=(last,),
-        in_specs=[pl.BlockSpec(memory_space=pltpu.SMEM)]
+        in_specs=[pl.BlockSpec(memory_space=pltpu.SMEM)] * 2
         + [anywhere] * 8
         + [
             whole(fam.shape),
             whole(ori.shape),
-            whole((1, d)),
-            whole((1, d)),
+            whole(gain.shape),
+            whole(bdn.shape),
             whole((1, ff)),
             whole((1, d)),
             whole((seg, d)),
@@ -1369,8 +1401,7 @@
             pltpu.VMEM((d, d), BF16),
             pltpu.VMEM((d, tokens), BF16),
             pltpu.VMEM((tokens, d), F32),
-            piece,
-            piece,
+            pltpu.VMEM((2, seg, d), BF16),
             piece,
             row,
             row,
@@ -1393,7 +1424,7 @@
         ),
         cost_estimate=cost(16 * tokens * d * d + 4 * tokens * d * ff, 8 * d * ff + 40 * tokens * d),
         name="tail",
-    )(ids, norm, att, row_cot, dq, dk, dv, wqkv, wout, fam, ori, gain, bdn, bup_part, bdn_part, far_att, both, wdn, wup, hid, cot)
+    )(fid, oid, norm, att, row_cot, dq, dk, dv, wqkv, wout, fam, ori, gain, bdn, bup_part, bdn_part, far_att, both, wdn, wup, hid, cot)
 
 
 def finish_kernel(ff, layer, inputs, qkv, out, up, down, sums, table, *outs):
@@ -1471,48 +1502,37 @@
     upper = dp_count // 2
     dp = lax.axis_index("dp")
     seq = lax.axis_index("seq")
-    ring = [(0, 1), (1, 0)]
-
-    def mine(pair):
-        return lax.dynamic_index_in_dim(pair, seq, 0, keepdims=False)
-
-    def theirs(pair):
-        return lax.dynamic_index_in_dim(pair, 1 - seq, 0, keepdims=False)
-
-    far_hidden = lax.ppermute(theirs(hidden_in), "seq", ring)
-
-    gain = norm_gain.reshape(1, d)
-    bias = norm_bias.reshape(1, d)
     hid = hidden_in.reshape(tokens, d)
     cot = cotangent.reshape(tokens, d)
-    ids = jnp.concatenate([family, orient])
-    row_ids = jnp.stack([family[0], mine(orient)])
-
     turned, both, up_bias_part, down_bias_part = ffn_forward(
-        ids, hid, cot, family_table, orient_table, gain, bias, up_weight, up_bias.reshape(1, ff), down_weight, rows
-    )
-    cosine, sine = rope_tables(jnp.arange(full).astype(F32), 128)
+        family, orient, hid, cot, family_table, orient_table, norm_gain, norm_bias, up_weight, up_bias, down_weight, rows
+    )
+    fine = 32
+    positions = jnp.concatenate([fine * jnp.arange(full // fine), jnp.arange(fine)]).astype(F32)
+    cosine, sine = rope_tables(positions, 128)
+    coarse = full // fine
+    angles = jnp.stack([cosine[:coarse], sine[:coarse], cosine[coarse:], sine[coarse:]])
     row_normed, row_cot, att, dq, dk, dv, far_att, up_total, down_total, *_ = middle(
-        row_ids,
-        mine(hidden_in),
-        far_hidden,
+        family,
+        orient,
+        hid,
         cot,
         turned,
         both,
         family_table,
         orient_table,
-        gain,
-        bias,
+        norm_gain,
+        norm_bias,
         qkv_weight,
         out_weight,
-        cosine,
-        sine,
+        angles,
         FFN_ORDERS,
         d // H,
         3,
     )
     layer_out, input_grad, qkv_total, out_total, sums, gathered = tail(
-        ids,
+        family,
+        orient,
         row_normed,
         att,
         row_cot,
@@ -1523,8 +1543,8 @@
         out_weight,
         family_table,
         orient_table,
-        gain,
-        down_bias.reshape(1, d),
+        norm_gain,
+        down_bias,
         up_bias_part,
         down_bias_part,
         far_att,
@@ -1561,7 +1581,7 @@
     hidden_in = args[0]
     dp_count = lax.axis_size("dp")
     two_rows = lax.axis_size("seq") == 2 and hidden_in.shape[0] == 2
-    if two_rows and dp_count == 16:
+    if two_rows and dp_count == 16 and hidden_in.shape[1] == 512:
         return body_by_rows(*args)
     return body_by_heads(*args)
 

time: 253 us -> 243 us (0.960)
  local copies, waits for them, and re-layouts: 6.66 us -> 0.01 us
  other arithmetic: 4.91 us -> 0.94 us
  Pallas kernels: 239 us -> 242 us
  starting transfers between devices: 2.97 us -> 0 us
    pallas_call x1, Pallas kernels: 116 us -> 131 us  [middle(): pl.pallas_call(functools.partial(middle_kernel, tiles, pairs, head_size,...]
    pallas_call x1, Pallas kernels: 88.9 us -> 78 us  [tail(): pl.pallas_call(functools.partial(tail_kernel, bits, orders, rows, marks),...]
    ppermute x1 -> x0, starting transfers between devices: 2.97 us -> none  [body_by_rows(): far_hidden = lax.ppermute(theirs(hidden_in), 'seq', ring)]
    select_n x1, other arithmetic: 3.07 us -> 0.2 us  [rope_tables(): cosine = jnp.where(rotary[None, :], jnp.cos(angles), 1.0)]
    squeeze x1 -> x0, local copies, waits for them, and re-layouts: 2.71 us -> none  [theirs(): return lax.dynamic_index_in_dim(pair, 1 - seq, 0, keepdims=False)]
  transfers between devices with their start and end apart: 1 -> 0, of which waited for: 0 -> 0; matrix products, arithmetic and copies ran while one was open for 3% -> 0% of each run, Pallas kernels for 10% -> 0%
where the time goes in v3:
time: 243 us; the launch traced here: 245 us
  Pallas kernels  242 us (100%)
    pallas_call x1, Pallas kernels, middle(): pl.pallas_call(functools.partial(middle_kernel, tiles, pairs, head_size,...  131 us
    pallas_call x1, Pallas kernels, tail(): pl.pallas_call(functools.partial(tail_kernel, bits, orders, rows, marks),...  78 us
    pallas_call x1, Pallas kernels, ffn_forward(): pl.pallas_call(functools.partial(ffn_kernel, rows), grid=(ff // tile,), i...  25.8 us
    pallas_call x1, Pallas kernels, finish(): pl.pallas_call(functools.partial(finish_kernel, ff), grid=(steps,), in_sp...  7.5 us

profile of v3, /device:TPU:0, one launch (start us, length us, event | category | flops | bytes accessed | tf_op | source)
XLA Modules:
  0.0 244.7 jit_solution(17958706886919594910)
XLA Ops:
  1.4 0.1 add_convert_fusion
  1.4 0.2 fusion
  1.7 0.6 pad_maximum_fusion.refs_12_
  2.3 25.8 %ffn_forward.1 = (bf16[1024,1024]{1,0:T(8,128)(2,1)}, bf16[2,1024,4096]{2,1,0:T(8,128)(2,1)}, f32[1,4096]{1,0:T(1,128)}, f32[1,1024]{1,0:T(1,128)}) custom-call(s32[1]{0:T(128)S(6)} %copy.26.fid.refs_0_, s32[2]{0:T(128)} %refs_1_.3, bf16[1024,1024]{1,0:T(8,128)(2,1)} %bitcast.21, bf16[1024,1024]{1,0:T(8,128)(2,1)} %bitcast.17, bf16[64,1024]{1,0:T(8,128)(2,1)} %refs_10_.3, ...), custom_call_target="tpu_custom_call" | custom-call | flops 17179869184 | bytes 33554432 | tf_op jit(solution)/shard_map/ffn_forward/pallas_call | solution.py:392
  28.1 130.8 %middle.1 = (bf16[1024,1024]{1,0:T(8,128)(2,1)}, bf16[1024,1024]{1,0:T(8,128)(2,1)}, bf16[1024,1024]{1,0:T(8,128)(2,1)}, bf16[1024,1024]{1,0:T(8,128)(2,1)}, bf1...) custom-call(s32[1]{0:T(128)S(6)} %copy.26.fid.refs_0_, ...), custom_call_target="tpu_custom_call" | custom-call | flops 30064771072 | bytes 27262976 | tf_op jit(solution)/shard_map/middle/pallas_call | solution.py:855
  159.0 78.0 %tail.1 = (bf16[1024,1024]{1,0:T(8,128)(2,1)}, f32[1024,1024]{1,0:T(8,128)}, f32[32,3072]{1,0:T(8,128)}, f32[32,1024]{1,0:T(8,128)}, f32[72,128]{1,0:T(8,128)}, /*index=5*/f32[16,16,128]{2,1,0:T(8,128)}) custom-call(s32[1]{0:T(128)S(6)} %copy.26.fid.refs_0_, s32[2]{0:T(128)} %refs_1_.3, bf16[1024,1024]{1,0:T(8,128)(2,1)} %get-tuple-element.45.refs_2_, ...), custom_call_target="tpu_custom_call" | custom-call | flops 34359738368 | bytes 75497472 | tf_op jit(solution)/shard_map/tail/pallas_call | solution.py:1359
  237.0 7.5 %finish.1 = (bf16[1024,1024]{1,0:T(8,128)(2,1)}, f32[1024,1024]{1,0:T(8,128)}, f32[32,3072]{1,0:T(8,128)}, f32[32,1024]{1,0:T(8,128)}, f32[32,4096]{1,0:T(8,128)...) custom-call(bf16[1024,1024]{1,0:T(8,128)(2,1)} %get-tuple-element.54, ...), custom_call_target="tpu_custom_call" | custom-call | tf_op jit(solution)/shard_map/finish/pallas_call | solution.py:1468
  (6 shorter events, 0.0 us)

commit v4 on v3

--- a/solution.py
+++ b/solution.py
@@ -498,19 +498,19 @@
 
 FFN_ORDERS = [
     [2, 1, "seq", 3],
-    [1, 2, "seq", 3],
-    [1, "seq", 3, 2],
+    [1, 2, 3, "seq"],
+    [2, 1, "seq", 3],
+    [1, "seq", 2, 3],
+    [1, "seq", 2, 3],
     [2, 1, "seq", 3],
     [2, 1, "seq", 3],
-    [2, 1, "seq", 3],
-    [1, 2, "seq", 3],
-    ["seq", 1, 3, 2],
+    ["seq", 2, 1, 3],
 ]
 LATE_ORDERS = [
-    [0, 2, 1, "seq", 3],
-    [0, 1, 3, 2, "seq"],
-    [0, 2, 1, "seq", 3],
-    [0, 1, "seq", 3, 2],
+    [0, 2, 1, 3, "seq"],
+    [0, 1, 3, "seq", 2],
+    [0, 2, "seq", 3, 1],
+    [0, 1, 2, "seq", 3],
 ]
 FFN_EVENTS = {
     4: [(0, 0)],
@@ -519,39 +519,34 @@
     9: [(3, 0)],
     14: [(0, 1)],
     15: [(1, 1)],
-    17: [(7, 0), (4, 0), (5, 0), (6, 0)],
-    18: [(3, 1)],
-    20: [(2, 1)],
+    17: [(7, 0), (4, 0), (5, 0), (6, 0), (2, 1)],
+    20: [(3, 1)],
     21: [(1, 2)],
     23: [(0, 2)],
-    25: [(4, 1)],
-    26: [(6, 1), (7, 1)],
-    27: [(3, 2), (2, 2), (5, 1), (1, 3)],
-    28: [(4, 2), (0, 3), (6, 2), (7, 2)],
-    29: [(3, 3), (2, 3), (5, 2)],
-    30: [(1, 4), (4, 3), (0, 4), (6, 3)],
-    31: [(7, 3), (5, 3), (3, 4)],
-    32: [(2, 4), (4, 4), (6, 4), (7, 4), (5, 4)],
+    26: [(5, 1), (7, 1), (4, 1)],
+    27: [(3, 2), (2, 2), (0, 3), (6, 1)],
+    28: [(1, 3), (5, 2), (4, 2)],
+    29: [(7, 2), (2, 3), (3, 3), (6, 2)],
+    30: [(0, 4), (1, 4), (4, 3), (5, 3)],
+    31: [(7, 3), (2, 4), (6, 3), (3, 4)],
+    32: [(4, 4), (5, 4), (7, 4), (6, 4)],
 }
 LATE_EVENTS = {
     2: [(0, 1)],
     3: [(1, 1)],
     4: [(2, 1)],
-    6: [(3, 1)],
-    7: [(0, 2)],
-    8: [(1, 2)],
-    13: [(2, 2)],
-    14: [(3, 2)],
-    17: [(0, 3)],
-    18: [(1, 3)],
-    20: [(3, 3), (2, 3)],
-    21: [(0, 4)],
-    23: [(1, 4)],
-    25: [(2, 4)],
-    26: [(3, 4)],
-    27: [(1, 5)],
-    28: [(0, 5)],
-    30: [(2, 5), (3, 5)],
+    6: [(0, 2)],
+    7: [(3, 1), (1, 2)],
+    10: [(0, 3), (2, 2)],
+    13: [(3, 2), (1, 3)],
+    15: [(2, 3), (0, 4)],
+    16: [(1, 4)],
+    17: [(3, 3), (0, 5)],
+    18: [(2, 4)],
+    19: [(1, 5)],
+    20: [(3, 4)],
+    21: [(2, 5)],
+    22: [(3, 5)],
 }
 
 
@@ -1087,7 +1082,7 @@
     return lax.optimization_barrier((entry, *others))[0]
 
 
-TAIL_TILE = 512
+TAIL_TILE = 1024
 TAIL_STEP = 256
 
 
@@ -1096,8 +1091,8 @@
     fam, ori, gain, bdn, bup_part, bdn_part, far_att = refs[10:17]
     both, wdn, wup, hid, cot = refs[17:22]
     layer_out, input_out, qkv_out, out_out, sums_out, all_out = refs[22:28]
-    left, right, dq, dk, dv, wqkv, wout, turned, acc, ng_here, ng_got = refs[28:39]
-    gg, bg, rg, load_sem, ng_sem, held, got, vec, vgot, table, ssem, rsem, gsend, grecv = refs[39:53]
+    left, dq, dk, dv, wqkv, wout, turned, acc, ng_here, ng_got = refs[28:38]
+    gg, bg, rg, load_sem, ng_sem, held, got, vec, vgot, table, ssem, rsem, gsend, grecv = refs[38:52]
     in_start, in_end, out_start, out_end, last = marks
     i = pl.program_id(0)
     me = lax.axis_index("seq")
@@ -1108,7 +1103,7 @@
     step = TAIL_STEP
     per_row = seg // step
     chunks = chunks_from(
-        refs[53:],
+        refs[52:],
         len(orders[0]),
         mine,
         [
@@ -1127,7 +1122,7 @@
                 ("dk", dk_hbm, dk),
                 ("dv", dv_hbm, dv),
                 ("wqkv", wqkv_hbm, wqkv),
-                ("cot", cot_hbm, right),
+                ("cot", cot_hbm, dq),
                 ("wout", wout_hbm, wout),
                 ("att", att_hbm, left),
             )
@@ -1157,9 +1152,51 @@
         loads["norm"].wait()
         turned[...] = left[...].T
         loads["dq"].wait()
-        for name in ("dk", "dv", "wqkv", "att", "cot", "wout"):
+        for name in ("dk", "dv", "wqkv", "att", "wout"):
             loads[name].start()
         gradient(0, dq)
+
+    def sums_main(index):
+        return remote(held.at[index], got.at[index], ssem.at[index], rsem.at[index], partners[index])
+
+    def sums_side(index):
+        if index == 0:
+            return remote(vec, vgot, gsend.at[0], grecv.at[0], partners[0])
+        size = 1 << (index - 1)
+        now = pl.ds(dp - lax.rem(dp, size), size)
+        return remote(table.at[now], table.at[now], gsend.at[index], grecv.at[index], partners[index])
+
+    @pl.when(i == out_start)
+    def _():
+        at = 0
+        for source in (bup_part[...], bdn_part[...], gg[...], bg[...], rg[0:1, :], rg[1:2, :]):
+            for lane in range(0, source.shape[1], 128):
+                held[0, at : at + 1, :] = source[:, lane : lane + 128]
+                at += 1
+        both_rows = rg[0:1, :] + rg[1:2, :]
+        for lane in range(0, d, 128):
+            vec[lane // 128 : lane // 128 + 1, :] = both_rows[:, lane : lane + 128]
+        extra = d // 128
+        vec[extra:, :] = jnp.full((vec.shape[0] - extra, 128), 0.5, F32) * fid[0].astype(F32)
+        sums_main(0).start()
+        sums_side(0).start()
+
+    for index in range(len(partners)):
+
+        @pl.when(i == out_start + (index + 1 if index < len(partners) - 1 else last - 1 - out_start))
+        def _():
+            sums_main(index).wait()
+            sums_side(index).wait()
+            total = held[index] + got[index]
+            if index == 0:
+                table[dp] = vec[...] + vgot[...]
+            if index + 1 < len(partners):
+                held[index + 1] = total
+                sums_main(index + 1).start()
+                sums_side(index + 1).start()
+            else:
+                sums_out[...] = total
+                all_out[...] = table[...]
 
     for when, what in LATE_EVENTS.items():
         if when < last:
@@ -1183,9 +1220,9 @@
     def _():
         loads["wqkv"].wait()
 
-    @pl.when((i == 3) | (i == 5))
-    def _():
-        first = (5 - i) // 2
+    @pl.when((i == 3) | (i == 4))
+    def _():
+        first = 4 - i
         half = first * (1 - me) + (1 - first) * me
         part = pl.ds(pl.multiple_of(half * seg, seg), seg)
         total = dot_nt(dq[part, :], wqkv[:, 0:d])
@@ -1197,12 +1234,13 @@
     def _():
         ng_crossing.start()
 
-    @pl.when(i == 4)
-    def _():
+    @pl.when(i == 5)
+    def _():
+        loads["cot"].start()
         loads["att"].wait()
+        turned[...] = left[...].T
         loads["cot"].wait()
-        turned[...] = left[...].T
-        gradient(3, right)
+        gradient(3, dq)
 
     @pl.when((i >= out_start) & (i < out_end))
     def _():
@@ -1277,48 +1315,6 @@
         sums = jnp.sum(result, 0, keepdims=True)
         which = lax.broadcasted_iota(jnp.int32, rg.shape, 0)
         rg[...] += jnp.where(which == flag, sums, 0.0)
-
-    def sums_main(index):
-        return remote(held.at[index], got.at[index], ssem.at[index], rsem.at[index], partners[index])
-
-    def sums_side(index):
-        if index == 0:
-            return remote(vec, vgot, gsend.at[0], grecv.at[0], partners[0])
-        size = 1 << (index - 1)
-        now = pl.ds(dp - lax.rem(dp, size), size)
-        return remote(table.at[now], table.at[now], gsend.at[index], grecv.at[index], partners[index])
-
-    @pl.when(i == out_start)
-    def _():
-        at = 0
-        for source in (bup_part[...], bdn_part[...], gg[...], bg[...], rg[0:1, :], rg[1:2, :]):
-            for lane in range(0, source.shape[1], 128):
-                held[0, at : at + 1, :] = source[:, lane : lane + 128]
-                at += 1
-        both_rows = rg[0:1, :] + rg[1:2, :]
-        for lane in range(0, d, 128):
-            vec[lane // 128 : lane // 128 + 1, :] = both_rows[:, lane : lane + 128]
-        extra = d // 128
-        vec[extra:, :] = jnp.full((vec.shape[0] - extra, 128), 0.5, F32) * fid[0].astype(F32)
-        sums_main(0).start()
-        sums_side(0).start()
-
-    for index in range(len(partners)):
-
-        @pl.when(i == out_start + 2 * (index + 1))
-        def _():
-            sums_main(index).wait()
-            sums_side(index).wait()
-            total = held[index] + got[index]
-            if index == 0:
-                table[dp] = vec[...] + vgot[...]
-            if index + 1 < len(partners):
-                held[index + 1] = total
-                sums_main(index + 1).start()
-                sums_side(index + 1).start()
-            else:
-                sums_out[...] = total
-                all_out[...] = table[...]
 
     @pl.when(i == last - 1)
     def _():
@@ -1396,7 +1392,6 @@
             square,
             square,
             square,
-            square,
             pltpu.VMEM((d, 3 * d), BF16),
             pltpu.VMEM((d, d), BF16),
             pltpu.VMEM((d, tokens), BF16),
@@ -1461,7 +1456,9 @@
     steps = 4
 
     def rows(entry):
-        return pl.BlockSpec((entry.shape[0] // steps, entry.shape[1]), lambda i: (i, 0))
+        count = max(entry.shape[0] // steps, 8)
+        each = steps * count // entry.shape[0]
+        return pl.BlockSpec((count, entry.shape[1]), lambda i: (i // each, 0))
 
     big = [layer, inputs, qkv, out, up, down]
     small = [(1, ff), (1, d), (1, d), (1, d), (families, d), (2, d)]

time: 243 us -> 238 us (0.979)
  Pallas kernels: 242 us -> 238 us
    pallas_call x1, Pallas kernels: 131 us -> 118 us  [middle(): pl.pallas_call(functools.partial(middle_kernel, tiles, pairs, head_size,...]
    pallas_call x1, Pallas kernels: 78 us -> 86.4 us  [tail(): pl.pallas_call(functools.partial(tail_kernel, bits, orders, rows, marks),...]
where the time goes in v4:
time: 238 us; the launch traced here: 240 us
  Pallas kernels  238 us (100%)
    pallas_call x1, Pallas kernels, middle(): pl.pallas_call(functools.partial(middle_kernel, tiles, pairs, head_size,...  118 us
    pallas_call x1, Pallas kernels, tail(): pl.pallas_call(functools.partial(tail_kernel, bits, orders, rows, marks),...  86.4 us
    pallas_call x1, Pallas kernels, ffn_forward(): pl.pallas_call(functools.partial(ffn_kernel, rows), grid=(ff // tile,), i...  25.8 us
    pallas_call x1, Pallas kernels, finish(): pl.pallas_call(functools.partial(finish_kernel, ff), grid=(steps,), in_sp...  7.5 us

profile of v4, /device:TPU:0, one launch (start us, length us, event | category | flops | bytes accessed | tf_op | source)
XLA Modules:
  0.0 240.3 jit_solution(13979777677044362141)
XLA Ops:
  1.4 0.1 add_convert_fusion
  1.4 0.2 fusion
  1.7 0.6 pad_maximum_fusion.refs_12_
  2.3 25.8 %ffn_forward.1 = (bf16[1024,1024]{1,0:T(8,128)(2,1)}, bf16[2,1024,4096]{2,1,0:T(8,128)(2,1)}, f32[1,4096]{1,0:T(1,128)}, f32[1,1024]{1,0:T(1,128)}) custom-call(s32[1]{0:T(128)S(6)} %copy.26.fid.refs_0_, s32[2]{0:T(128)} %refs_1_.3, bf16[1024,1024]{1,0:T(8,128)(2,1)} %bitcast.21, bf16[1024,1024]{1,0:T(8,128)(2,1)} %bitcast.17, bf16[64,1024]{1,0:T(8,128)(2,1)} %refs_10_.3, ...), custom_call_target="tpu_custom_call" | custom-call | flops 17179869184 | bytes 33554432 | tf_op jit(solution)/shard_map/ffn_forward/pallas_call | solution.py:392
  28.1 118.0 %middle.1 = (bf16[1024,1024]{1,0:T(8,128)(2,1)}, bf16[1024,1024]{1,0:T(8,128)(2,1)}, bf16[1024,1024]{1,0:T(8,128)(2,1)}, bf16[1024,1024]{1,0:T(8,128)(2,1)}, bf1...) custom-call(s32[1]{0:T(128)S(6)} %copy.26.fid.refs_0_, ...), custom_call_target="tpu_custom_call" | custom-call | flops 30064771072 | bytes 27262976 | tf_op jit(solution)/shard_map/middle/pallas_call | solution.py:850
  146.1 86.4 %tail.1 = (bf16[1024,1024]{1,0:T(8,128)(2,1)}, f32[1024,1024]{1,0:T(8,128)}, f32[32,3072]{1,0:T(8,128)}, f32[32,1024]{1,0:T(8,128)}, f32[72,128]{1,0:T(8,128)}, /*index=5*/f32[16,16,128]{2,1,0:T(8,128)}) custom-call(s32[1]{0:T(128)S(6)} %copy.26.fid.refs_0_, s32[2]{0:T(128)} %refs_1_.3, bf16[1024,1024]{1,0:T(8,128)(2,1)} %get-tuple-element.45.refs_2_, ...), custom_call_target="tpu_custom_call" | custom-call | flops 34359738368 | bytes 75497472 | tf_op jit(solution)/shard_map/tail/pallas_call | solution.py:1355
  232.5 7.5 %finish.1 = (bf16[1024,1024]{1,0:T(8,128)(2,1)}, f32[1024,1024]{1,0:T(8,128)}, f32[32,3072]{1,0:T(8,128)}, f32[32,1024]{1,0:T(8,128)}, f32[32,4096]{1,0:T(8,128)...) custom-call(bf16[1024,1024]{1,0:T(8,128)(2,1)} %get-tuple-element.54, ...), custom_call_target="tpu_custom_call" | custom-call | tf_op jit(solution)/shard_map/finish/pallas_call | solution.py:1465
  (6 shorter events, 0.0 us)

commit v5 on v4

--- a/solution.py
+++ b/solution.py
@@ -508,8 +508,8 @@
 ]
 LATE_ORDERS = [
     [0, 2, 1, 3, "seq"],
-    [0, 1, 3, "seq", 2],
-    [0, 2, "seq", 3, 1],
+    [0, 1, 2, 3, "seq"],
+    [0, 2, "seq", 1, 3],
     [0, 1, 2, "seq", 3],
 ]
 FFN_EVENTS = {
@@ -537,15 +537,15 @@
     4: [(2, 1)],
     6: [(0, 2)],
     7: [(3, 1), (1, 2)],
-    10: [(0, 3), (2, 2)],
-    13: [(3, 2), (1, 3)],
-    15: [(2, 3), (0, 4)],
-    16: [(1, 4)],
-    17: [(3, 3), (0, 5)],
-    18: [(2, 4)],
-    19: [(1, 5)],
+    9: [(0, 3), (2, 2)],
+    10: [(1, 3)],
+    13: [(3, 2), (0, 4)],
+    14: [(2, 3)],
+    15: [(0, 5), (1, 4)],
+    16: [(2, 4)],
+    17: [(1, 5), (3, 3)],
+    18: [(2, 5)],
     20: [(3, 4)],
-    21: [(2, 5)],
     22: [(3, 5)],
 }
 

time: 238 us -> 238 us (level)
  no operation moved by 1% of the time
where the time goes in v5:
time: 238 us; the launch traced here: 240 us
  Pallas kernels  237 us (100%)
    pallas_call x1, Pallas kernels, middle(): pl.pallas_call(functools.partial(middle_kernel, tiles, pairs, head_size,...  118 us
    pallas_call x1, Pallas kernels, tail(): pl.pallas_call(functools.partial(tail_kernel, bits, orders, rows, marks),...  86 us
    pallas_call x1, Pallas kernels, ffn_forward(): pl.pallas_call(functools.partial(ffn_kernel, rows), grid=(ff // tile,), i...  25.8 us
    pallas_call x1, Pallas kernels, finish(): pl.pallas_call(functools.partial(finish_kernel, ff), grid=(steps,), in_sp...  7.5 us

profile of v5, /device:TPU:0, one launch (start us, length us, event | category | flops | bytes accessed | tf_op | source)
XLA Modules:
  0.0 239.9 jit_solution(3661240150457299593)
XLA Ops:
  1.4 0.1 add_convert_fusion
  1.4 0.2 fusion
  1.7 0.6 pad_maximum_fusion.refs_12_
  2.3 25.8 %ffn_forward.1 = (bf16[1024,1024]{1,0:T(8,128)(2,1)}, bf16[2,1024,4096]{2,1,0:T(8,128)(2,1)}, f32[1,4096]{1,0:T(1,128)}, f32[1,1024]{1,0:T(1,128)}) custom-call(s32[1]{0:T(128)S(6)} %copy.26.fid.refs_0_, s32[2]{0:T(128)} %refs_1_.3, bf16[1024,1024]{1,0:T(8,128)(2,1)} %bitcast.21, bf16[1024,1024]{1,0:T(8,128)(2,1)} %bitcast.17, bf16[64,1024]{1,0:T(8,128)(2,1)} %refs_10_.3, ...), custom_call_target="tpu_custom_call" | custom-call | flops 17179869184 | bytes 33554432 | tf_op jit(solution)/shard_map/ffn_forward/pallas_call | solution.py:392
  28.1 118.0 %middle.1 = (bf16[1024,1024]{1,0:T(8,128)(2,1)}, bf16[1024,1024]{1,0:T(8,128)(2,1)}, bf16[1024,1024]{1,0:T(8,128)(2,1)}, bf16[1024,1024]{1,0:T(8,128)(2,1)}, bf1...) custom-call(s32[1]{0:T(128)S(6)} %copy.26.fid.refs_0_, ...), custom_call_target="tpu_custom_call" | custom-call | flops 30064771072 | bytes 27262976 | tf_op jit(solution)/shard_map/middle/pallas_call | solution.py:850
  146.1 86.0 %tail.1 = (bf16[1024,1024]{1,0:T(8,128)(2,1)}, f32[1024,1024]{1,0:T(8,128)}, f32[32,3072]{1,0:T(8,128)}, f32[32,1024]{1,0:T(8,128)}, f32[72,128]{1,0:T(8,128)}, /*index=5*/f32[16,16,128]{2,1,0:T(8,128)}) custom-call(s32[1]{0:T(128)S(6)} %copy.26.fid.refs_0_, s32[2]{0:T(128)} %refs_1_.3, bf16[1024,1024]{1,0:T(8,128)(2,1)} %get-tuple-element.45.refs_2_, ...), custom_call_target="tpu_custom_call" | custom-call | flops 34359738368 | bytes 75497472 | tf_op jit(solution)/shard_map/tail/pallas_call | solution.py:1355
  232.1 7.5 %finish.1 = (bf16[1024,1024]{1,0:T(8,128)(2,1)}, f32[1024,1024]{1,0:T(8,128)}, f32[32,3072]{1,0:T(8,128)}, f32[32,1024]{1,0:T(8,128)}, f32[32,4096]{1,0:T(8,128)...) custom-call(bf16[1024,1024]{1,0:T(8,128)(2,1)} %get-tuple-element.54, ...), custom_call_target="tpu_custom_call" | custom-call | tf_op jit(solution)/shard_map/finish/pallas_call | solution.py:1465
  (6 shorter events, 0.0 us)
